TPU v7x, 512 devices: a whole 4x8x8 slice. The times are simulated.
512 devices in a mesh: src: 16 (over y, core), vocab: 32 (over x, z).
Axes of the slice: x: 4, y: 8, z: 8, core: 2. Of those that a mesh axis runs over, the one named last changes fastest.
Arguments:
- queries: bfloat16 [8192, 2048], P('vocab', 'src'), may hold values from -35 to 35
- enc_keys: bfloat16 [32, 256, 2048], P('vocab', None, 'src'), may hold values from -4 to 4
- enc_values: bfloat16 [32, 256, 2048], P('vocab', None, 'src'), may hold values from -48 to 48
- source_lengths: int32 [32], P('vocab'), may hold values from 1 to 256, 4096 in all
- out_proj: bfloat16 [2048, 2048], P('src'), may hold values from -0.125 to 0.125
- dec_state: bfloat16 [8192, 2048], P('vocab', 'src'), may hold values from -24 to 24
- norm_gain: float32 [2048], P('src'), may hold values from 0.25 to 1.75
- norm_bias: float32 [2048], P('src'), may hold values from -3 to 3
- head_weight: bfloat16 [2048, 258048], P('src', 'vocab'), may hold values from -2 to 2
- shortlist: int32 [8192, 8], P('vocab'), may hold values from 0 to 2015, all different within a row; in each aligned block of 256 rows (0 to 255, 256 to 511, ...) at most 2 rows name the same one
- target_slot: int32 [8192], P('vocab'), may hold values from 0 to 7
- target_offset: int32 [8192], P('vocab'), may hold values from 0 to 127
Outputs:
- row_loss: float32 [8192], P('vocab')
- grad_state: float32 [8192, 2048], P('vocab', 'src')
Inputs may be any that keep to these rules, and one draw needn't show every extreme that they name: `shortlist`: each row lists 8 different blocks; the rows of one sentence list one block at most 2 times.
All inputs are finite; a program needn't handle non-finite values. No bound on the sum of `source_lengths` on one device may be relied on, other than what follows from the above.
Results may differ from a plain program's by a relative error of at most 0.0055.
Values may be sent and summed in bfloat16 or wider, within the bound.
No kernel may reach another device: no remote copies, remote signals or barrier semaphores. Data moves between devices by JAX's collectives and lax.ppermute only.
A program may use at most 64 MiB of HBM per device.

v0:
```python
import math

import jax
import jax.numpy as jnp
from jax import lax
from jax.sharding import PartitionSpec as P

HD = 128
BLK = 128


MASKED = -1e30
EPSILON = 1e-05


def slot_stats(full_logits, code_grid):
    slot_top = jnp.max(full_logits, axis=-1)
    slot_spread = jnp.sum(jnp.exp(full_logits - slot_top[..., None]), axis=-1)
    offsets = lax.broadcasted_iota(jnp.int32, full_logits.shape, 3)
    slot_pick = jnp.sum(jnp.where(offsets == code_grid[..., None], full_logits, 0.0), axis=-1)
    return (slot_top, slot_spread, slot_pick)


def slot_delta(full_logits, row_totals, code_grid):
    offsets = lax.broadcasted_iota(jnp.int32, full_logits.shape, 3)
    target_hit = (offsets == code_grid[..., None]).astype(jnp.float32)
    return (jnp.exp(full_logits - row_totals[..., None]) - target_hit).astype(jnp.bfloat16)


def shards(
    queries,
    enc_keys,
    enc_values,
    source_lengths,
    out_proj,
    dec_state,
    norm_gain,
    norm_bias,
    head_weight,
    shortlist,
    target_slot,
    target_offset,
):
    voc_count = lax.axis_size("vocab")
    row_count = queries.shape[0]
    mem_count = enc_keys.shape[1]
    model_width = out_proj.shape[1]
    width_dev = dec_state.shape[1]
    heads_dev = enc_keys.shape[2] // HD
    q_heads = queries.reshape(row_count, heads_dev, HD)
    key_heads = enc_keys[0].reshape(mem_count, heads_dev, HD)
    value_heads = enc_values[0].reshape(mem_count, heads_dev, HD)
    scores = jnp.einsum("rhe,phe->hrp", q_heads, key_heads, preferred_element_type=jnp.float32) * (
        1.0 / math.sqrt(HD)
    )
    positions = lax.iota(jnp.int32, mem_count)
    usable = (positions < source_lengths[0])[None, None, :]
    scores = jnp.where(usable, scores, MASKED)
    row_top = jnp.max(scores, axis=-1)
    raw_weights = jnp.where(usable, jnp.exp(scores - row_top[..., None]), 0.0)
    totals = jnp.sum(raw_weights, axis=-1)
    mixture = jnp.einsum(
        "hrp,phe->rhe",
        raw_weights.astype(jnp.bfloat16),
        value_heads,
        preferred_element_type=jnp.float32,
    )
    own_mix = mixture / totals.T[..., None]
    attn_own = own_mix.astype(jnp.bfloat16).reshape(row_count, heads_dev * HD)
    projected = lax.psum_scatter(
        lax.dot_general(
            out_proj, attn_own, (((0,), (1,)), ((), ())), preferred_element_type=jnp.float32
        ),
        "src",
        scatter_dimension=0,
        tiled=True,
    )
    residual = dec_state.astype(jnp.float32) + projected.T
    sum_rows, square_rows = lax.psum(
        (jnp.sum(residual, axis=1), jnp.sum(residual * residual, axis=1)), "src"
    )
    row_mean = sum_rows / model_width
    variance = square_rows / model_width - row_mean * row_mean
    inv_std = lax.rsqrt(variance + EPSILON)
    centered = (residual - row_mean[:, None]) * inv_std[:, None]
    normed = (centered * norm_gain + norm_bias).astype(jnp.bfloat16)
    list_count = shortlist.shape[1]
    blocks_dev = head_weight.shape[1] // BLK
    vocab_blocks = blocks_dev * voc_count
    bucket_most = max(2, 2 * row_count * list_count // vocab_blocks)
    slot_total = vocab_blocks * bucket_most
    pair_count = row_count * list_count
    listed = shortlist.reshape(pair_count)
    sort_order = jnp.argsort(listed, stable=True)
    sorted_ids = listed[sort_order]
    firsts = jnp.searchsorted(sorted_ids, sorted_ids, side="left")
    slot_ranks = (
        jnp.zeros((pair_count,), jnp.int32)
        .at[sort_order]
        .set(jnp.arange(pair_count, dtype=jnp.int32) - firsts)
    )
    slot_ids = listed * bucket_most + slot_ranks
    pair_rows = jnp.arange(pair_count, dtype=jnp.int32) // list_count
    pair_lists = jnp.arange(pair_count, dtype=jnp.int32) % list_count
    outgoing = jnp.zeros((slot_total, width_dev), jnp.bfloat16).at[slot_ids].set(normed[pair_rows])
    is_target = pair_lists == target_slot[pair_rows]
    target_codes = (
        jnp.full((slot_total,), -2, jnp.int32)
        .at[slot_ids]
        .set(jnp.where(is_target, target_offset[pair_rows], -1))
    )
    incoming = lax.all_to_all(
        outgoing.reshape(voc_count, blocks_dev * bucket_most, width_dev),
        "vocab",
        split_axis=0,
        concat_axis=0,
        tiled=True,
    )
    in_codes = lax.all_to_all(
        target_codes.reshape(voc_count, blocks_dev * bucket_most),
        "vocab",
        split_axis=0,
        concat_axis=0,
        tiled=True,
    )
    received = incoming.reshape(voc_count, blocks_dev, bucket_most, width_dev)
    code_grid = in_codes.reshape(voc_count, blocks_dev, bucket_most)
    weight_view = head_weight.reshape(width_dev, blocks_dev, BLK)
    partial_logits = jnp.einsum(
        "slmd,dlt->slmt", received, weight_view, preferred_element_type=jnp.float32
    )
    full_logits = lax.psum(partial_logits, "src")
    slot_top, slot_spread, slot_pick = slot_stats(full_logits, code_grid)
    back_top, back_spread, back_pick = (
        lax.all_to_all(
            slot_top.reshape(voc_count, blocks_dev * bucket_most),
            "vocab",
            split_axis=0,
            concat_axis=0,
            tiled=True,
        ),
        lax.all_to_all(
            slot_spread.reshape(voc_count, blocks_dev * bucket_most),
            "vocab",
            split_axis=0,
            concat_axis=0,
            tiled=True,
        ),
        lax.all_to_all(
            slot_pick.reshape(voc_count, blocks_dev * bucket_most),
            "vocab",
            split_axis=0,
            concat_axis=0,
            tiled=True,
        ),
    )
    pair_top = back_top.reshape(slot_total)[slot_ids].reshape(row_count, list_count)
    pair_spread = back_spread.reshape(slot_total)[slot_ids].reshape(row_count, list_count)
    pair_pick = back_pick.reshape(slot_total)[slot_ids].reshape(row_count, list_count)
    row_best = jnp.max(pair_top, axis=1)
    log_total = row_best + jnp.log(
        jnp.sum(jnp.exp(pair_top - row_best[:, None]) * pair_spread, axis=1)
    )
    list_iota = lax.broadcasted_iota(jnp.int32, (row_count, list_count), 1)
    target_logit = jnp.sum(jnp.where(list_iota == target_slot[:, None], pair_pick, 0.0), axis=1)
    row_loss = log_total - target_logit
    total_out = jnp.zeros((slot_total,), jnp.float32).at[slot_ids].set(log_total[pair_rows])
    total_in = lax.all_to_all(
        total_out.reshape(voc_count, blocks_dev * bucket_most),
        "vocab",
        split_axis=0,
        concat_axis=0,
        tiled=True,
    )
    total_in = total_in.reshape(voc_count, blocks_dev, bucket_most)
    deltas = slot_delta(full_logits, total_in, code_grid)
    grad_slots = jnp.einsum(
        "slmt,dlt->slmd", deltas, weight_view, preferred_element_type=jnp.float32
    )
    returned = lax.all_to_all(
        grad_slots.reshape(voc_count, blocks_dev * bucket_most, width_dev).astype(jnp.bfloat16),
        "vocab",
        split_axis=0,
        concat_axis=0,
        tiled=True,
    ).astype(jnp.float32)
    returned = returned.reshape(slot_total, width_dev)
    grad_normed = jnp.sum(returned[slot_ids].reshape(row_count, list_count, width_dev), axis=1)
    gained = grad_normed * norm_gain
    sum_g, sum_gx = lax.psum((jnp.sum(gained, axis=1), jnp.sum(gained * centered, axis=1)), "src")
    grad_state = inv_std[:, None] * (
        gained - (sum_g / model_width)[:, None] - centered * (sum_gx / model_width)[:, None]
    )
    return (row_loss, grad_state)


def solution(mesh):
    placed = (
        P("vocab", "src"),
        P("vocab", None, "src"),
        P("vocab", None, "src"),
        P("vocab"),
        P("src", None),
        P("vocab", "src"),
        P("src"),
        P("src"),
        P("src", "vocab"),
        P("vocab", None),
        P("vocab"),
        P("vocab"),
    )
    return jax.shard_map(
        shards,
        mesh=mesh,
        in_specs=placed,
        out_specs=(P("vocab"), P("vocab", "src")),
        check_vma=False,
    )
```

profile of v0, /device:TPU:1, one launch (start us, length us, event | category | flops | bytes accessed | tf_op | source)
XLA Modules:
  0.0 582.9 jit_solution(5455073962247566520)
XLA Ops:
  17.4 11.8 %gather_fusion.1 = s32[2048]{0:T(1024)S(1)} fusion(s32[2048]{0:T(1024)S(1)} %reshape.164, s32[2048]{0:T(1024)S(1)} %get-tuple-element.111), kind=kCustom, calls=%fused_computation.1 | custom fusion | bytes 24576 | tf_op jit(solution)/shard_map/gather | solution.py:95
  29.2 142.4 %while.25 = (s32[]{:T(128)}, u32[2048]{0:T(1024)S(1)}, u32[2048]{0:T(1024)S(1)}, s32[2048]{0:T(1024)S(1)}, s32[]{:T(128)}, /*index=5*/s32[]{:T(128)}, s32[]{}) while((s32[]{:T(128)}, u32[2048]{0:T(1024)S(1)}, u32[2048]{0:T(1024)S(1)}, s32[2048]{0:T(1024)S(1)}, s32[]{:T(128)}, /*index=5*/s32[]{:T(128)}, s32[]{}) %tuple.49), condition=%wide.region_2.3_spmd.clone, body=%wide.region_1.2_spmd.clone.sunk | while | flops 38916 | bytes 135269 | solution.py:96
  29.2 11.8 %gather_fusion = s32[2048]{0:T(1024)S(1)} fusion(s32[2048]{0:T(1024)S(1)} %get-tuple-element.164, u32[2048]{0:T(1024)S(1)} %broadcast_clamp_fusion.5), kind=kCustom, calls=%fused_computation.clone.clone.1 | custom fusion | bytes 24576 | tf_op jit(solution)/shard_map/jit(searchsorted)/jit(_searchsorted_scan_impl)/vmap(jit(_searchsorted_scan_impl))/while/body/eval_jaxpr/gather | solution.py:96
  41.1 11.8 %gather_fusion = s32[2048]{0:T(1024)S(1)} fusion(s32[2048]{0:T(1024)S(1)} %get-tuple-element.164, u32[2048]{0:T(1024)S(1)} %broadcast_clamp_fusion.5), kind=kCustom, calls=%fused_computation.clone.clone.1 | custom fusion | bytes 24576 | tf_op jit(solution)/shard_map/jit(searchsorted)/jit(_searchsorted_scan_impl)/vmap(jit(_searchsorted_scan_impl))/while/body/eval_jaxpr/gather | solution.py:96
  53.0 11.8 %gather_fusion = s32[2048]{0:T(1024)S(1)} fusion(s32[2048]{0:T(1024)S(1)} %get-tuple-element.164, u32[2048]{0:T(1024)S(1)} %broadcast_clamp_fusion.5), kind=kCustom, calls=%fused_computation.clone.clone.1 | custom fusion | bytes 24576 | tf_op jit(solution)/shard_map/jit(searchsorted)/jit(_searchsorted_scan_impl)/vmap(jit(_searchsorted_scan_impl))/while/body/eval_jaxpr/gather | solution.py:96
  64.8 11.8 %gather_fusion = s32[2048]{0:T(1024)S(1)} fusion(s32[2048]{0:T(1024)S(1)} %get-tuple-element.164, u32[2048]{0:T(1024)S(1)} %broadcast_clamp_fusion.5), kind=kCustom, calls=%fused_computation.clone.clone.1 | custom fusion | bytes 24576 | tf_op jit(solution)/shard_map/jit(searchsorted)/jit(_searchsorted_scan_impl)/vmap(jit(_searchsorted_scan_impl))/while/body/eval_jaxpr/gather | solution.py:96
  76.7 11.8 %gather_fusion = s32[2048]{0:T(1024)S(1)} fusion(s32[2048]{0:T(1024)S(1)} %get-tuple-element.164, u32[2048]{0:T(1024)S(1)} %broadcast_clamp_fusion.5), kind=kCustom, calls=%fused_computation.clone.clone.1 | custom fusion | bytes 24576 | tf_op jit(solution)/shard_map/jit(searchsorted)/jit(_searchsorted_scan_impl)/vmap(jit(_searchsorted_scan_impl))/while/body/eval_jaxpr/gather | solution.py:96
  88.6 11.8 %gather_fusion = s32[2048]{0:T(1024)S(1)} fusion(s32[2048]{0:T(1024)S(1)} %get-tuple-element.164, u32[2048]{0:T(1024)S(1)} %broadcast_clamp_fusion.5), kind=kCustom, calls=%fused_computation.clone.clone.1 | custom fusion | bytes 24576 | tf_op jit(solution)/shard_map/jit(searchsorted)/jit(_searchsorted_scan_impl)/vmap(jit(_searchsorted_scan_impl))/while/body/eval_jaxpr/gather | solution.py:96
  100.4 11.8 %gather_fusion = s32[2048]{0:T(1024)S(1)} fusion(s32[2048]{0:T(1024)S(1)} %get-tuple-element.164, u32[2048]{0:T(1024)S(1)} %broadcast_clamp_fusion.5), kind=kCustom, calls=%fused_computation.clone.clone.1 | custom fusion | bytes 24576 | tf_op jit(solution)/shard_map/jit(searchsorted)/jit(_searchsorted_scan_impl)/vmap(jit(_searchsorted_scan_impl))/while/body/eval_jaxpr/gather | solution.py:96
  112.3 11.8 %gather_fusion = s32[2048]{0:T(1024)S(1)} fusion(s32[2048]{0:T(1024)S(1)} %get-tuple-element.164, u32[2048]{0:T(1024)S(1)} %broadcast_clamp_fusion.5), kind=kCustom, calls=%fused_computation.clone.clone.1 | custom fusion | bytes 24576 | tf_op jit(solution)/shard_map/jit(searchsorted)/jit(_searchsorted_scan_impl)/vmap(jit(_searchsorted_scan_impl))/while/body/eval_jaxpr/gather | solution.py:96
  124.2 11.8 %gather_fusion = s32[2048]{0:T(1024)S(1)} fusion(s32[2048]{0:T(1024)S(1)} %get-tuple-element.164, u32[2048]{0:T(1024)S(1)} %broadcast_clamp_fusion.5), kind=kCustom, calls=%fused_computation.clone.clone.1 | custom fusion | bytes 24576 | tf_op jit(solution)/shard_map/jit(searchsorted)/jit(_searchsorted_scan_impl)/vmap(jit(_searchsorted_scan_impl))/while/body/eval_jaxpr/gather | solution.py:96
  136.0 11.8 %gather_fusion = s32[2048]{0:T(1024)S(1)} fusion(s32[2048]{0:T(1024)S(1)} %get-tuple-element.164, u32[2048]{0:T(1024)S(1)} %broadcast_clamp_fusion.5), kind=kCustom, calls=%fused_computation.clone.clone.1 | custom fusion | bytes 24576 | tf_op jit(solution)/shard_map/jit(searchsorted)/jit(_searchsorted_scan_impl)/vmap(jit(_searchsorted_scan_impl))/while/body/eval_jaxpr/gather | solution.py:96
  147.9 11.8 %gather_fusion = s32[2048]{0:T(1024)S(1)} fusion(s32[2048]{0:T(1024)S(1)} %get-tuple-element.164, u32[2048]{0:T(1024)S(1)} %broadcast_clamp_fusion.5), kind=kCustom, calls=%fused_computation.clone.clone.1 | custom fusion | bytes 24576 | tf_op jit(solution)/shard_map/jit(searchsorted)/jit(_searchsorted_scan_impl)/vmap(jit(_searchsorted_scan_impl))/while/body/eval_jaxpr/gather | solution.py:96
  159.8 11.8 %gather_fusion = s32[2048]{0:T(1024)S(1)} fusion(s32[2048]{0:T(1024)S(1)} %get-tuple-element.164, u32[2048]{0:T(1024)S(1)} %broadcast_clamp_fusion.5), kind=kCustom, calls=%fused_computation.clone.clone.1 | custom fusion | bytes 24576 | tf_op jit(solution)/shard_map/jit(searchsorted)/jit(_searchsorted_scan_impl)/vmap(jit(_searchsorted_scan_impl))/while/body/eval_jaxpr/gather | solution.py:96
  180.8 29.7 %all-reduce.1 = (f32[256]{0:T(256)S(1)}, f32[256]{0:T(256)S(1)}) all-reduce(f32[256]{0:T(256)S(1)} %get-tuple-element.90, f32[256]{0:T(256)S(1)} %get-tuple-element.89), channel_id=1, replica_groups=mesh['src'=16,'vocab'=32] {'src'}, use_global_device_ids=true, to_apply=%region_10.11 | all-reduce | flops 512 | bytes 4096 | tf_op jit(solution)/shard_map/psum | solution.py:79
  211.6 12.2 %scatter_custom_fusion.1 = bf16[4032,128]{1,0:T(8,128)(2,1)S(1)} fusion(s32[2048]{0:T(1024)S(1)} %get-tuple-element.110, bf16[256,128]{1,0:T(8,128)(2,1)S(1)} %add_convert_fusion, s32[2048]{0:T(1024)S(1)} %get-tuple-element.117, bf16[]{:T(256)} %constant.75.clone.1), kind=kCustom, calls=%fused_computation.34 | custom fusion | bytes 1032194 | tf_op jit(solution)/shard_map/scatter | solution.py:105
  225.1 8.3 %all-to-all-start = ((bf16[32,126,128]{2,1,0:T(8,128)(2,1)}), bf16[32,126,128]{2,1,0:T(8,128)(2,1)}, u32[]{:S(2)}, u32[]{:S(2)}) async-start(bf16[32,126,128]{2,1,0:T(8,128)(2,1)} %reshape.168), calls=%async_computation.1 | async-start | bytes 2097152 | tf_op jit(solution)/shard_map/all_to_all | solution.py:112
  236.4 19.0 %all-to-all-done = bf16[32,126,128]{2,1,0:T(8,128)(2,1)} async-done(((bf16[32,126,128]{2,1,0:T(8,128)(2,1)}), bf16[32,126,128]{2,1,0:T(8,128)(2,1)}, u32[]{:S(2)}, u32[]{:S(2)}) %all-to-all-start) | async-done | bytes 1032224 | tf_op jit(solution)/shard_map/all_to_all | solution.py:112
  260.7 13.1 %gather_fusion.4 = s32[2048]{0:T(1024)S(1)} fusion(s32[256]{0:T(256)S(1)} %copy-done.1, s32[2048]{0:T(1024)S(1)} %get-tuple-element.117), kind=kCustom, calls=%fused_computation.5 | custom fusion | bytes 24576 | tf_op jit(solution)/shard_map/gather | solution.py:106
  273.9 13.1 %gather_fusion.5 = s32[2048]{0:T(1024)S(1)} fusion(s32[256]{0:T(256)S(1)} %copy-done.2, s32[2048]{0:T(1024)S(1)} %get-tuple-element.117), kind=kCustom, calls=%fused_computation.6 | custom fusion | bytes 24576 | tf_op jit(solution)/shard_map/gather | solution.py:110
  287.1 8.2 %scatter_custom_fusion.2 = s32[4032]{0:T(1024)S(1)} fusion(s32[2048]{0:T(1024)S(1)} %get-tuple-element.110, s32[2048]{0:T(1024)S(1)} %fusion.31, s32[]{:T(128)} %constant.93.clone.1), kind=kCustom, calls=%fused_computation.70 | custom fusion | bytes 16132 | tf_op jit(solution)/shard_map/scatter | solution.py:110
  295.4 17.2 %all_to_all.55 = s32[32,1,126]{2,1,0:T(1,128)S(1)} all-to-all(s32[32,1,126]{2,1,0:T(1,128)S(1)} %bitcast.79), channel_id=1, replica_groups=mesh['src'=16,'vocab'=32] {'vocab'}, dimensions={0} | all-to-all | bytes 32256 | tf_op jit(solution)/shard_map/all_to_all | solution.py:119
  312.8 70.9 %all-reduce.4.cloned.1.call-done = f32[32,63,2,128]{3,0,2,1:T(8,128)} async-done(((f32[32,63,2,128]{3,0,2,1:T(8,128)}), f32[32,63,2,128]{3,0,2,1:T(8,128)}) %all-reduce.4.cloned.1.call-update) | async-done | bytes 2064400 | tf_op jit(solution)/shard_map/psum | solution.py:132
  390.6 9.9 %all-to-all-start.2 = ((f32[32,1,126]{2,1,0:T(1,128)}), f32[32,1,126]{2,1,0:T(1,128)S(1)}, u32[]{:S(2)}, u32[]{:S(2)}) async-start(f32[32,1,126]{2,1,0:T(1,128)} %copy.42), calls=%async_computation.3 | async-start | bytes 32768 | tf_op jit(solution)/shard_map/all_to_all | solution.py:142
  426.7 11.8 %gather_fusion.3 = f32[2048]{0:T(1024)S(1)} fusion(f32[4032]{0:T(1024)S(1)} %reshape.173, s32[2048]{0:T(1024)S(1)} %get-tuple-element.109), kind=kCustom, calls=%fused_computation.4 | custom fusion | bytes 24576 | tf_op jit(solution)/shard_map/gather | solution.py:158
  439.4 11.8 %gather_fusion.2 = f32[2048]{0:T(1024)S(1)} fusion(f32[4032]{0:T(1024)S(1)} %reshape.171, s32[2048]{0:T(1024)S(1)} %get-tuple-element.109), kind=kCustom, calls=%fused_computation.3 | custom fusion | bytes 24576 | tf_op jit(solution)/shard_map/gather | solution.py:157
  452.2 11.8 %gather_fusion.6 = f32[2048]{0:T(1024)S(1)} fusion(f32[4032]{0:T(1024)S(1)} %reshape.175, s32[2048]{0:T(1024)S(1)} %get-tuple-element.109), kind=kCustom, calls=%fused_computation.7 | custom fusion | bytes 24576 | tf_op jit(solution)/shard_map/gather | solution.py:159
  465.1 13.1 %gather_fusion.7 = f32[2048]{0:T(1024)S(1)} fusion(f32[256]{0:T(256)S(1)} %get-tuple-element.108, s32[2048]{0:T(1024)S(1)} %get-tuple-element.117), kind=kCustom, calls=%fused_computation.8 | custom fusion | bytes 24576 | tf_op jit(solution)/shard_map/gather | solution.py:167
  478.2 8.1 %scatter_custom_fusion.3 = f32[4032]{0:T(1024)S(1)} fusion(s32[2048]{0:T(1024)S(1)} %get-tuple-element.110, f32[2048]{0:T(1024)S(1)} %gather_fusion.7, f32[]{:T(128)} %constant.85.clone.1), kind=kCustom, calls=%fused_computation.65 | custom fusion | bytes 16132 | tf_op jit(solution)/shard_map/scatter | solution.py:167
  486.4 17.7 %all_to_all.56 = f32[32,1,126]{2,1,0:T(1,128)S(1)} all-to-all(f32[32,1,126]{2,1,0:T(1,128)S(1)} %bitcast.80), channel_id=1, replica_groups=mesh['src'=16,'vocab'=32] {'vocab'}, dimensions={0} | all-to-all | bytes 32256 | tf_op jit(solution)/shard_map/all_to_all | solution.py:168
  507.4 23.7 %all_to_all.57 = bf16[32,126,128]{2,1,0:T(8,128)(2,1)} all-to-all(bf16[32,126,128]{2,1,0:T(8,128)(2,1)S(1)} %copy.49), channel_id=1, replica_groups=mesh['src'=16,'vocab'=32] {'vocab'}, dimensions={0} | all-to-all | bytes 2064384 | tf_op jit(solution)/shard_map/all_to_all | solution.py:180
  541.8 33.4 %all-reduce = (f32[256]{0:T(256)S(1)}, f32[256]{0:T(256)S(1)}) all-reduce(f32[256]{0:T(256)S(1)} %get-tuple-element.92, f32[256]{0:T(256)S(1)} %get-tuple-element.91), channel_id=1, replica_groups=mesh['src'=16,'vocab'=32] {'src'}, use_global_device_ids=true, to_apply=%region_25.26 | all-reduce | flops 512 | bytes 4096 | tf_op jit(solution)/shard_map/psum | solution.py:190
  (134 shorter events, 80.8 us)
Async XLA Ops:
  7.2 2.0 copy-start
  7.2 172.6 %reduce-scatter.2.cloned.1.call-start = ((), (), s32[]{:S(2)}) async-start(), calls=%async_computation.8 | async-start | bytes 2228224 | tf_op jit(solution)/shard_map/reduce_scatter | solution.py:70
  9.2 2.9 copy-start.5
  29.2 150.6 %copy-start.4 = (bf16[256,128]{1,0:T(8,128)(2,1)S(1)}, bf16[256,128]{1,0:T(8,128)(2,1)}, u32[]{:S(2)}) copy-start(bf16[256,128]{1,0:T(8,128)(2,1)} %param.19) | copy-start | bytes 196612
  29.2 181.4 %copy-start.6 = (f32[128]{0:T(128)S(1)}, f32[128]{0:T(128)}, u32[]{:S(2)}) copy-start(f32[128]{0:T(128)} %param.20) | copy-start | bytes 1540
  29.2 181.4 %copy-start.7 = (f32[128]{0:T(128)S(1)}, f32[128]{0:T(128)}, u32[]{:S(2)}) copy-start(f32[128]{0:T(128)} %param.21) | copy-start | bytes 1540
  225.1 30.2 %all-to-all-start = ((bf16[32,126,128]{2,1,0:T(8,128)(2,1)}), bf16[32,126,128]{2,1,0:T(8,128)(2,1)}, u32[]{:S(2)}, u32[]{:S(2)}) async-start(bf16[32,126,128]{2,1,0:T(8,128)(2,1)} %reshape.168), calls=%async_computation.1 | async-start | bytes 2097152 | tf_op jit(solution)/shard_map/all_to_all | solution.py:112
  233.4 150.3 %all-reduce.4.cloned.1.call-start = ((), (), s32[]{:S(2)}) async-start(), calls=%async_computation.9 | async-start | bytes 4128768 | tf_op jit(solution)/shard_map/psum | solution.py:132
  260.1 0.7 copy-start.1
  260.7 13.1 %copy-start.2 = (s32[256]{0:T(256)S(1)}, s32[256]{0:T(256)}, u32[]{:S(2)}) copy-start(s32[256]{0:T(256)} %param.25) | copy-start | bytes 3076
  390.6 18.5 %all-to-all-start.2 = ((f32[32,1,126]{2,1,0:T(1,128)}), f32[32,1,126]{2,1,0:T(1,128)S(1)}, u32[]{:S(2)}, u32[]{:S(2)}) async-start(f32[32,1,126]{2,1,0:T(1,128)} %copy.42), calls=%async_computation.3 | async-start | bytes 32768 | tf_op jit(solution)/shard_map/all_to_all | solution.py:142
  409.1 12.5 %all-to-all-start.1 = ((f32[32,1,126]{2,1,0:T(1,128)}), f32[32,1,126]{2,1,0:T(1,128)S(1)}, u32[]{:S(2)}, u32[]{:S(2)}) async-start(f32[32,1,126]{2,1,0:T(1,128)} %copy.41), calls=%async_computation.2 | async-start | bytes 32768 | tf_op jit(solution)/shard_map/all_to_all | solution.py:135
  421.6 29.9 %all-to-all-start.4 = ((f32[32,1,126]{2,1,0:T(1,128)}), f32[32,1,126]{2,1,0:T(1,128)S(1)}, u32[]{:S(2)}, u32[]{:S(2)}) async-start(f32[32,1,126]{2,1,0:T(1,128)} %copy.45), calls=%async_computation.5 | async-start | bytes 32768 | tf_op jit(solution)/shard_map/all_to_all | solution.py:149
  532.5 9.1 %copy-start.3 = (f32[128,256]{0,1:T(8,128)S(1)}, f32[128,256]{0,1:T(8,128)}, u32[]{:S(2)}) copy-start(f32[128,256]{0,1:T(8,128)} %reduce-scatter.2.cloned.1.call-done) | copy-start | bytes 393220
Sparse Core Ops, SparseCore 0:
  12.2 66.1 reduce-scatter.1
  260.2 123.4 all-reduce.3
where the time goes:
time: 584 us; the launch traced here: 583 us
  local copies, waits for them, and re-layouts  285 us (49%)
  blocking collectives  122 us (21%)
  waiting for transfers between devices  106 us (18%)
  starting transfers between devices  26 us (4%)
  other arithmetic  19.5 us (3%)
  between operations  15.2 us (3%)
  matrix products  9.54 us (2%)
    gather x12, local copies, waits for them, and re-layouts, shards(): firsts = jnp.searchsorted(sorted_ids, sorted_ids, side='left')  141 us
    psum x1, waiting for transfers between devices, shards(): full_logits = lax.psum(partial_logits, 'src')  70.9 us
    psum x1, blocking collectives, shards(): lax.psum((jnp.sum(gained, axis=1), jnp.sum(gained * centered, axis=1)), '...  33.4 us
    psum x1, blocking collectives, shards(): lax.psum((jnp.sum(residual, axis=1), jnp.sum(residual * residual, axis=1)...  29.7 us
    all_to_all x1, blocking collectives, shards(): lax.all_to_all(grad_slots.reshape(voc_count, blocks_dev * bucket_most, wi...  23.7 us
    all_to_all x1, waiting for transfers between devices, shards(): lax.all_to_all(outgoing.reshape(voc_count, blocks_dev * bucket_most, widt...  19 us
    all_to_all x1, blocking collectives, shards(): lax.all_to_all(total_out.reshape(voc_count, blocks_dev * bucket_most), 'v...  17.7 us
    all_to_all x1, blocking collectives, shards(): lax.all_to_all(target_codes.reshape(voc_count, blocks_dev * bucket_most),...  17.2 us
  transfers between devices with their start and end apart: 6, of which 4 were waited for; matrix products, arithmetic and copies ran while one was open for 40% of the time, Pallas kernels for 0%

commit v1 on v0

v1 whole, which is shorter than its diff:
```python
import math

import jax
import jax.numpy as jnp
from jax import lax
from jax.experimental import pallas as pl
from jax.experimental.pallas import tpu as pltpu
from jax.sharding import PartitionSpec as P

HD = 128
BLK = 128
MOST = 2
EPSILON = 1e-05
MASKED = -1e30
F32 = jnp.float32
BF16 = jnp.bfloat16
I32 = jnp.int32

VM = pl.BlockSpec(memory_space=pltpu.VMEM)
SM = pl.BlockSpec(memory_space=pltpu.SMEM)


def call(body, outs, specs, scratch=(), name=None):
    return pl.pallas_call(
        body,
        out_shape=tuple(jax.ShapeDtypeStruct(s, d) for s, d in outs),
        in_specs=specs,
        out_specs=tuple(VM for _ in outs),
        scratch_shapes=list(scratch),
        name=name,
    )


def dot(a, b, ca, cb):
    return lax.dot_general(a, b, (((ca,), (cb,)), ((), ())), preferred_element_type=F32)


def thirds(x):
    hi = x.astype(BF16)
    rest = x - hi.astype(F32)
    mid = rest.astype(BF16)
    low = (rest - mid.astype(F32)).astype(BF16)
    return hi, mid, low


def pack_kernel(head_ref, wsend_ref):
    groups, width, tokens = wsend_ref.shape
    last = head_ref.shape[1] - (groups - 1) * tokens
    for u in range(groups - 1):
        wsend_ref[u] = head_ref[:, u * tokens : (u + 1) * tokens]
    wsend_ref[groups - 1, :, :last] = head_ref[:, (groups - 1) * tokens :]
    if last < tokens:
        wsend_ref[groups - 1, :, last:] = jnp.zeros((width, tokens - last), BF16)


def slots_kernel(where_ref, list_ref, tslot_ref, toff_ref, m_ref, mj_ref, code_ref, *, blocks, group, most):
    pieces = group * most
    slots, rows = m_ref.shape
    vocs = code_ref.shape[0] // pieces
    listed = list_ref[...]
    picks = listed.shape[0]
    r0 = lax.broadcasted_iota(I32, (rows, rows), 0)
    r1 = lax.broadcasted_iota(I32, (rows, rows), 1)
    earlier = (r0 < r1).astype(F32).astype(BF16)
    tslot = tslot_ref[...]
    target_block = jnp.zeros((1, rows), I32)
    for k in range(picks):
        target_block = jnp.where(tslot == k, listed[k : k + 1, :], target_block)

    def mask_of(u, v, j):
        local = u * group + lax.rem(j, group)
        block = jnp.where(local < blocks, v * blocks + local, -1)
        named = block == listed[0:1, :]
        for k in range(1, picks):
            named = jnp.logical_or(named, block == listed[k : k + 1, :])
        named = named.astype(F32)
        rank = dot(named.astype(BF16), earlier, 1, 0)
        want = lax.div(j, group).astype(F32)
        return jnp.where(rank == want, named, 0.0), block

    step = 512
    span = vocs * pieces
    sub = lax.broadcasted_iota(I32, (step, 1), 0)

    def travel(t, carry):
        i = t * step + sub
        u = lax.div(i, span)
        v = lax.div(lax.rem(i, span), pieces)
        j = lax.rem(i, pieces)
        m, _ = mask_of(u, v, j)
        m_ref[pl.ds(pl.multiple_of(t * step, step), step), :] = m.astype(BF16)
        return carry

    lax.fori_loop(0, slots // step, travel, 0)
    pairs = slots // pieces

    def major(t, carry):
        w = lax.broadcasted_iota(I32, (pairs, 1), 0)
        m, _ = mask_of(lax.div(w, vocs), lax.rem(w, vocs), jnp.full((pairs, 1), t, I32))
        mj_ref[t] = m.astype(BF16)
        return carry

    lax.fori_loop(0, pieces, major, 0)

    i = lax.broadcasted_iota(I32, (span, 1), 0)
    m, block = mask_of(jnp.full((span, 1), where_ref[0], I32), lax.div(i, pieces), lax.rem(i, pieces))
    hit = jnp.where(block == target_block, toff_ref[...].astype(F32) + 1.0, 0.0)
    code = jnp.sum(m * (hit + 1.0), axis=1, keepdims=True) - 2.0
    code_ref[...] = jnp.broadcast_to(code, code_ref.shape)


EXTRA = 16


def attend_kernel(len_ref, q_ref, k_ref, v_ref, proj_ref, dec_ref, gain_ref, bias_ref, out_ref):
    groups, _, width = out_ref.shape
    rows = q_ref.shape[0]
    scores = dot(q_ref[...], k_ref[0], 1, 1) * (1.0 / math.sqrt(HD))
    usable = lax.broadcasted_iota(I32, scores.shape, 1) < len_ref[0]
    scores = jnp.where(usable, scores, MASKED)
    top = jnp.max(scores, axis=1, keepdims=True)
    raw = jnp.where(usable, jnp.exp(scores - top), 0.0)
    totals = jnp.sum(raw, axis=1, keepdims=True)
    mixed = dot(raw.astype(BF16), v_ref[0], 1, 0)
    att = (mixed / totals).astype(BF16)
    proj_sums = jnp.zeros((8, width), F32)
    ones = jnp.ones((8, width), BF16)
    for u in range(groups):
        piece = proj_ref[:, u * width : (u + 1) * width]
        out_ref[u, :rows, :] = dot(att, piece, 1, 0).astype(BF16)
        proj_sums = proj_sums + dot(ones, piece, 1, 1)
    part = dot(ones, dec_ref[...], 1, 1)
    for third in thirds(proj_sums):
        part = part + dot(third, att, 1, 1)
    sub = lax.broadcasted_iota(I32, (EXTRA, width), 0)
    extra = jnp.zeros((EXTRA, width), F32)
    lines = []
    for third in thirds(part[0:1, :]):
        lines += [third[:, c * 128 : (c + 1) * 128] for c in range(rows // 128)]
    lines += list(thirds(gain_ref[...])) + list(thirds(bias_ref[...]))
    for n, line in enumerate(lines):
        extra = jnp.where(sub == n, line.astype(F32), extra)
    extra = extra.astype(BF16)
    for u in range(groups):
        out_ref[u, rows:, :] = extra


def residual_kernel(part_ref, dec_ref, gain_ref, m_ref, c_ref, extra_ref, out_ref):
    groups, _, width = part_ref.shape
    rows = dec_ref.shape[0]
    acc = dec_ref[...].astype(F32)
    lines = jnp.zeros((EXTRA, width), F32)
    for u in range(groups):
        acc = acc + part_ref[u, :rows, :].astype(F32)
        lines = lines + part_ref[u, rows:, :].astype(F32)
        extra_ref[u] = part_ref[u, rows:, :]
    n = rows // 128
    halves = []
    for c in range(n):
        line = lines[c : c + 1] + lines[n + c : n + c + 1] + lines[2 * n + c : 2 * n + c + 1]
        halves.append(jnp.transpose(jnp.broadcast_to(line, (8, 128)))[:, 0:1])
    mean = jnp.concatenate(halves, axis=0) / (groups * width)
    c = acc - mean
    c_ref[...] = c
    x = (c * gain_ref[...]).astype(BF16)
    out_ref[...] = dot(m_ref[...], x, 1, 0).astype(BF16)


def spread_lanes(cols, shape):
    lane = lax.broadcasted_iota(I32, shape, 1)
    out = jnp.zeros(shape, F32)
    for n, col in enumerate(cols):
        out = jnp.where(lane == n, col, out)
    return out


STATS = 8


def score_kernel(x_ref, w_ref, extra_ref, code_ref, l_ref, row_ref, stat_ref, *, group, lines):
    groups, slots, width = x_ref.shape
    pieces = 2 * group
    tokens = group * BLK
    acc = jnp.zeros((slots, tokens), F32)
    sums = jnp.zeros((EXTRA, tokens), F32)
    squares = jnp.zeros((slots, width), F32)
    for u in range(groups):
        x = x_ref[u]
        w = w_ref[u]
        acc = acc + dot(x, w, 1, 0)
        small = extra_ref[u]
        gain = small.astype(F32)
        gain = gain[lines : lines + 1] + gain[lines + 1 : lines + 2] + gain[lines + 2 : lines + 3]
        plain = x.astype(F32) / gain
        squares = squares + plain * plain
        sums = sums + dot(small, w, 1, 0)
    wg = sums[lines : lines + 1] + sums[lines + 1 : lines + 2] + sums[lines + 2 : lines + 3]
    wb = sums[lines + 3 : lines + 4] + sums[lines + 4 : lines + 5] + sums[lines + 5 : lines + 6]
    inv = lax.rsqrt(jnp.sum(squares, axis=1, keepdims=True) / (groups * width) + EPSILON)
    place = lax.rem(lax.broadcasted_iota(I32, (slots, 1), 0), group)
    dots = acc[:, 0:BLK]
    gains = jnp.broadcast_to(wg[:, 0:BLK], dots.shape)
    biases = jnp.broadcast_to(wb[:, 0:BLK], dots.shape)
    for b in range(1, group):
        here = place == b
        cut = slice(b * BLK, (b + 1) * BLK)
        dots = jnp.where(here, acc[:, cut], dots)
        gains = jnp.where(here, wg[:, cut], gains)
        biases = jnp.where(here, wb[:, cut], biases)
    bare = inv * dots
    logits = bare + biases
    l_ref[...] = logits
    top = jnp.max(logits, axis=1, keepdims=True)
    shifted = jnp.exp(logits - top)
    spread = jnp.sum(shifted, axis=1, keepdims=True)
    lse = top + jnp.log(spread)
    soft = shifted / spread
    lane = lax.broadcasted_iota(I32, logits.shape, 1).astype(F32)
    hit = lane == code_ref[...]

    def row_sum(v):
        return jnp.sum(v, axis=1, keepdims=True)

    stat_ref[...] = spread_lanes(
        [
            lse,
            row_sum(jnp.where(hit, logits, 0.0)),
            inv,
            row_sum(soft * gains),
            row_sum(soft * bare),
            row_sum(jnp.where(hit, gains, 0.0)),
            row_sum(jnp.where(hit, bare, 0.0)),
        ],
        logits.shape,
    )
    sents = slots // pieces
    lane_s = lax.broadcasted_iota(I32, (sents, 128), 1)
    packed = jnp.zeros((sents, 128), F32)
    for j in range(pieces):
        z = stat_ref[pl.ds(j, sents, stride=pieces), :]
        if j:
            z = pltpu.roll(z, j * STATS, 1)
        packed = jnp.where(lane_s // STATS == j, z, packed)
    for u in range(groups):
        row_ref[u * sents : (u + 1) * sents, :] = packed


def total_kernel(where_ref, e_ref, mj_ref, m_ref, tot_ref, loss_ref, back_ref):
    pieces, pairs, rows = mj_ref.shape
    low = jnp.full((1, rows), MASKED, F32)
    for j in range(pieces):
        lse = e_ref[:, j * STATS : j * STATS + 1]
        low = jnp.maximum(low, jnp.max(jnp.where(mj_ref[j].astype(F32) > 0.0, lse, MASKED), axis=0, keepdims=True))
    total = jnp.zeros((1, rows), F32)
    picked = jnp.zeros((1, rows), F32)
    for j in range(pieces):
        there = mj_ref[j].astype(F32) > 0.0
        lse = e_ref[:, j * STATS : j * STATS + 1]
        pick = e_ref[:, j * STATS + 1 : j * STATS + 2]
        total = total + jnp.sum(jnp.where(there, jnp.exp(lse - low), 0.0), axis=0, keepdims=True)
        picked = picked + jnp.sum(jnp.where(there, pick, 0.0), axis=0, keepdims=True)
    log_total = low + jnp.log(total)
    tot_ref[...] = jnp.broadcast_to(log_total, tot_ref.shape)
    loss_ref[...] = log_total - picked
    slots = back_ref.shape[0]
    own = m_ref[pl.ds(pl.multiple_of(where_ref[0] * slots, slots), slots), :].astype(F32)
    back_ref[...] = jnp.broadcast_to(jnp.sum(own * log_total, axis=1, keepdims=True), back_ref.shape)


def delta_kernel(l_ref, code_ref, back_ref, w_ref, out_ref, *, group):
    groups, width, tokens = w_ref.shape
    logits = l_ref[...]
    code = code_ref[...]
    lane = lax.broadcasted_iota(I32, logits.shape, 1).astype(F32)
    deltas = jnp.exp(logits - back_ref[...]) - jnp.where(lane == code, 1.0, 0.0)
    deltas = jnp.where(code > -1.5, deltas, 0.0)
    place = lax.rem(lax.broadcasted_iota(I32, logits.shape, 0), group)
    wide = jnp.concatenate([jnp.where(place == b, deltas, 0.0) for b in range(group)], axis=1).astype(BF16)
    for u in range(groups):
        out_ref[u] = dot(wide, w_ref[u], 1, 1).astype(BF16)


def sums_kernel(e_ref, mj_ref, tot_ref, out_ref):
    pieces, pairs, rows = mj_ref.shape
    log_total = tot_ref[0:1, :]
    sum_g = jnp.zeros((1, rows), F32)
    sum_gx = jnp.zeros((1, rows), F32)
    inv = jnp.zeros((1, rows), F32)
    for j in range(pieces):
        there = mj_ref[j].astype(F32) > 0.0

        def col(n):
            return e_ref[:, j * STATS + n : j * STATS + n + 1]

        share = jnp.where(there, jnp.exp(col(0) - log_total), 0.0)
        sum_g = sum_g + jnp.sum(jnp.where(there, share * col(3) - col(5), 0.0), axis=0, keepdims=True)
        sum_gx = sum_gx + jnp.sum(jnp.where(there, share * col(4) - col(6), 0.0), axis=0, keepdims=True)
        inv = jnp.maximum(inv, jnp.max(jnp.where(there, col(2), 0.0), axis=0, keepdims=True))
    sub = lax.broadcasted_iota(I32, (8, rows), 0)
    out = jnp.where(sub == 0, sum_g, jnp.where(sub == 1, sum_gx, inv))
    out_ref[...] = out


def final_kernel(r_ref, m_ref, c_ref, gain_ref, sums_ref, out_ref, *, total):
    grad = dot(m_ref[...], r_ref[...], 0, 0)
    rows = grad.shape[0]
    cols = jnp.concatenate(
        [jnp.transpose(sums_ref[:, c * 128 : (c + 1) * 128])[:, 0:3] for c in range(rows // 128)], axis=0
    )
    inv = cols[:, 2:3]
    g = grad * gain_ref[...]
    centered = c_ref[...] * inv
    out_ref[...] = inv * (g - cols[:, 0:1] / total - centered * (cols[:, 1:2] / total))


def shards(
    queries,
    enc_keys,
    enc_values,
    source_lengths,
    out_proj,
    dec_state,
    norm_gain,
    norm_bias,
    head_weight,
    shortlist,
    target_slot,
    target_offset,
):
    vocs = lax.axis_size("vocab")
    groups = lax.axis_size("src")
    both = ("src", "vocab")
    rows, width = dec_state.shape
    total = out_proj.shape[1]
    blocks = head_weight.shape[1] // BLK
    group = -(-blocks // groups)
    tokens = group * BLK
    pieces = group * MOST
    pairs = groups * vocs
    slots = pairs * pieces
    here = lax.axis_index("src").reshape(1).astype(I32)
    gain = norm_gain.reshape(1, width)
    bias = norm_bias.reshape(1, width)

    def exchange(x, axis):
        return lax.all_to_all(x, axis, split_axis=0, concat_axis=0, tiled=True)

    (parts,) = call(attend_kernel, [((groups, rows + EXTRA, width), BF16)], [SM] + [VM] * 7, name="attend")(
        source_lengths, queries, enc_keys, enc_values, out_proj, dec_state, gain, bias
    )
    parts = exchange(parts, "src")
    (wsend,) = call(pack_kernel, [((groups, width, tokens), BF16)], [VM], name="pack")(head_weight)
    win = exchange(wsend, "src")
    m, mj, code = call(
        lambda *refs: slots_kernel(*refs, blocks=blocks, group=group, most=MOST),
        [((slots, rows), BF16), ((pieces, pairs, rows), BF16), ((vocs * pieces, 128), F32)],
        [SM, VM, VM, VM],
        name="slots",
    )(here, shortlist.T, target_slot.reshape(1, rows), target_offset.reshape(1, rows))
    codes = exchange(code.reshape(vocs, pieces, 128), "vocab").reshape(vocs * pieces, 128)
    c, extras, outgoing = call(
        residual_kernel,
        [((rows, width), F32), ((groups, EXTRA, width), BF16), ((slots, width), BF16)],
        [VM] * 4,
        name="residual",
    )(parts, dec_state, gain, m)
    incoming = exchange(outgoing.reshape(pairs, pieces, width), both)
    logits, stats = call(
        lambda *refs: score_kernel(*refs, group=group, lines=3 * (rows // 128)),
        [((vocs * pieces, BLK), F32), ((pairs, 128), F32)],
        [VM] * 4,
        scratch=[pltpu.VMEM((vocs * pieces, BLK), F32)],
        name="score",
    )(incoming.reshape(groups, vocs * pieces, width), win, extras, codes)
    back_stats = exchange(stats.reshape(pairs, 1, 128), both).reshape(pairs, 128)
    totals, loss, back = call(
        total_kernel,
        [((8, rows), F32), ((1, rows), F32), ((vocs * pieces, 128), F32)],
        [SM, VM, VM, VM],
        name="total",
    )(here, back_stats, mj, m)
    back_in = exchange(back.reshape(vocs, pieces, 128), "vocab").reshape(vocs * pieces, 128)
    (grads,) = call(
        lambda *refs: delta_kernel(*refs, group=group),
        [((groups, vocs * pieces, width), BF16)],
        [VM] * 4,
        name="delta",
    )(logits, codes, back_in, win)
    returned = exchange(grads.reshape(pairs, pieces, width), both).reshape(slots, width)
    (sums,) = call(sums_kernel, [((8, rows), F32)], [VM] * 3, name="sums")(back_stats, mj, totals)
    (grad_state,) = call(
        lambda *refs: final_kernel(*refs, total=total), [((rows, width), F32)], [VM] * 5, name="final"
    )(returned, m, c, gain, sums)
    return (loss.reshape(rows), grad_state)


def solution(mesh):
    placed = (
        P("vocab", "src"),
        P("vocab", None, "src"),
        P("vocab", None, "src"),
        P("vocab"),
        P("src", None),
        P("vocab", "src"),
        P("src"),
        P("src"),
        P("src", "vocab"),
        P("vocab", None),
        P("vocab"),
        P("vocab"),
    )
    return jax.shard_map(
        shards,
        mesh=mesh,
        in_specs=placed,
        out_specs=(P("vocab"), P("vocab", "src")),
        check_vma=False,
    )
```

time: 584 us -> 276 us (0.47)
  local copies, waits for them, and re-layouts: 285 us -> 0.98 us
  Pallas kernels: 0 us -> 46.9 us
  blocking collectives: 122 us -> 86.6 us
  other arithmetic: 19.5 us -> 0 us
  between operations: 15.2 us -> 1.33 us
  starting transfers between devices: 26 us -> 36.8 us
  matrix products: 9.54 us -> 0 us
    gather x20 -> x0, local copies, waits for them, and re-layouts: 235 us -> none  [the longest x12 141 us: shards(): firsts = jnp.searchsorted(sorted_ids, sorted_ids, side='left')]
    psum x1 -> x0, waiting for transfers between devices: 70.9 us -> none  [shards(): full_logits = lax.psum(partial_logits, 'src')]
    all_to_all x4, waiting for transfers between devices: 34.7 us -> 103 us  [exchange(): return lax.all_to_all(x, axis, split_axis=0, concat_axis=0, tiled=True)]
    psum x2 -> x0, blocking collectives: 63.1 us -> none  [the longest x1 33.4 us: shards(): lax.psum((jnp.sum(gained, axis=1), jnp.sum(gained * centered, axis=1)), '...]
    pallas_call x0 -> x9, Pallas kernels: none -> 46.9 us  [the longest x1 12.3 us: shards(): call(lambda *refs: slots_kernel(*refs, blocks=blocks, group=group, most=M...]
    scatter x4 -> x0, local copies, waits for them, and re-layouts: 36.5 us -> none  [the longest x1 12.2 us: shards(): jnp.zeros((slot_total, width_dev), jnp.bfloat16).at[slot_ids]]
    all_to_all x3, blocking collectives: 58.6 us -> 86.6 us  [exchange(): return lax.all_to_all(x, axis, split_axis=0, concat_axis=0, tiled=True)]
    all_to_all x4, starting transfers between devices: 25.9 us -> 36.8 us  [exchange(): return lax.all_to_all(x, axis, split_axis=0, concat_axis=0, tiled=True)]
  transfers between devices with their start and end apart: 6 -> 4, of which waited for: 4 -> 4; matrix products, arithmetic and copies ran while one was open for 40% -> 0% of each run, Pallas kernels for 0% -> 6%
where the time goes in v1:
time: 276 us
  waiting for transfers between devices  103 us (37%)
  blocking collectives  86.6 us (31%)
  Pallas kernels  46.9 us (17%)
  starting transfers between devices  36.8 us (13%)
    all_to_all x4, waiting for transfers between devices, exchange(): return lax.all_to_all(x, axis, split_axis=0, concat_axis=0, tiled=True)  103 us
    all_to_all x3, blocking collectives, exchange(): return lax.all_to_all(x, axis, split_axis=0, concat_axis=0, tiled=True)  86.6 us
    all_to_all x4, starting transfers between devices, exchange(): return lax.all_to_all(x, axis, split_axis=0, concat_axis=0, tiled=True)  36.8 us
    pallas_call x1, Pallas kernels, shards(): call(lambda *refs: slots_kernel(*refs, blocks=blocks, group=group, most=M...  12.3 us
    pallas_call x1, Pallas kernels, shards(): call(sums_kernel, [((8, rows), F32)], [VM] * 3, name='sums')  6.23 us
    pallas_call x1, Pallas kernels, shards(): call(total_kernel, [((8, rows), F32), ((1, rows), F32), ((vocs * pieces,...  5.64 us
  transfers between devices with their start and end apart: 4, of which 4 were waited for; matrix products, arithmetic and copies ran while one was open for 0% of the time, Pallas kernels for 6%

profile of v1, /device:TPU:1, one launch (start us, length us, event | category | flops | bytes accessed | tf_op | source)
XLA Modules:
  0.0 275.6 jit_solution(10517592499946320069)
XLA Ops:
  0.6 12.3 %slots.1 = (bf16[4096,256]{1,0:T(8,128)(2,1)}, bf16[8,512,256]{2,1,0:T(8,128)(2,1)}, f32[256,128]{1,0:T(8,128)}) custom-call(s32[1]{0:T(128)} %bitcast.refs_0_.where_ref, s32[8,256]{1,0:T(8,128)} %bitcast.31, s32[1,256]{1,0:T(1,128)} %bitcast.35, s32[1,256]{1,0:T(1,128)} %bitcast.36), custom_call_target="tpu_custom_call" | custom-call | tf_op jit(solution)/shard_map/slots/pallas_call | solution.py:354
  13.0 13.7 %all-to-all-start.3 = ((f32[32,8,128]{2,1,0:T(8,128)}), f32[32,8,128]{2,1,0:T(8,128)S(1)}, u32[]{:S(2)}, u32[]{:S(2)}) async-start(f32[32,8,128]{2,1,0:T(8,128)} %bitcast.29), calls=%async_computation.3 | async-start | bytes 262144 | tf_op jit(solution)/shard_map/all_to_all | solution.py:346
  27.3 3.4 %attend.1 = bf16[16,272,128]{2,1,0:T(8,128)(2,1)} custom-call(s32[1]{0:T(128)S(6)} %copy.15.len_ref, bf16[256,128]{1,0:T(8,128)(2,1)} %q_ref.1, bf16[1,256,128]{2,1,0:T(8,128)(2,1)} %k_ref.1, bf16[1,256,128]{2,1,0:T(8,128)(2,1)} %v_ref.1, bf16[128,2048]{1,0:T(8,128)(2,1)} %proj_ref.1, bf16[256,128]{1,0:T(8,128)(2,1)} %dec_ref.3, f32[1,128]{1,0:T(1,128)} %bitcast.32, ...), custom_call_target="tpu_custom_call" | custom-call | tf_op jit(solution)/shard_map/attend/pallas_call | solution.py:348
  30.7 5.1 %all-to-all-done.3 = f32[32,8,128]{2,1,0:T(8,128)S(1)} async-done(((f32[32,8,128]{2,1,0:T(8,128)}), f32[32,8,128]{2,1,0:T(8,128)S(1)}, u32[]{:S(2)}, u32[]{:S(2)}) %all-to-all-start.3) | async-done | bytes 131104 | tf_op jit(solution)/shard_map/all_to_all | solution.py:346
  35.8 0.0 copy-start.3
  35.8 9.2 %all-to-all-start = ((bf16[16,272,128]{2,1,0:T(8,128)(2,1)}), bf16[16,272,128]{2,1,0:T(8,128)(2,1)S(1)}, u32[]{:S(2)}, u32[]{:S(2)}) async-start(bf16[16,272,128]{2,1,0:T(8,128)(2,1)} %attend.1), calls=%async_computation | async-start | bytes 2228224 | tf_op jit(solution)/shard_map/all_to_all | solution.py:346
  45.0 3.1 %pack.1 = bf16[16,128,512]{2,1,0:T(8,128)(2,1)} custom-call(bf16[128,8064]{1,0:T(8,128)(2,1)} %head_ref.1), custom_call_target="tpu_custom_call" | custom-call | tf_op jit(solution)/shard_map/pack/pallas_call | solution.py:352
  48.1 0.0 copy-done.3
  48.1 26.2 %all-to-all-done.part_ref = bf16[16,272,128]{2,1,0:T(8,128)(2,1)S(1)} async-done(((bf16[16,272,128]{2,1,0:T(8,128)(2,1)}), bf16[16,272,128]{2,1,0:T(8,128)(2,1)S(1)}, u32[]{:S(2)}, u32[]{:S(2)}) %all-to-all-start) | async-done | bytes 1114144 | tf_op jit(solution)/shard_map/all_to_all | solution.py:346
  74.3 0.0 copy-start.1
  74.3 3.6 %all-to-all-start.2 = ((bf16[16,128,512]{2,1,0:T(8,128)(2,1)}), bf16[16,128,512]{2,1,0:T(8,128)(2,1)S(1)}, u32[]{:S(2)}, u32[]{:S(2)}) async-start(bf16[16,128,512]{2,1,0:T(8,128)(2,1)} %pack.1), calls=%async_computation.2 | async-start | bytes 4194304 | tf_op jit(solution)/shard_map/all_to_all | solution.py:346
  78.0 0.0 copy-done.1
  78.0 4.0 %residual.1 = (f32[256,128]{1,0:T(8,128)}, bf16[16,16,128]{2,1,0:T(8,128)(2,1)}, bf16[4096,128]{1,0:T(8,128)(2,1)}) custom-call(bf16[16,272,128]{2,1,0:T(8,128)(2,1)} %copy-done.1, bf16[256,128]{1,0:T(8,128)(2,1)} %dec_ref.3, f32[1,128]{1,0:T(1,128)} %bitcast.33, bf16[4096,256]{1,0:T(8,128)(2,1)} %get-tuple-element.13.m_ref.refs_1_), custom_call_target="tpu_custom_call" | custom-call | tf_op jit(solution)/shard_map/residual/pallas_call | solution.py:361
  82.0 44.9 %all-to-all-done.2.refs_1_.refs_3_ = bf16[16,128,512]{2,1,0:T(8,128)(2,1)S(1)} async-done(((bf16[16,128,512]{2,1,0:T(8,128)(2,1)}), bf16[16,128,512]{2,1,0:T(8,128)(2,1)S(1)}, u32[]{:S(2)}, u32[]{:S(2)}) %all-to-all-start.2) | async-done | bytes 2097184 | tf_op jit(solution)/shard_map/all_to_all | solution.py:346
  126.9 0.0 copy-start
  126.9 43.3 %all_to_all.35 = bf16[512,8,128]{2,1,0:T(8,128)(2,1)} all-to-all(bf16[512,8,128]{2,1,0:T(8,128)(2,1)} %bitcast.26), channel_id=1, replica_groups=mesh['src'=16,'vocab'=32] {'src','vocab'}, dimensions={0} | all-to-all | bytes 2097152 | tf_op jit(solution)/shard_map/all_to_all | solution.py:346
  170.2 0.0 copy-done
  170.2 4.7 %score.1 = (f32[256,128]{1,0:T(8,128)}, f32[512,128]{1,0:T(8,128)}) custom-call(bf16[16,256,128]{2,1,0:T(8,128)(2,1)} %bitcast.20, bf16[16,128,512]{2,1,0:T(8,128)(2,1)} %copy-done, bf16[16,16,128]{2,1,0:T(8,128)(2,1)} %get-tuple-element.15.refs_2_, f32[256,128]{1,0:T(8,128)} %bitcast.24), custom_call_target="tpu_custom_call" | custom-call | tf_op jit(solution)/shard_map/score/pallas_call | solution.py:368
  175.0 28.8 %all_to_all.36 = f32[512,1,128]{2,1,0:T(1,128)} all-to-all(f32[512,1,128]{2,1,0:T(1,128)} %bitcast.28), channel_id=1, replica_groups=mesh['src'=16,'vocab'=32] {'src','vocab'}, dimensions={0} | all-to-all | bytes 524288 | tf_op jit(solution)/shard_map/all_to_all | solution.py:346
  203.8 5.6 %total.1 = (f32[8,256]{1,0:T(8,128)}, f32[1,256]{1,0:T(1,128)}, f32[256,128]{1,0:T(8,128)}) custom-call(s32[1]{0:T(128)} %bitcast.refs_0_.where_ref, f32[512,128]{1,0:T(8,128)} %bitcast.22, bf16[8,512,256]{2,1,0:T(8,128)(2,1)} %get-tuple-element.18.mj_ref, bf16[4096,256]{1,0:T(8,128)(2,1)} %get-tuple-element.13.m_ref.refs_1_), custom_call_target="tpu_custom_call" | custom-call | tf_op jit(solution)/shard_map/total/pallas_call | solution.py:376
  209.4 14.5 %all_to_all.37 = f32[32,8,128]{2,1,0:T(8,128)} all-to-all(f32[32,8,128]{2,1,0:T(8,128)} %bitcast.30), channel_id=1, replica_groups=mesh['src'=16,'vocab'=32] {'vocab'}, dimensions={0} | all-to-all | bytes 262144 | tf_op jit(solution)/shard_map/all_to_all | solution.py:346
  223.9 4.1 %delta.1 = bf16[16,256,128]{2,1,0:T(8,128)(2,1)} custom-call(f32[256,128]{1,0:T(8,128)} %get-tuple-element.20.refs_0_, f32[256,128]{1,0:T(8,128)} %bitcast.25, f32[256,128]{1,0:T(8,128)} %bitcast.27, bf16[16,128,512]{2,1,0:T(8,128)(2,1)} %copy-done), custom_call_target="tpu_custom_call" | custom-call | tf_op jit(solution)/shard_map/delta/pallas_call | solution.py:383
  228.0 10.3 %all-to-all-start.6 = ((bf16[512,8,128]{2,1,0:T(8,128)(2,1)}), bf16[512,8,128]{2,1,0:T(8,128)(2,1)S(1)}, u32[]{:S(2)}, u32[]{:S(2)}) async-start(bf16[512,8,128]{2,1,0:T(8,128)(2,1)} %bitcast.19), calls=%async_computation.6 | async-start | bytes 2097152 | tf_op jit(solution)/shard_map/all_to_all | solution.py:346
  238.3 6.2 %sums.1.refs_4_ = f32[8,256]{1,0:T(8,128)} custom-call(f32[512,128]{1,0:T(8,128)} %bitcast.23, bf16[8,512,256]{2,1,0:T(8,128)(2,1)} %get-tuple-element.18.mj_ref, f32[8,256]{1,0:T(8,128)} %get-tuple-element.23.tot_ref), custom_call_target="tpu_custom_call" | custom-call | tf_op jit(solution)/shard_map/sums/pallas_call | solution.py:390
  244.5 26.7 %all-to-all-done.6 = bf16[512,8,128]{2,1,0:T(8,128)(2,1)S(1)} async-done(((bf16[512,8,128]{2,1,0:T(8,128)(2,1)}), bf16[512,8,128]{2,1,0:T(8,128)(2,1)S(1)}, u32[]{:S(2)}, u32[]{:S(2)}) %all-to-all-start.6) | async-done | bytes 1048608 | tf_op jit(solution)/shard_map/all_to_all | solution.py:346
  271.2 0.0 copy-start.2
  271.3 1.0 copy-done.2
  272.2 3.4 %final.1 = f32[256,128]{1,0:T(8,128)} custom-call(bf16[4096,128]{1,0:T(8,128)(2,1)} %bitcast.21, bf16[4096,256]{1,0:T(8,128)(2,1)} %get-tuple-element.13.m_ref.refs_1_, f32[256,128]{1,0:T(8,128)} %get-tuple-element.22.refs_2_, f32[1,128]{1,0:T(1,128)} %bitcast.34, f32[8,256]{1,0:T(8,128)} %sums.1.refs_4_), custom_call_target="tpu_custom_call" | custom-call | tf_op jit(solution)/shard_map/final/pallas_call | solution.py:391
Async XLA Ops:
  13.0 22.9 %all-to-all-start.3 = ((f32[32,8,128]{2,1,0:T(8,128)}), f32[32,8,128]{2,1,0:T(8,128)S(1)}, u32[]{:S(2)}, u32[]{:S(2)}) async-start(f32[32,8,128]{2,1,0:T(8,128)} %bitcast.29), calls=%async_computation.3 | async-start | bytes 262144 | tf_op jit(solution)/shard_map/all_to_all | solution.py:346
  35.8 12.3 %copy-start.3 = (f32[32,8,128]{2,1,0:T(8,128)}, f32[32,8,128]{2,1,0:T(8,128)S(1)}, u32[]{:S(2)}) copy-start(f32[32,8,128]{2,1,0:T(8,128)S(1)} %all-to-all-done.3) | copy-start | bytes 393220
  35.8 38.5 %all-to-all-start = ((bf16[16,272,128]{2,1,0:T(8,128)(2,1)}), bf16[16,272,128]{2,1,0:T(8,128)(2,1)S(1)}, u32[]{:S(2)}, u32[]{:S(2)}) async-start(bf16[16,272,128]{2,1,0:T(8,128)(2,1)} %attend.1), calls=%async_computation | async-start | bytes 2228224 | tf_op jit(solution)/shard_map/all_to_all | solution.py:346
  74.3 3.6 %copy-start.1 = (bf16[16,272,128]{2,1,0:T(8,128)(2,1)}, bf16[16,272,128]{2,1,0:T(8,128)(2,1)S(1)}, u32[]{:S(2)}) copy-start(bf16[16,272,128]{2,1,0:T(8,128)(2,1)S(1)} %all-to-all-done.part_ref) | copy-start | bytes 3342340
  74.3 52.6 %all-to-all-start.2 = ((bf16[16,128,512]{2,1,0:T(8,128)(2,1)}), bf16[16,128,512]{2,1,0:T(8,128)(2,1)S(1)}, u32[]{:S(2)}, u32[]{:S(2)}) async-start(bf16[16,128,512]{2,1,0:T(8,128)(2,1)} %pack.1), calls=%async_computation.2 | async-start | bytes 4194304 | tf_op jit(solution)/shard_map/all_to_all | solution.py:346
  126.9 43.3 %copy-start = (bf16[16,128,512]{2,1,0:T(8,128)(2,1)}, bf16[16,128,512]{2,1,0:T(8,128)(2,1)S(1)}, u32[]{:S(2)}) copy-start(bf16[16,128,512]{2,1,0:T(8,128)(2,1)S(1)} %all-to-all-done.2.refs_1_.refs_3_) | copy-start | bytes 6291460
  228.0 43.3 %all-to-all-start.6 = ((bf16[512,8,128]{2,1,0:T(8,128)(2,1)}), bf16[512,8,128]{2,1,0:T(8,128)(2,1)S(1)}, u32[]{:S(2)}, u32[]{:S(2)}) async-start(bf16[512,8,128]{2,1,0:T(8,128)(2,1)} %bitcast.19), calls=%async_computation.6 | async-start | bytes 2097152 | tf_op jit(solution)/shard_map/all_to_all | solution.py:346
  271.2 1.0 copy-start.2

commit v2 on v1

v2 whole, which is shorter than its diff:
```python
import math

import jax
import jax.numpy as jnp
from jax import lax
from jax.experimental import pallas as pl
from jax.experimental.pallas import tpu as pltpu
from jax.sharding import Mesh
from jax.sharding import PartitionSpec as P


HD = 128
BLK = 128
MOST = 2
EPSILON = 1e-05
MASKED = -1e30
F32 = jnp.float32
BF16 = jnp.bfloat16
I32 = jnp.int32

VM = pl.BlockSpec(memory_space=pltpu.VMEM)
SM = pl.BlockSpec(memory_space=pltpu.SMEM)
CORES = 2
STATS = 8
EXTRA = 16


def call(body, outs, specs, scratch=()):
    return pl.pallas_call(
        body,
        out_shape=tuple(jax.ShapeDtypeStruct(s, d) for s, d in outs),
        in_specs=specs,
        out_specs=tuple(VM for _ in outs),
        scratch_shapes=list(scratch),
    )


def dot(a, b, ca, cb):
    return lax.dot_general(a, b, (((ca,), (cb,)), ((), ())), preferred_element_type=F32)


def thirds(x):
    hi = x.astype(BF16)
    rest = x - hi.astype(F32)
    mid = rest.astype(BF16)
    low = (rest - mid.astype(F32)).astype(BF16)
    return hi, mid, low


def stack_rows(lines, count, width):
    sub = lax.broadcasted_iota(I32, (count, width), 0)
    out = jnp.zeros((count, width), F32)
    for n, line in enumerate(lines):
        out = jnp.where(sub == n, line.astype(F32), out)
    return out


def pack_kernel(where_ref, head_ref, *out_refs):
    chips = len(out_refs)
    _, tokens = out_refs[0].shape
    cols = head_ref.shape[1]
    for o in range(chips):
        to = lax.rem(where_ref[0] + o, chips)
        start = pl.multiple_of(to * tokens, BLK)
        for t in range(tokens // BLK):
            first = start + t * BLK
            there = first < cols
            safe = pl.multiple_of(jnp.minimum(first, cols - BLK), BLK)
            piece = head_ref[:, pl.ds(safe, BLK)]
            out_refs[o][:, t * BLK : (t + 1) * BLK] = jnp.where(there, piece, jnp.zeros_like(piece))


def share_kernel(where_ref, q_ref, k_ref, v_ref, proj_ref, dec_ref, out_ref):
    rows, width = q_ref.shape
    mem = k_ref.shape[1]
    chips = proj_ref.shape[1] // (CORES * width)
    other = 1 - where_ref[1]
    out_ref[0:rows, :] = q_ref[...]
    out_ref[rows : rows + mem, :] = k_ref[0]
    out_ref[rows + mem : rows + 2 * mem, :] = v_ref[0]
    base = rows + 2 * mem
    for y in range(chips):
        cols = pl.ds(pl.multiple_of((y * CORES + other) * width, width), width)
        out_ref[base + y * width : base + (y + 1) * width, :] = proj_ref[:, cols]
    base = base + chips * width
    sums = dot(jnp.ones((8, proj_ref.shape[1]), BF16), proj_ref[...], 1, 1)
    dec_sums = dot(jnp.ones((8, width), BF16), dec_ref[...], 1, 1)
    lines = list(thirds(sums[0:1, :]))
    for third in thirds(dec_sums[0:1, :]):
        lines += [third[:, c * 128 : (c + 1) * 128] for c in range(rows // 128)]
    out_ref[base:, :] = stack_rows(lines, EXTRA, width).astype(BF16)


def mask_of(listed, earlier, u, v, j, blocks, group):
    local = u * group + lax.rem(j, group)
    block = jnp.where(local < blocks, v * blocks + local, -1)
    named = block == listed[0:1, :]
    for k in range(1, listed.shape[0]):
        named = jnp.logical_or(named, block == listed[k : k + 1, :])
    named = named.astype(F32)
    rank = dot(named.astype(BF16), earlier, 1, 0)
    return jnp.where(rank == lax.div(j, group).astype(F32), named, 0.0), block


def earlier_of(rows):
    r0 = lax.broadcasted_iota(I32, (rows, rows), 0)
    r1 = lax.broadcasted_iota(I32, (rows, rows), 1)
    return (r0 < r1).astype(F32).astype(BF16)


def code_kernel(where_ref, list_ref, tslot_ref, toff_ref, code_ref, *, blocks, group):
    pieces = group * MOST
    span = code_ref.shape[0]
    listed = list_ref[...]
    tslot = tslot_ref[...]
    rows = listed.shape[1]
    target_block = jnp.zeros((1, rows), I32)
    for k in range(listed.shape[0]):
        target_block = jnp.where(tslot == k, listed[k : k + 1, :], target_block)
    i = lax.broadcasted_iota(I32, (span, 1), 0)
    u = jnp.full((span, 1), where_ref[0], I32)
    m, block = mask_of(listed, earlier_of(rows), u, lax.div(i, pieces), lax.rem(i, pieces), blocks, group)
    hit = jnp.where(block == target_block, toff_ref[...].astype(F32) + 1.0, 0.0)
    code = jnp.sum(m * (hit + 1.0), axis=1, keepdims=True) - 2.0
    code_ref[...] = jnp.broadcast_to(code, code_ref.shape).astype(BF16)


def slots_kernel(list_ref, m_ref, mj_ref, *, blocks, group, vocs):
    pieces = group * MOST
    slots, rows = m_ref.shape
    pairs = slots // pieces
    listed = list_ref[...]
    earlier = earlier_of(rows)
    step = 256
    span = vocs * pieces
    sub = lax.broadcasted_iota(I32, (step, 1), 0)

    def travel(t, carry):
        i = t * step + sub
        u = lax.div(i, span)
        v = lax.div(lax.rem(i, span), pieces)
        m, _ = mask_of(listed, earlier, u, v, lax.rem(i, pieces), blocks, group)
        m_ref[pl.ds(pl.multiple_of(t * step, step), step), :] = m.astype(BF16)
        return carry

    lax.fori_loop(0, slots // step, travel, 0)
    w = lax.broadcasted_iota(I32, (pairs, 1), 0)

    def major(t, carry):
        j = jnp.full((pairs, 1), t, I32)
        m, _ = mask_of(listed, earlier, lax.div(w, vocs), lax.rem(w, vocs), j, blocks, group)
        mj_ref[t] = m.astype(BF16)
        return carry

    lax.fori_loop(0, pieces, major, 0)


def whole_line(lines, first, n):
    cut = [lines[first + i : first + i + 1] for i in range(3 * n)]
    return jnp.concatenate([cut[c] + cut[n + c] + cut[2 * n + c] for c in range(n)], axis=1)


def attend(q, k, v, length):
    scores = dot(q, k, 1, 1) * (1.0 / math.sqrt(HD))
    usable = lax.broadcasted_iota(I32, scores.shape, 1) < length
    scores = jnp.where(usable, scores, MASKED)
    top = jnp.max(scores, axis=1, keepdims=True)
    raw = jnp.where(usable, jnp.exp(scores - top), 0.0)
    totals = jnp.sum(raw, axis=1, keepdims=True)
    return (dot(raw.astype(BF16), v, 1, 0) / totals).astype(BF16)


def attend_kernel(
    where_ref, len_ref, q_ref, k_ref, v_ref, proj_ref, dec_ref, gain_ref, bias_ref, other_ref, out_ref
):
    chips, _, width = out_ref.shape
    rows = q_ref.shape[0]
    mem = k_ref.shape[1]
    core = where_ref[1]
    length = len_ref[0]
    att = attend(q_ref[...], k_ref[0], v_ref[0], length)
    q2, k2, v2 = other_ref[0:rows, :], other_ref[rows : rows + mem, :], other_ref[rows + mem : rows + 2 * mem, :]
    att2 = attend(q2, k2, v2, length)
    base = rows + 2 * mem
    for y in range(chips):
        own = proj_ref[:, pl.ds(pl.multiple_of((y * CORES + core) * width, width), width)]
        out_ref[y, :rows, :] = (
            dot(att, own, 1, 0) + dot(att2, other_ref[base + y * width : base + (y + 1) * width, :], 1, 0)
        ).astype(BF16)
    base = base + chips * width
    sums = dot(jnp.ones((8, proj_ref.shape[1]), BF16), proj_ref[...], 1, 1)
    part = dot(jnp.ones((8, width), BF16), dec_ref[...], 1, 1)
    for third in thirds(sums):
        part = part + dot(third, att, 1, 1)
    other_sums = dot(other_ref[base:, :], att2, 1, 1)
    line = part[0:1, :] + (other_sums[0:1, :] + other_sums[1:2, :] + other_sums[2:3, :])
    line = line + whole_line(other_ref[base:, :].astype(F32), 3, rows // 128)
    lines = []
    for third in thirds(line):
        lines += [third[:, c * 128 : (c + 1) * 128] for c in range(rows // 128)]
    lines += list(thirds(gain_ref[...])) + list(thirds(bias_ref[...]))
    extra = stack_rows(lines, EXTRA, width).astype(BF16)
    for y in range(chips):
        out_ref[y, rows:, :] = extra


def columns(line):
    n = line.shape[1] // 128
    parts = [jnp.transpose(jnp.broadcast_to(line[:, c * 128 : (c + 1) * 128], (8, 128)))[:, 0:1] for c in range(n)]
    return jnp.concatenate(parts, axis=0)


def residual_kernel(part_ref, dec_ref, gain_ref, m_ref, c_ref, extra_ref, out_ref, *, total):
    chips, _, width = part_ref.shape
    rows = dec_ref.shape[0]
    acc = dec_ref[...].astype(F32)
    lines = jnp.zeros((EXTRA, width), F32)
    for y in range(chips):
        acc = acc + part_ref[y, :rows, :].astype(F32)
        lines = lines + part_ref[y, rows:, :].astype(F32)
        extra_ref[y] = part_ref[y, rows:, :]
    line = whole_line(lines, 0, rows // 128)
    c = acc - columns(line) / total
    c_ref[...] = c
    x = (c * gain_ref[...]).astype(BF16)
    out_ref[...] = dot(m_ref[...], x, 1, 0).astype(BF16)


def third_sum(x, first):
    return x[first : first + 1] + x[first + 1 : first + 2] + x[first + 2 : first + 3]


def half_kernel(where_ref, x_ref, extra_ref, *refs, group, lines):
    w_refs, out_ref = refs[:-1], refs[-1]
    chips, slots, width = x_ref.shape
    tokens = group * BLK
    acc = jnp.zeros((slots, tokens), F32)
    sums = jnp.zeros((EXTRA, tokens), F32)
    squares = jnp.zeros((slots, width), F32)
    for o in range(chips):
        y = lax.rem(where_ref[0] + (chips - o), chips)
        x = x_ref[y]
        w = w_refs[o][...]
        acc = acc + dot(x, w, 1, 0)
        small = extra_ref[y]
        plain = x.astype(F32) / third_sum(small.astype(F32), lines)
        squares = squares + plain * plain
        sums = sums + dot(small, w, 1, 0)
    place = lax.rem(lax.broadcasted_iota(I32, (slots, 1), 0), group)
    dots = acc[:, 0:BLK]
    for b in range(1, group):
        dots = jnp.where(place == b, acc[:, b * BLK : (b + 1) * BLK], dots)
    out_ref[0:slots, :] = dots
    ones = jnp.ones((8, width), BF16)
    total = jnp.zeros((8, slots), F32)
    for third in thirds(squares):
        total = total + dot(ones, third, 1, 1)
    base = slots
    n = slots // 128
    for c in range(n):
        out_ref[base + c : base + c + 1, :] = total[0:1, c * 128 : (c + 1) * 128]
    base = base + n
    for first in (lines, lines + 3):
        line = third_sum(sums, first)
        for b in range(group):
            out_ref[base + b : base + b + 1, :] = line[:, b * BLK : (b + 1) * BLK]
        base = base + group
    if base < out_ref.shape[0]:
        out_ref[base:, :] = jnp.zeros((out_ref.shape[0] - base, BLK), F32)


def score_kernel(own_ref, other_ref, code_ref, l_ref, row_ref, stat_ref, *, group, total):
    slots = l_ref.shape[0]
    pieces = MOST * group
    both = own_ref[...] + other_ref[...]
    dots = both[0:slots]
    n = slots // 128
    squares = columns(jnp.concatenate([both[slots + c : slots + c + 1] for c in range(n)], axis=1))
    inv = lax.rsqrt(squares / total + EPSILON)
    place = lax.rem(lax.broadcasted_iota(I32, (slots, 1), 0), group)
    at = slots + n
    gains = jnp.broadcast_to(both[at : at + 1], dots.shape)
    biases = jnp.broadcast_to(both[at + group : at + group + 1], dots.shape)
    for b in range(1, group):
        gains = jnp.where(place == b, both[at + b : at + b + 1], gains)
        biases = jnp.where(place == b, both[at + group + b : at + group + b + 1], biases)
    bare = inv * dots
    logits = bare + biases
    l_ref[...] = logits
    top = jnp.max(logits, axis=1, keepdims=True)
    shifted = jnp.exp(logits - top)
    spread = jnp.sum(shifted, axis=1, keepdims=True)
    lse = top + jnp.log(spread)
    soft = shifted / spread
    lane = lax.broadcasted_iota(I32, logits.shape, 1)
    hit = lane.astype(F32) == code_ref[...].astype(F32)

    def row_sum(v):
        return jnp.sum(v, axis=1, keepdims=True)

    cols = [
        lse,
        row_sum(jnp.where(hit, logits, 0.0)),
        inv,
        row_sum(soft * gains),
        row_sum(soft * bare),
        row_sum(jnp.where(hit, gains, 0.0)),
        row_sum(jnp.where(hit, bare, 0.0)),
    ]
    out = jnp.zeros(logits.shape, F32)
    for n, col in enumerate(cols):
        out = jnp.where(lane == n, col, out)
    stat_ref[...] = out
    sents = slots // pieces
    lane_s = lax.div(lax.broadcasted_iota(I32, (sents, 128), 1), STATS)
    packed = jnp.zeros((sents, 128), F32)
    for j in range(pieces):
        z = stat_ref[pl.ds(j, sents, stride=pieces), :]
        if j:
            z = pltpu.roll(z, j * STATS, 1)
        packed = jnp.where(lane_s == j, z, packed)
    for u in range(row_ref.shape[0] // sents):
        row_ref[u * sents : (u + 1) * sents, :] = packed


def total_kernel(where_ref, e_ref, mj_ref, m_ref, tot_ref, loss_ref, back_ref):
    pieces, pairs, rows = mj_ref.shape
    low = jnp.full((8, rows), MASKED, F32)
    for j in range(pieces):
        lse = jnp.where(mj_ref[j].astype(F32) > 0.0, e_ref[:, j * STATS : j * STATS + 1], MASKED)
        low = jnp.maximum(low, jnp.max(lse.reshape(pairs // 8, 8, rows), axis=0))
    low = jnp.max(low, axis=0, keepdims=True)
    total = jnp.zeros((8, rows), F32)
    picked = jnp.zeros((8, rows), F32)
    for j in range(pieces):
        there = mj_ref[j].astype(F32) > 0.0
        lse = e_ref[:, j * STATS : j * STATS + 1]
        pick = e_ref[:, j * STATS + 1 : j * STATS + 2]
        total = total + jnp.sum(jnp.where(there, jnp.exp(lse - low), 0.0).reshape(pairs // 8, 8, rows), axis=0)
        picked = picked + jnp.sum(jnp.where(there, pick, 0.0).reshape(pairs // 8, 8, rows), axis=0)
    log_total = low + jnp.log(jnp.sum(total, axis=0, keepdims=True))
    tot_ref[...] = jnp.broadcast_to(log_total, tot_ref.shape)
    loss_ref[...] = log_total - jnp.sum(picked, axis=0, keepdims=True)
    slots = back_ref.shape[0]
    own = m_ref[pl.ds(pl.multiple_of(where_ref[0] * slots, slots), slots), :].astype(F32)
    back_ref[...] = jnp.broadcast_to(jnp.sum(own * log_total, axis=1, keepdims=True), back_ref.shape)


def delta_kernel(where_ref, l_ref, code_ref, back_ref, *refs, group):
    w_refs, out_ref = refs[:-1], refs[-1]
    chips = len(w_refs)
    logits = l_ref[...]
    code = code_ref[...].astype(F32)
    lane = lax.broadcasted_iota(I32, logits.shape, 1).astype(F32)
    deltas = jnp.exp(logits - back_ref[...]) - jnp.where(lane == code, 1.0, 0.0)
    deltas = jnp.where(code > -1.5, deltas, 0.0)
    place = lax.rem(lax.broadcasted_iota(I32, logits.shape, 0), group)
    wide = jnp.concatenate([jnp.where(place == b, deltas, 0.0).astype(BF16) for b in range(group)], axis=1)
    for o in range(chips):
        y = lax.rem(where_ref[0] + (chips - o), chips)
        out_ref[y] = dot(wide, w_refs[o][...], 1, 1).astype(BF16)


def sums_kernel(e_ref, mj_ref, tot_ref, out_ref):
    pieces, pairs, rows = mj_ref.shape
    log_total = tot_ref[0:1, :]
    sum_g = jnp.zeros((8, rows), F32)
    sum_gx = jnp.zeros((8, rows), F32)
    inv = jnp.zeros((8, rows), F32)
    for j in range(pieces):
        there = mj_ref[j].astype(F32) > 0.0

        def col(n):
            return e_ref[:, j * STATS + n : j * STATS + n + 1]

        share = jnp.exp(col(0) - log_total)
        g = jnp.where(there, share * col(3) - col(5), 0.0).reshape(pairs // 8, 8, rows)
        gx = jnp.where(there, share * col(4) - col(6), 0.0).reshape(pairs // 8, 8, rows)
        sum_g = sum_g + jnp.sum(g, axis=0)
        sum_gx = sum_gx + jnp.sum(gx, axis=0)
        inv = jnp.maximum(inv, jnp.max(jnp.where(there, col(2), 0.0).reshape(pairs // 8, 8, rows), axis=0))
    sub = lax.broadcasted_iota(I32, (8, rows), 0)
    sum_g = jnp.sum(sum_g, axis=0, keepdims=True)
    sum_gx = jnp.sum(sum_gx, axis=0, keepdims=True)
    inv = jnp.max(inv, axis=0, keepdims=True)
    out_ref[...] = jnp.where(sub == 0, sum_g, jnp.where(sub == 1, sum_gx, inv))


def final_kernel(r_ref, m_ref, c_ref, gain_ref, sums_ref, out_ref, *, total):
    grad = dot(m_ref[...], r_ref[...], 0, 0)
    rows = grad.shape[0]
    cols = jnp.concatenate(
        [jnp.transpose(sums_ref[:, c * 128 : (c + 1) * 128])[:, 0:3] for c in range(rows // 128)], axis=0
    )
    inv = cols[:, 2:3]
    g = grad * gain_ref[...]
    centered = c_ref[...] * inv
    out_ref[...] = inv * (g - cols[:, 0:1] / total - centered * (cols[:, 1:2] / total))


def step(
    queries,
    enc_keys,
    enc_values,
    source_lengths,
    out_proj,
    dec_state,
    norm_gain,
    norm_bias,
    head_weight,
    shortlist,
    target_slot,
    target_offset,
):
    vocs = lax.axis_size("vocab")
    chips = lax.axis_size("chip")
    places = ("chip", "vocab")
    rows, width = dec_state.shape
    mem = enc_keys.shape[1]
    total = out_proj.shape[1]
    blocks = head_weight.shape[1] // BLK
    group = -(-blocks // chips)
    tokens = group * BLK
    pieces = group * MOST
    pairs = chips * vocs
    slots = pairs * pieces
    span = vocs * pieces
    here = jnp.stack([lax.axis_index("chip"), lax.axis_index("core")]).astype(I32)
    gain = norm_gain.reshape(1, width)
    bias = norm_bias.reshape(1, width)
    partner = [(i, CORES - 1 - i) for i in range(CORES)]
    lists = shortlist.T

    def exchange(x, axis):
        return lax.all_to_all(x, axis, split_axis=0, concat_axis=0, tiled=True)

    (code,) = call(
        lambda *refs: code_kernel(*refs, blocks=blocks, group=group), [((span, 128), BF16)], [SM, VM, VM, VM]
    )(here, lists, target_slot.reshape(1, rows), target_offset.reshape(1, rows))
    codes = exchange(code.reshape(vocs, pieces, 128), "vocab").reshape(span, 128)
    (share,) = call(
        share_kernel, [((rows + 2 * mem + chips * width + EXTRA, width), BF16)], [SM] + [VM] * 5
    )(here, queries, enc_keys, enc_values, out_proj, dec_state)
    other = lax.ppermute(share, "core", partner)
    wsend = call(pack_kernel, [((width, tokens), BF16)] * chips, [SM, VM])(here, head_weight)
    win = [wsend[0]]
    for o in range(1, chips):
        win.append(lax.ppermute(wsend[o], "chip", [(i, (i + o) % chips) for i in range(chips)]))
    m, mj = call(
        lambda *refs: slots_kernel(*refs, blocks=blocks, group=group, vocs=vocs),
        [((slots, rows), BF16), ((pieces, pairs, rows), BF16)],
        [VM],
    )(lists)
    (parts,) = call(attend_kernel, [((chips, rows + EXTRA, width), BF16)], [SM, SM] + [VM] * 8)(
        here, source_lengths, queries, enc_keys, enc_values, out_proj, dec_state, gain, bias, other
    )
    parts = exchange(parts, "chip")
    c, extras, outgoing = call(
        lambda *refs: residual_kernel(*refs, total=total),
        [((rows, width), F32), ((chips, EXTRA, width), BF16), ((slots, width), BF16)],
        [VM] * 4,
    )(parts, dec_state, gain, m)
    incoming = exchange(outgoing.reshape(pairs, pieces, width), places)
    lines = 3 * (rows // 128)
    height = -(-(span + span // 128 + 2 * group) // 8) * 8
    (half,) = call(
        lambda *refs: half_kernel(*refs, group=group, lines=lines), [((height, BLK), F32)], [SM] + [VM] * (2 + chips)
    )(here, incoming.reshape(chips, span, width), extras, *win)
    half_in = lax.ppermute(half, "core", partner)
    logits, stats = call(
        lambda *refs: score_kernel(*refs, group=group, total=total),
        [((span, BLK), F32), ((pairs, 128), F32)],
        [VM] * 3,
        scratch=[pltpu.VMEM((span, BLK), F32)],
    )(half, half_in, codes)
    back_stats = exchange(stats.reshape(pairs, 1, 128), places).reshape(pairs, 128)
    totals, loss, back = call(
        total_kernel, [((8, rows), F32), ((1, rows), F32), ((span, 128), F32)], [SM, VM, VM, VM]
    )(here, back_stats, mj, m)
    back_in = exchange(back.reshape(vocs, pieces, 128), "vocab").reshape(span, 128)
    (grads,) = call(
        lambda *refs: delta_kernel(*refs, group=group), [((chips, span, width), BF16)], [SM] + [VM] * (3 + chips)
    )(here, logits, codes, back_in, *win)
    returned = exchange(grads.reshape(pairs, pieces, width), places).reshape(slots, width)
    (sums,) = call(sums_kernel, [((8, rows), F32)], [VM] * 3)(back_stats, mj, totals)
    (grad_state,) = call(
        lambda *refs: final_kernel(*refs, total=total), [((rows, width), F32)], [VM] * 5
    )(returned, m, c, gain, sums)
    return (loss.reshape(rows), grad_state)


def solution(mesh):
    src, vocs = mesh.devices.shape
    finer = Mesh(mesh.devices.reshape(src // CORES, CORES, vocs), ("chip", "core", "vocab"))
    feats = ("chip", "core")
    placed = (
        P("vocab", feats),
        P("vocab", None, feats),
        P("vocab", None, feats),
        P("vocab"),
        P(feats, None),
        P("vocab", feats),
        P(feats),
        P(feats),
        P(feats, "vocab"),
        P("vocab", None),
        P("vocab"),
        P("vocab"),
    )
    return jax.shard_map(
        step,
        mesh=finer,
        in_specs=placed,
        out_specs=(P("vocab"), P("vocab", feats)),
        check_vma=False,
    )
```

time: 276 us -> 260 us (0.942)
  the two profiles are of different devices: /device:TPU:1 before, /device:TPU:2 now
where the time goes in v2:
time: 260 us; the launch traced here: 259 us
  starting transfers between devices  68.6 us (26%)
  waiting for transfers between devices  65.5 us (25%)
  blocking collectives  59.6 us (23%)
  Pallas kernels  58.3 us (22%)
  local copies, waits for them, and re-layouts  4.56 us (2%)
    all_to_all x3, blocking collectives, exchange(): return lax.all_to_all(x, axis, split_axis=0, concat_axis=0, tiled=True)  59.6 us
    ppermute x7, waiting for transfers between devices, step(): lax.ppermute(wsend[o], 'chip', [(i, (i + o) % chips) for i in range(chips)])  37.2 us
    all_to_all x3, starting transfers between devices, exchange(): return lax.all_to_all(x, axis, split_axis=0, concat_axis=0, tiled=True)  33.9 us
    ppermute x7, starting transfers between devices, step(): lax.ppermute(wsend[o], 'chip', [(i, (i + o) % chips) for i in range(chips)])  30.9 us
    all_to_all x3, waiting for transfers between devices, exchange(): return lax.all_to_all(x, axis, split_axis=0, concat_axis=0, tiled=True)  27 us
    pallas_call x1, Pallas kernels, step(): call(lambda *refs: slots_kernel(*refs, blocks=blocks, group=group, vocs=v...  14.4 us
    pallas_call x1, Pallas kernels, step(): call(sums_kernel, [((8, rows), F32)], [VM] * 3)(back_stats, mj, totals)  6.21 us
    pallas_call x1, Pallas kernels, step(): call(total_kernel, [((8, rows), F32), ((1, rows), F32), ((span, 128), F32...  5.61 us
  transfers between devices with their start and end apart: 12, of which 7 were waited for; matrix products, arithmetic and copies ran while one was open for 0% of the time, Pallas kernels for 10%

profile of v2, /device:TPU:2, one launch (start us, length us, event | category | flops | bytes accessed | tf_op | source)
XLA Modules:
  0.0 258.6 jit_solution(12590747685191076812)
XLA Ops:
  1.2 2.2 shard_map.131
  8.1 3.7 %shard_map.132 = bf16[8,272,128]{2,1,0:T(8,128)(2,1)} custom-call(s32[2]{0:T(128)} %pad_add_fusion.where_ref.refs_0_, s32[1]{0:T(128)S(6)} %copy.15.len_ref, bf16[256,128]{1,0:T(8,128)(2,1)} %q_ref.3, bf16[1,256,128]{2,1,0:T(8,128)(2,1)} %k_ref.3, bf16[1,256,128]{2,1,0:T(8,128)(2,1)} %v_ref.3, bf16[128,2048]{1,0:T(8,128)(2,1)} %proj_ref.3, ...), custom_call_target="tpu_custom_call" | custom-call | tf_op jit(solution)/shard_map/pallas_call | solution.py:454
  11.8 7.1 %all-to-all-start = ((bf16[8,272,128]{2,1,0:T(8,128)(2,1)}), bf16[8,272,128]{2,1,0:T(8,128)(2,1)S(1)}, u32[]{:S(2)}, u32[]{:S(2)}) async-start(bf16[8,272,128]{2,1,0:T(8,128)(2,1)} %shard_map.132), calls=%async_computation | async-start | bytes 1114112 | tf_op jit(solution)/shard_map/all_to_all | solution.py:435
  18.9 14.4 %shard_map.133 = (bf16[4096,256]{1,0:T(8,128)(2,1)}, bf16[16,256,256]{2,1,0:T(8,128)(2,1)}) custom-call(s32[8,256]{1,0:T(8,128)} %bitcast.32), custom_call_target="tpu_custom_call" | custom-call | tf_op jit(solution)/shard_map/pallas_call | solution.py:449
  33.3 4.1 %all-to-all-done.refs_0_ = bf16[8,272,128]{2,1,0:T(8,128)(2,1)S(1)} async-done(((bf16[8,272,128]{2,1,0:T(8,128)(2,1)}), bf16[8,272,128]{2,1,0:T(8,128)(2,1)S(1)}, u32[]{:S(2)}, u32[]{:S(2)}) %all-to-all-start) | async-done | bytes 557088 | tf_op jit(solution)/shard_map/all_to_all | solution.py:435
  38.2 3.8 %shard_map.134 = (f32[256,128]{1,0:T(8,128)}, bf16[8,16,128]{2,1,0:T(8,128)(2,1)}, bf16[4096,128]{1,0:T(8,128)(2,1)}) custom-call(bf16[8,272,128]{2,1,0:T(8,128)(2,1)} %copy-done.2, bf16[256,128]{1,0:T(8,128)(2,1)} %refs_1_.1, f32[1,128]{1,0:T(1,128)} %bitcast.35, bf16[4096,256]{1,0:T(8,128)(2,1)} %get-tuple-element.20.refs_3_.m_ref.refs_1_), custom_call_target="tpu_custom_call" | custom-call | tf_op jit(solution)/shard_map/pallas_call | solution.py:458
  42.0 17.5 %all-to-all-start.1 = ((bf16[256,16,128]{2,1,0:T(8,128)(2,1)}), bf16[256,16,128]{2,1,0:T(8,128)(2,1)S(1)}, u32[]{:S(2)}, u32[]{:S(2)}) async-start(bf16[256,16,128]{2,1,0:T(8,128)(2,1)} %bitcast.28), calls=%async_computation.1 | async-start | bytes 2097152 | tf_op jit(solution)/shard_map/all_to_all | solution.py:435
  59.4 3.6 %shard_map.135 = (bf16[128,1024]{1,0:T(8,128)(2,1)}, bf16[128,1024]{1,0:T(8,128)(2,1)}, bf16[128,1024]{1,0:T(8,128)(2,1)}, bf16[128,1024]{1,0:T(8,128)(2,1)}, bf...) custom-call(s32[2]{0:T(128)} %pad_add_fusion.where_ref.refs_0_, ...), custom_call_target="tpu_custom_call" | custom-call | tf_op jit(solution)/shard_map/pallas_call | solution.py:445
  63.0 3.5 %collective-permute-start.1 = (bf16[128,1024]{1,0:T(8,128)(2,1)}, bf16[128,1024]{1,0:T(8,128)(2,1)S(1)}, u32[]{:S(2)}, u32[]{:S(2)}) collective-permute-start(bf16[128,1024]{1,0:T(8,128)(2,1)} %get-tuple-element.24), channel_id=1, source_target_pairs={{0,64},{64,128},{128,192},{192,256},{256,320},{320,384},{384,448},... | collective-permute-start | bytes 786440 | tf_op jit(solution)/shard_map/ppermute | solution.py:448
  66.5 4.7 %collective-permute-start.2 = (bf16[128,1024]{1,0:T(8,128)(2,1)}, bf16[128,1024]{1,0:T(8,128)(2,1)S(1)}, u32[]{:S(2)}, u32[]{:S(2)}) collective-permute-start(bf16[128,1024]{1,0:T(8,128)(2,1)} %get-tuple-element.25), channel_id=1, source_target_pairs={{0,128},{64,192},{128,256},{192,320},{256,384},{320,448},{384,0},{... | collective-permute-start | bytes 786440 | tf_op jit(solution)/shard_map/ppermute | solution.py:448
  71.2 5.2 %collective-permute-start.3 = (bf16[128,1024]{1,0:T(8,128)(2,1)}, bf16[128,1024]{1,0:T(8,128)(2,1)S(1)}, u32[]{:S(2)}, u32[]{:S(2)}) collective-permute-start(bf16[128,1024]{1,0:T(8,128)(2,1)} %get-tuple-element.26), channel_id=1, source_target_pairs={{0,192},{64,256},{128,320},{192,384},{256,448},{320,0},{384,64},{4... | collective-permute-start | bytes 786440 | tf_op jit(solution)/shard_map/ppermute | solution.py:448
  76.5 3.4 %collective-permute-start.4 = (bf16[128,1024]{1,0:T(8,128)(2,1)}, bf16[128,1024]{1,0:T(8,128)(2,1)S(1)}, u32[]{:S(2)}, u32[]{:S(2)}) collective-permute-start(bf16[128,1024]{1,0:T(8,128)(2,1)} %get-tuple-element.27), channel_id=1, source_target_pairs={{0,256},{64,320},{128,384},{192,448},{256,0},{320,64},{384,128},{4... | collective-permute-start | bytes 786440 | tf_op jit(solution)/shard_map/ppermute | solution.py:448
  79.9 5.7 %collective-permute-start.5 = (bf16[128,1024]{1,0:T(8,128)(2,1)}, bf16[128,1024]{1,0:T(8,128)(2,1)S(1)}, u32[]{:S(2)}, u32[]{:S(2)}) collective-permute-start(bf16[128,1024]{1,0:T(8,128)(2,1)} %get-tuple-element.28), channel_id=1, source_target_pairs={{0,320},{64,384},{128,448},{192,0},{256,64},{320,128},{384,192},{4... | collective-permute-start | bytes 786440 | tf_op jit(solution)/shard_map/ppermute | solution.py:448
  85.6 5.9 %collective-permute-done.1.refs_4_.refs_5_ = bf16[128,1024]{1,0:T(8,128)(2,1)S(1)} collective-permute-done((bf16[128,1024]{1,0:T(8,128)(2,1)}, bf16[128,1024]{1,0:T(8,128)(2,1)S(1)}, u32[]{:S(2)}, u32[]{:S(2)}) %collective-permute-start.1) | collective-permute-done | bytes 262176 | tf_op jit(solution)/shard_map/ppermute | solution.py:448
  91.5 4.0 %collective-permute-start.6 = (bf16[128,1024]{1,0:T(8,128)(2,1)}, bf16[128,1024]{1,0:T(8,128)(2,1)S(1)}, u32[]{:S(2)}, u32[]{:S(2)}) collective-permute-start(bf16[128,1024]{1,0:T(8,128)(2,1)} %get-tuple-element.29), channel_id=1, source_target_pairs={{0,384},{64,448},{128,0},{192,64},{256,128},{320,192},{384,256},{4... | collective-permute-start | bytes 786440 | tf_op jit(solution)/shard_map/ppermute | solution.py:448
  95.5 8.3 %collective-permute-done.2.refs_5_.refs_6_ = bf16[128,1024]{1,0:T(8,128)(2,1)S(1)} collective-permute-done((bf16[128,1024]{1,0:T(8,128)(2,1)}, bf16[128,1024]{1,0:T(8,128)(2,1)S(1)}, u32[]{:S(2)}, u32[]{:S(2)}) %collective-permute-start.2) | collective-permute-done | bytes 262176 | tf_op jit(solution)/shard_map/ppermute | solution.py:448
  103.8 4.3 %collective-permute-start.7 = (bf16[128,1024]{1,0:T(8,128)(2,1)}, bf16[128,1024]{1,0:T(8,128)(2,1)S(1)}, u32[]{:S(2)}, u32[]{:S(2)}) collective-permute-start(bf16[128,1024]{1,0:T(8,128)(2,1)} %get-tuple-element.30), channel_id=1, source_target_pairs={{0,448},{64,0},{128,64},{192,128},{256,192},{320,256},{384,320},{4... | collective-permute-start | bytes 786440 | tf_op jit(solution)/shard_map/ppermute | solution.py:448
  108.1 9.5 %collective-permute-done.3.refs_6_.refs_7_ = bf16[128,1024]{1,0:T(8,128)(2,1)S(1)} collective-permute-done((bf16[128,1024]{1,0:T(8,128)(2,1)}, bf16[128,1024]{1,0:T(8,128)(2,1)S(1)}, u32[]{:S(2)}, u32[]{:S(2)}) %collective-permute-start.3) | collective-permute-done | bytes 262176 | tf_op jit(solution)/shard_map/ppermute | solution.py:448
  117.6 13.5 %collective-permute-done.4.refs_7_.refs_8_ = bf16[128,1024]{1,0:T(8,128)(2,1)S(1)} collective-permute-done((bf16[128,1024]{1,0:T(8,128)(2,1)}, bf16[128,1024]{1,0:T(8,128)(2,1)S(1)}, u32[]{:S(2)}, u32[]{:S(2)}) %collective-permute-start.4) | collective-permute-done | bytes 262176 | tf_op jit(solution)/shard_map/ppermute | solution.py:448
  132.5 5.4 %shard_map.136.refs_0_ = f32[536,128]{1,0:T(8,128)} custom-call(s32[2]{0:T(128)} %pad_add_fusion.where_ref.refs_0_, bf16[8,512,128]{2,1,0:T(8,128)(2,1)} %bitcast.20, bf16[8,16,128]{2,1,0:T(8,128)(2,1)} %get-tuple-element.22.refs_2_, bf16[128,1024]{1,0:T(8,128)(2,1)} %get-tuple-element.23.refs_3_.refs_4_, bf16[128,1024]{1,0:T(8,128)(2,1)} %copy-done.3, ...), custom_call_target="tpu_custom_call" | custom-call | tf_op jit(solution)/shard_map/pallas_call | solution.py:466
  137.9 1.9 collective-permute-start.8
  139.8 2.2 shard_map.137
  141.9 19.7 %all_to_all.30 = bf16[32,16,128]{2,1,0:T(8,128)(2,1)} all-to-all(bf16[32,16,128]{2,1,0:T(8,128)(2,1)} %bitcast.29), channel_id=1, replica_groups=mesh['chip'=8,'core'=2,'vocab'=32] {'vocab'}, dimensions={0} | all-to-all | bytes 262144 | tf_op jit(solution)/shard_map/all_to_all | solution.py:435
  162.3 2.7 %shard_map.138 = (f32[512,128]{1,0:T(8,128)}, f32[256,128]{1,0:T(8,128)}) custom-call(f32[536,128]{1,0:T(8,128)} %shard_map.136.refs_0_, f32[536,128]{1,0:T(8,128)} %copy-done.11, bf16[512,128]{1,0:T(8,128)(2,1)} %bitcast.25), custom_call_target="tpu_custom_call" | custom-call | tf_op jit(solution)/shard_map/pallas_call | solution.py:470
  165.1 24.6 %all_to_all.31 = f32[256,1,128]{2,1,0:T(1,128)} all-to-all(f32[256,1,128]{2,1,0:T(1,128)} %bitcast.31), channel_id=1, replica_groups=mesh['chip'=8,'core'=2,'vocab'=32] {'chip','vocab'}, dimensions={0} | all-to-all | bytes 262144 | tf_op jit(solution)/shard_map/all_to_all | solution.py:435
  189.6 5.6 %shard_map.139 = (f32[8,256]{1,0:T(8,128)}, f32[1,256]{1,0:T(1,128)}, f32[512,128]{1,0:T(8,128)}) custom-call(s32[2]{0:T(128)} %pad_add_fusion.where_ref.refs_0_, f32[256,128]{1,0:T(8,128)} %bitcast.23, bf16[16,256,256]{2,1,0:T(8,128)(2,1)} %get-tuple-element.32.mj_ref, bf16[4096,256]{1,0:T(8,128)(2,1)} %get-tuple-element.20.refs_3_.m_ref.refs_1_), custom_call_target="tpu_custom_call" | custom-call | tf_op jit(solution)/shard_map/pallas_call | solution.py:477
  195.2 15.4 %all_to_all.32 = f32[32,16,128]{2,1,0:T(8,128)} all-to-all(f32[32,16,128]{2,1,0:T(8,128)} %bitcast.30), channel_id=1, replica_groups=mesh['chip'=8,'core'=2,'vocab'=32] {'vocab'}, dimensions={0} | all-to-all | bytes 524288 | tf_op jit(solution)/shard_map/all_to_all | solution.py:435
  210.7 5.1 %shard_map.140 = bf16[8,512,128]{2,1,0:T(8,128)(2,1)} custom-call(s32[2]{0:T(128)} %pad_add_fusion.where_ref.refs_0_, f32[512,128]{1,0:T(8,128)} %get-tuple-element.34.refs_1_, bf16[512,128]{1,0:T(8,128)(2,1)} %bitcast.26, f32[512,128]{1,0:T(8,128)} %bitcast.27, bf16[128,1024]{1,0:T(8,128)(2,1)} %get-tuple-element.23.refs_3_.refs_4_, ...), custom_call_target="tpu_custom_call" | custom-call | tf_op jit(solution)/shard_map/pallas_call | solution.py:481
  215.8 9.3 %all-to-all-start.5 = ((bf16[256,16,128]{2,1,0:T(8,128)(2,1)}), bf16[256,16,128]{2,1,0:T(8,128)(2,1)S(1)}, u32[]{:S(2)}, u32[]{:S(2)}) async-start(bf16[256,16,128]{2,1,0:T(8,128)(2,1)} %bitcast.22), calls=%async_computation.5 | async-start | bytes 2097152 | tf_op jit(solution)/shard_map/all_to_all | solution.py:435
  225.1 6.2 %shard_map.141.refs_4_ = f32[8,256]{1,0:T(8,128)} custom-call(f32[256,128]{1,0:T(8,128)} %bitcast.24, bf16[16,256,256]{2,1,0:T(8,128)(2,1)} %get-tuple-element.32.mj_ref, f32[8,256]{1,0:T(8,128)} %get-tuple-element.37.tot_ref), custom_call_target="tpu_custom_call" | custom-call | tf_op jit(solution)/shard_map/pallas_call | solution.py:485
  231.3 22.9 %all-to-all-done.5 = bf16[256,16,128]{2,1,0:T(8,128)(2,1)S(1)} async-done(((bf16[256,16,128]{2,1,0:T(8,128)(2,1)}), bf16[256,16,128]{2,1,0:T(8,128)(2,1)S(1)}, u32[]{:S(2)}, u32[]{:S(2)}) %all-to-all-start.5) | async-done | bytes 1048608 | tf_op jit(solution)/shard_map/all_to_all | solution.py:435
  255.2 3.4 %shard_map.142 = f32[256,128]{1,0:T(8,128)} custom-call(bf16[4096,128]{1,0:T(8,128)(2,1)} %bitcast.21, bf16[4096,256]{1,0:T(8,128)(2,1)} %get-tuple-element.20.refs_3_.m_ref.refs_1_, f32[256,128]{1,0:T(8,128)} %get-tuple-element.36.refs_2_, f32[1,128]{1,0:T(1,128)} %bitcast.36, f32[8,256]{1,0:T(8,128)} %shard_map.141.refs_4_), custom_call_target="tpu_custom_call" | custom-call | tf_op jit(solution)/shard_map/pallas_call | solution.py:486
  (32 shorter events, 8.4 us)
Async XLA Ops:
  3.4 3.9 %collective-permute-start = (bf16[1808,128]{1,0:T(8,128)(2,1)}, bf16[1808,128]{1,0:T(8,128)(2,1)S(1)}, u32[]{:S(2)}, u32[]{:S(2)}) collective-permute-start(bf16[1808,128]{1,0:T(8,128)(2,1)} %shard_map.131), channel_id=1, source_target_pairs={{0,32},{32,0},{1,33},{33,1},{2,34},{34,2},{3,35},{35,3},{4,36},{36... | collective-permute-start | bytes 1388552 | tf_op jit(solution)/shard_map/ppermute | solution.py:444
  7.3 0.8 copy-start.10
  11.8 25.6 %all-to-all-start = ((bf16[8,272,128]{2,1,0:T(8,128)(2,1)}), bf16[8,272,128]{2,1,0:T(8,128)(2,1)S(1)}, u32[]{:S(2)}, u32[]{:S(2)}) async-start(bf16[8,272,128]{2,1,0:T(8,128)(2,1)} %shard_map.132), calls=%async_computation | async-start | bytes 1114112 | tf_op jit(solution)/shard_map/all_to_all | solution.py:435
  37.4 0.8 copy-start.2
  42.0 89.2 %all-to-all-start.1 = ((bf16[256,16,128]{2,1,0:T(8,128)(2,1)}), bf16[256,16,128]{2,1,0:T(8,128)(2,1)S(1)}, u32[]{:S(2)}, u32[]{:S(2)}) async-start(bf16[256,16,128]{2,1,0:T(8,128)(2,1)} %bitcast.28), calls=%async_computation.1 | async-start | bytes 2097152 | tf_op jit(solution)/shard_map/all_to_all | solution.py:435
  63.0 28.5 %collective-permute-start.1 = (bf16[128,1024]{1,0:T(8,128)(2,1)}, bf16[128,1024]{1,0:T(8,128)(2,1)S(1)}, u32[]{:S(2)}, u32[]{:S(2)}) collective-permute-start(bf16[128,1024]{1,0:T(8,128)(2,1)} %get-tuple-element.24), channel_id=1, source_target_pairs={{0,64},{64,128},{128,192},{192,256},{256,320},{320,384},{384,448},... | collective-permute-start | bytes 786440 | tf_op jit(solution)/shard_map/ppermute | solution.py:448
  66.5 37.2 %collective-permute-start.2 = (bf16[128,1024]{1,0:T(8,128)(2,1)}, bf16[128,1024]{1,0:T(8,128)(2,1)S(1)}, u32[]{:S(2)}, u32[]{:S(2)}) collective-permute-start(bf16[128,1024]{1,0:T(8,128)(2,1)} %get-tuple-element.25), channel_id=1, source_target_pairs={{0,128},{64,192},{128,256},{192,320},{256,384},{320,448},{384,0},{... | collective-permute-start | bytes 786440 | tf_op jit(solution)/shard_map/ppermute | solution.py:448
  71.2 46.3 %collective-permute-start.3 = (bf16[128,1024]{1,0:T(8,128)(2,1)}, bf16[128,1024]{1,0:T(8,128)(2,1)S(1)}, u32[]{:S(2)}, u32[]{:S(2)}) collective-permute-start(bf16[128,1024]{1,0:T(8,128)(2,1)} %get-tuple-element.26), channel_id=1, source_target_pairs={{0,192},{64,256},{128,320},{192,384},{256,448},{320,0},{384,64},{4... | collective-permute-start | bytes 786440 | tf_op jit(solution)/shard_map/ppermute | solution.py:448
  76.5 54.6 %collective-permute-start.4 = (bf16[128,1024]{1,0:T(8,128)(2,1)}, bf16[128,1024]{1,0:T(8,128)(2,1)S(1)}, u32[]{:S(2)}, u32[]{:S(2)}) collective-permute-start(bf16[128,1024]{1,0:T(8,128)(2,1)} %get-tuple-element.27), channel_id=1, source_target_pairs={{0,256},{64,320},{128,384},{192,448},{256,0},{320,64},{384,128},{4... | collective-permute-start | bytes 786440 | tf_op jit(solution)/shard_map/ppermute | solution.py:448
  79.9 51.2 %collective-permute-start.5 = (bf16[128,1024]{1,0:T(8,128)(2,1)}, bf16[128,1024]{1,0:T(8,128)(2,1)S(1)}, u32[]{:S(2)}, u32[]{:S(2)}) collective-permute-start(bf16[128,1024]{1,0:T(8,128)(2,1)} %get-tuple-element.28), channel_id=1, source_target_pairs={{0,320},{64,384},{128,448},{192,0},{256,64},{320,128},{384,192},{4... | collective-permute-start | bytes 786440 | tf_op jit(solution)/shard_map/ppermute | solution.py:448
  91.5 39.7 %copy-start.3 = (bf16[128,1024]{1,0:T(8,128)(2,1)}, bf16[128,1024]{1,0:T(8,128)(2,1)S(1)}, u32[]{:S(2)}) copy-start(bf16[128,1024]{1,0:T(8,128)(2,1)S(1)} %collective-permute-done.1.refs_4_.refs_5_) | copy-start | bytes 786436
  91.5 39.6 %collective-permute-start.6 = (bf16[128,1024]{1,0:T(8,128)(2,1)}, bf16[128,1024]{1,0:T(8,128)(2,1)S(1)}, u32[]{:S(2)}, u32[]{:S(2)}) collective-permute-start(bf16[128,1024]{1,0:T(8,128)(2,1)} %get-tuple-element.29), channel_id=1, source_target_pairs={{0,384},{64,448},{128,0},{192,64},{256,128},{320,192},{384,256},{4... | collective-permute-start | bytes 786440 | tf_op jit(solution)/shard_map/ppermute | solution.py:448
  103.8 27.4 %copy-start.4 = (bf16[128,1024]{1,0:T(8,128)(2,1)}, bf16[128,1024]{1,0:T(8,128)(2,1)S(1)}, u32[]{:S(2)}) copy-start(bf16[128,1024]{1,0:T(8,128)(2,1)S(1)} %collective-permute-done.2.refs_5_.refs_6_) | copy-start | bytes 786436
  103.8 27.3 %collective-permute-start.7 = (bf16[128,1024]{1,0:T(8,128)(2,1)}, bf16[128,1024]{1,0:T(8,128)(2,1)S(1)}, u32[]{:S(2)}, u32[]{:S(2)}) collective-permute-start(bf16[128,1024]{1,0:T(8,128)(2,1)} %get-tuple-element.30), channel_id=1, source_target_pairs={{0,448},{64,0},{128,64},{192,128},{256,192},{320,256},{384,320},{4... | collective-permute-start | bytes 786440 | tf_op jit(solution)/shard_map/ppermute | solution.py:448
  117.6 13.6 %copy-start.5 = (bf16[128,1024]{1,0:T(8,128)(2,1)}, bf16[128,1024]{1,0:T(8,128)(2,1)S(1)}, u32[]{:S(2)}) copy-start(bf16[128,1024]{1,0:T(8,128)(2,1)S(1)} %collective-permute-done.3.refs_6_.refs_7_) | copy-start | bytes 786436
  131.1 0.7 copy-start.6
  131.1 0.8 copy-start.7
  131.1 0.9 copy-start.8
  131.1 0.9 copy-start.9
  131.2 1.3 copy-start
  137.9 23.7 %collective-permute-start.8 = (f32[536,128]{1,0:T(8,128)}, f32[536,128]{1,0:T(8,128)S(1)}, u32[]{:S(2)}, u32[]{:S(2)}) collective-permute-start(f32[536,128]{1,0:T(8,128)} %shard_map.136.refs_0_), channel_id=1, source_target_pairs={{0,32},{32,0},{1,33},{33,1},{2,34},{34,2},{3,35},{35,3},{4,36},{36... | collective-permute-start | bytes 823304 | tf_op jit(solution)/shard_map/ppermute | solution.py:469
  161.6 0.7 copy-start.11
  215.8 38.4 %all-to-all-start.5 = ((bf16[256,16,128]{2,1,0:T(8,128)(2,1)}), bf16[256,16,128]{2,1,0:T(8,128)(2,1)S(1)}, u32[]{:S(2)}, u32[]{:S(2)}) async-start(bf16[256,16,128]{2,1,0:T(8,128)(2,1)} %bitcast.22), calls=%async_computation.5 | async-start | bytes 2097152 | tf_op jit(solution)/shard_map/all_to_all | solution.py:435
  254.2 1.0 copy-start.1

commit v3 on v2

--- a/solution.py
+++ b/solution.py
@@ -125,10 +125,9 @@
     code_ref[...] = jnp.broadcast_to(code, code_ref.shape).astype(BF16)
 
 
-def slots_kernel(list_ref, m_ref, mj_ref, *, blocks, group, vocs):
+def slots_kernel(list_ref, m_ref, *, blocks, group, vocs):
     pieces = group * MOST
     slots, rows = m_ref.shape
-    pairs = slots // pieces
     listed = list_ref[...]
     earlier = earlier_of(rows)
     step = 256
@@ -144,6 +143,12 @@
         return carry
 
     lax.fori_loop(0, slots // step, travel, 0)
+
+
+def major_kernel(list_ref, mj_ref, *, blocks, group, vocs):
+    pieces, pairs, rows = mj_ref.shape
+    listed = list_ref[...]
+    earlier = earlier_of(rows)
     w = lax.broadcasted_iota(I32, (pairs, 1), 0)
 
     def major(t, carry):
@@ -446,10 +451,11 @@
     win = [wsend[0]]
     for o in range(1, chips):
         win.append(lax.ppermute(wsend[o], "chip", [(i, (i + o) % chips) for i in range(chips)]))
-    m, mj = call(
-        lambda *refs: slots_kernel(*refs, blocks=blocks, group=group, vocs=vocs),
-        [((slots, rows), BF16), ((pieces, pairs, rows), BF16)],
-        [VM],
+    (m,) = call(
+        lambda *refs: slots_kernel(*refs, blocks=blocks, group=group, vocs=vocs), [((slots, rows), BF16)], [VM]
+    )(lists)
+    (mj,) = call(
+        lambda *refs: major_kernel(*refs, blocks=blocks, group=group, vocs=vocs), [((pieces, pairs, rows), BF16)], [VM]
     )(lists)
     (parts,) = call(attend_kernel, [((chips, rows + EXTRA, width), BF16)], [SM, SM] + [VM] * 8)(
         here, source_lengths, queries, enc_keys, enc_values, out_proj, dec_state, gain, bias, other

time: 260 us -> 262 us (level)
  the two profiles are of different devices: /device:TPU:2 before, /device:TPU:1 now
where the time goes in v3:
time: 262 us; the launch traced here: 257 us
  starting transfers between devices  82 us (31%)
  waiting for transfers between devices  74.1 us (28%)
  Pallas kernels  60.3 us (23%)
  blocking collectives  33 us (13%)
  local copies, waits for them, and re-layouts  5.15 us (2%)
    all_to_all x4, starting transfers between devices, exchange(): return lax.all_to_all(x, axis, split_axis=0, concat_axis=0, tiled=True)  41.6 us
    ppermute x7, waiting for transfers between devices, step(): lax.ppermute(wsend[o], 'chip', [(i, (i + o) % chips) for i in range(chips)])  38.1 us
    all_to_all x4, waiting for transfers between devices, exchange(): return lax.all_to_all(x, axis, split_axis=0, concat_axis=0, tiled=True)  35 us
    all_to_all x2, blocking collectives, exchange(): return lax.all_to_all(x, axis, split_axis=0, concat_axis=0, tiled=True)  33 us
    ppermute x7, starting transfers between devices, step(): lax.ppermute(wsend[o], 'chip', [(i, (i + o) % chips) for i in range(chips)])  26.5 us
    ppermute x1, starting transfers between devices, step(): other = lax.ppermute(share, 'core', partner)  8.73 us
    pallas_call x1, Pallas kernels, step(): call(lambda *refs: slots_kernel(*refs, blocks=blocks, group=group, vocs=v...  8.39 us
    pallas_call x1, Pallas kernels, step(): call(lambda *refs: major_kernel(*refs, blocks=blocks, group=group, vocs=v...  8.15 us
  transfers between devices with their start and end apart: 13, of which 8 were waited for; matrix products, arithmetic and copies ran while one was open for 0% of the time, Pallas kernels for 11%

profile of v3, /device:TPU:1, one launch (start us, length us, event | category | flops | bytes accessed | tf_op | source)
XLA Modules:
  0.0 256.7 jit_solution(1116533919294532058)
XLA Ops:
  3.4 8.7 %collective-permute-start = (bf16[1808,128]{1,0:T(8,128)(2,1)}, bf16[1808,128]{1,0:T(8,128)(2,1)S(1)}, u32[]{:S(2)}, u32[]{:S(2)}) collective-permute-start(bf16[1808,128]{1,0:T(8,128)(2,1)} %shard_map.131), channel_id=1, source_target_pairs={{0,32},{32,0},{1,33},{33,1},{2,34},{34,2},{3,35},{35,3},{4,36},{36... | collective-permute-start | bytes 1388552 | tf_op jit(solution)/shard_map/ppermute | solution.py:449
  14.5 3.7 %shard_map.132 = bf16[8,272,128]{2,1,0:T(8,128)(2,1)} custom-call(s32[2]{0:T(128)} %pad_add_fusion.where_ref.refs_0_, s32[1]{0:T(128)S(6)} %copy.15.len_ref, bf16[256,128]{1,0:T(8,128)(2,1)} %q_ref.3, bf16[1,256,128]{2,1,0:T(8,128)(2,1)} %k_ref.3, bf16[1,256,128]{2,1,0:T(8,128)(2,1)} %v_ref.3, bf16[128,2048]{1,0:T(8,128)(2,1)} %proj_ref.3, ...), custom_call_target="tpu_custom_call" | custom-call | tf_op jit(solution)/shard_map/pallas_call | solution.py:460
  18.2 3.5 %all-to-all-start = ((bf16[8,272,128]{2,1,0:T(8,128)(2,1)}), bf16[8,272,128]{2,1,0:T(8,128)(2,1)S(1)}, u32[]{:S(2)}, u32[]{:S(2)}) async-start(bf16[8,272,128]{2,1,0:T(8,128)(2,1)} %shard_map.132), calls=%async_computation | async-start | bytes 1114112 | tf_op jit(solution)/shard_map/all_to_all | solution.py:440
  21.7 8.4 %shard_map.133.refs_3_.m_ref.refs_1_ = bf16[4096,256]{1,0:T(8,128)(2,1)} custom-call(s32[8,256]{1,0:T(8,128)} %bitcast.32), custom_call_target="tpu_custom_call" | custom-call | tf_op jit(solution)/shard_map/pallas_call | solution.py:454
  30.1 10.2 %all-to-all-done.refs_0_ = bf16[8,272,128]{2,1,0:T(8,128)(2,1)S(1)} async-done(((bf16[8,272,128]{2,1,0:T(8,128)(2,1)}), bf16[8,272,128]{2,1,0:T(8,128)(2,1)S(1)}, u32[]{:S(2)}, u32[]{:S(2)}) %all-to-all-start) | async-done | bytes 557088 | tf_op jit(solution)/shard_map/all_to_all | solution.py:440
  41.2 3.7 %shard_map.134 = (f32[256,128]{1,0:T(8,128)}, bf16[8,16,128]{2,1,0:T(8,128)(2,1)}, bf16[4096,128]{1,0:T(8,128)(2,1)}) custom-call(bf16[8,272,128]{2,1,0:T(8,128)(2,1)} %copy-done.2, bf16[256,128]{1,0:T(8,128)(2,1)} %refs_1_.1, f32[1,128]{1,0:T(1,128)} %bitcast.36, bf16[4096,256]{1,0:T(8,128)(2,1)} %shard_map.133.refs_3_.m_ref.refs_1_), custom_call_target="tpu_custom_call" | custom-call | tf_op jit(solution)/shard_map/pallas_call | solution.py:464
  44.9 15.1 %all-to-all-start.1 = ((bf16[256,16,128]{2,1,0:T(8,128)(2,1)}), bf16[256,16,128]{2,1,0:T(8,128)(2,1)S(1)}, u32[]{:S(2)}, u32[]{:S(2)}) async-start(bf16[256,16,128]{2,1,0:T(8,128)(2,1)} %bitcast.28), calls=%async_computation.1 | async-start | bytes 2097152 | tf_op jit(solution)/shard_map/all_to_all | solution.py:440
  60.0 3.6 %shard_map.135 = (bf16[128,1024]{1,0:T(8,128)(2,1)}, bf16[128,1024]{1,0:T(8,128)(2,1)}, bf16[128,1024]{1,0:T(8,128)(2,1)}, bf16[128,1024]{1,0:T(8,128)(2,1)}, bf...) custom-call(s32[2]{0:T(128)} %pad_add_fusion.where_ref.refs_0_, ...), custom_call_target="tpu_custom_call" | custom-call | tf_op jit(solution)/shard_map/pallas_call | solution.py:450
  65.5 4.2 %collective-permute-start.2 = (bf16[128,1024]{1,0:T(8,128)(2,1)}, bf16[128,1024]{1,0:T(8,128)(2,1)S(1)}, u32[]{:S(2)}, u32[]{:S(2)}) collective-permute-start(bf16[128,1024]{1,0:T(8,128)(2,1)} %get-tuple-element.22), channel_id=1, source_target_pairs={{0,128},{64,192},{128,256},{192,320},{256,384},{320,448},{384,0},{... | collective-permute-start | bytes 786440 | tf_op jit(solution)/shard_map/ppermute | solution.py:453
  69.7 5.0 %collective-permute-start.3 = (bf16[128,1024]{1,0:T(8,128)(2,1)}, bf16[128,1024]{1,0:T(8,128)(2,1)S(1)}, u32[]{:S(2)}, u32[]{:S(2)}) collective-permute-start(bf16[128,1024]{1,0:T(8,128)(2,1)} %get-tuple-element.23), channel_id=1, source_target_pairs={{0,192},{64,256},{128,320},{192,384},{256,448},{320,0},{384,64},{4... | collective-permute-start | bytes 786440 | tf_op jit(solution)/shard_map/ppermute | solution.py:453
  74.7 3.1 %collective-permute-start.4 = (bf16[128,1024]{1,0:T(8,128)(2,1)}, bf16[128,1024]{1,0:T(8,128)(2,1)S(1)}, u32[]{:S(2)}, u32[]{:S(2)}) collective-permute-start(bf16[128,1024]{1,0:T(8,128)(2,1)} %get-tuple-element.24), channel_id=1, source_target_pairs={{0,256},{64,320},{128,384},{192,448},{256,0},{320,64},{384,128},{4... | collective-permute-start | bytes 786440 | tf_op jit(solution)/shard_map/ppermute | solution.py:453
  77.8 5.4 %collective-permute-start.5 = (bf16[128,1024]{1,0:T(8,128)(2,1)}, bf16[128,1024]{1,0:T(8,128)(2,1)S(1)}, u32[]{:S(2)}, u32[]{:S(2)}) collective-permute-start(bf16[128,1024]{1,0:T(8,128)(2,1)} %get-tuple-element.25), channel_id=1, source_target_pairs={{0,320},{64,384},{128,448},{192,0},{256,64},{320,128},{384,192},{4... | collective-permute-start | bytes 786440 | tf_op jit(solution)/shard_map/ppermute | solution.py:453
  83.2 6.0 %collective-permute-done.1.refs_4_.refs_5_ = bf16[128,1024]{1,0:T(8,128)(2,1)S(1)} collective-permute-done((bf16[128,1024]{1,0:T(8,128)(2,1)}, bf16[128,1024]{1,0:T(8,128)(2,1)S(1)}, u32[]{:S(2)}, u32[]{:S(2)}) %collective-permute-start.1) | collective-permute-done | bytes 262176 | tf_op jit(solution)/shard_map/ppermute | solution.py:453
  89.2 3.6 %collective-permute-start.6 = (bf16[128,1024]{1,0:T(8,128)(2,1)}, bf16[128,1024]{1,0:T(8,128)(2,1)S(1)}, u32[]{:S(2)}, u32[]{:S(2)}) collective-permute-start(bf16[128,1024]{1,0:T(8,128)(2,1)} %get-tuple-element.26), channel_id=1, source_target_pairs={{0,384},{64,448},{128,0},{192,64},{256,128},{320,192},{384,256},{4... | collective-permute-start | bytes 786440 | tf_op jit(solution)/shard_map/ppermute | solution.py:453
  92.8 6.9 %collective-permute-done.2.refs_5_.refs_6_ = bf16[128,1024]{1,0:T(8,128)(2,1)S(1)} collective-permute-done((bf16[128,1024]{1,0:T(8,128)(2,1)}, bf16[128,1024]{1,0:T(8,128)(2,1)S(1)}, u32[]{:S(2)}, u32[]{:S(2)}) %collective-permute-start.2) | collective-permute-done | bytes 262176 | tf_op jit(solution)/shard_map/ppermute | solution.py:453
  99.7 3.4 %collective-permute-start.7 = (bf16[128,1024]{1,0:T(8,128)(2,1)}, bf16[128,1024]{1,0:T(8,128)(2,1)S(1)}, u32[]{:S(2)}, u32[]{:S(2)}) collective-permute-start(bf16[128,1024]{1,0:T(8,128)(2,1)} %get-tuple-element.27), channel_id=1, source_target_pairs={{0,448},{64,0},{128,64},{192,128},{256,192},{320,256},{384,320},{4... | collective-permute-start | bytes 786440 | tf_op jit(solution)/shard_map/ppermute | solution.py:453
  103.0 13.7 %collective-permute-done.3.refs_6_.refs_7_ = bf16[128,1024]{1,0:T(8,128)(2,1)S(1)} collective-permute-done((bf16[128,1024]{1,0:T(8,128)(2,1)}, bf16[128,1024]{1,0:T(8,128)(2,1)S(1)}, u32[]{:S(2)}, u32[]{:S(2)}) %collective-permute-start.3) | collective-permute-done | bytes 262176 | tf_op jit(solution)/shard_map/ppermute | solution.py:453
  116.7 11.6 %collective-permute-done.4.refs_7_.refs_8_ = bf16[128,1024]{1,0:T(8,128)(2,1)S(1)} collective-permute-done((bf16[128,1024]{1,0:T(8,128)(2,1)}, bf16[128,1024]{1,0:T(8,128)(2,1)S(1)}, u32[]{:S(2)}, u32[]{:S(2)}) %collective-permute-start.4) | collective-permute-done | bytes 262176 | tf_op jit(solution)/shard_map/ppermute | solution.py:453
  129.6 5.4 %shard_map.136.refs_0_ = f32[536,128]{1,0:T(8,128)} custom-call(s32[2]{0:T(128)} %pad_add_fusion.where_ref.refs_0_, bf16[8,512,128]{2,1,0:T(8,128)(2,1)} %bitcast.20, bf16[8,16,128]{2,1,0:T(8,128)(2,1)} %get-tuple-element.19.refs_2_, bf16[128,1024]{1,0:T(8,128)(2,1)} %get-tuple-element.20.refs_3_.refs_4_, bf16[128,1024]{1,0:T(8,128)(2,1)} %copy-done.4, ...), custom_call_target="tpu_custom_call" | custom-call | tf_op jit(solution)/shard_map/pallas_call | solution.py:472
  135.0 5.1 %collective-permute-start.8 = (f32[536,128]{1,0:T(8,128)}, f32[536,128]{1,0:T(8,128)S(1)}, u32[]{:S(2)}, u32[]{:S(2)}) collective-permute-start(f32[536,128]{1,0:T(8,128)} %shard_map.136.refs_0_), channel_id=1, source_target_pairs={{0,32},{32,0},{1,33},{33,1},{2,34},{34,2},{3,35},{35,3},{4,36},{36... | collective-permute-start | bytes 823304 | tf_op jit(solution)/shard_map/ppermute | solution.py:475
  142.3 18.6 %all_to_all.30 = bf16[32,16,128]{2,1,0:T(8,128)(2,1)} all-to-all(bf16[32,16,128]{2,1,0:T(8,128)(2,1)} %bitcast.29), channel_id=1, replica_groups=mesh['chip'=8,'core'=2,'vocab'=32] {'vocab'}, dimensions={0} | all-to-all | bytes 262144 | tf_op jit(solution)/shard_map/all_to_all | solution.py:440
  161.6 2.7 %shard_map.138 = (f32[512,128]{1,0:T(8,128)}, f32[256,128]{1,0:T(8,128)}) custom-call(f32[536,128]{1,0:T(8,128)} %shard_map.136.refs_0_, f32[536,128]{1,0:T(8,128)} %copy-done.12, bf16[512,128]{1,0:T(8,128)(2,1)} %bitcast.25), custom_call_target="tpu_custom_call" | custom-call | tf_op jit(solution)/shard_map/pallas_call | solution.py:476
  164.4 9.3 %all-to-all-start.3 = ((f32[256,1,128]{2,1,0:T(1,128)}), f32[256,1,128]{2,1,0:T(1,128)S(1)}, u32[]{:S(2)}, u32[]{:S(2)}) async-start(f32[256,1,128]{2,1,0:T(1,128)} %bitcast.31), calls=%async_computation.3 | async-start | bytes 262144 | tf_op jit(solution)/shard_map/all_to_all | solution.py:440
  173.7 8.2 %shard_map.139.mj_ref = bf16[16,256,256]{2,1,0:T(8,128)(2,1)} custom-call(s32[8,256]{1,0:T(8,128)} %bitcast.34), custom_call_target="tpu_custom_call" | custom-call | tf_op jit(solution)/shard_map/pallas_call | solution.py:457
  181.9 4.0 %all-to-all-done.3 = f32[256,1,128]{2,1,0:T(1,128)S(1)} async-done(((f32[256,1,128]{2,1,0:T(1,128)}), f32[256,1,128]{2,1,0:T(1,128)S(1)}, u32[]{:S(2)}, u32[]{:S(2)}) %all-to-all-start.3) | async-done | bytes 131104 | tf_op jit(solution)/shard_map/all_to_all | solution.py:440
  186.5 5.6 %shard_map.140 = (f32[8,256]{1,0:T(8,128)}, f32[1,256]{1,0:T(1,128)}, f32[512,128]{1,0:T(8,128)}) custom-call(s32[2]{0:T(128)} %pad_add_fusion.where_ref.refs_0_, f32[256,128]{1,0:T(8,128)} %bitcast.23, bf16[16,256,256]{2,1,0:T(8,128)(2,1)} %shard_map.139.mj_ref, bf16[4096,256]{1,0:T(8,128)(2,1)} %shard_map.133.refs_3_.m_ref.refs_1_), custom_call_target="tpu_custom_call" | custom-call | tf_op jit(solution)/shard_map/pallas_call | solution.py:483
  192.1 14.4 %all_to_all.31 = f32[32,16,128]{2,1,0:T(8,128)} all-to-all(f32[32,16,128]{2,1,0:T(8,128)} %bitcast.30), channel_id=1, replica_groups=mesh['chip'=8,'core'=2,'vocab'=32] {'vocab'}, dimensions={0} | all-to-all | bytes 524288 | tf_op jit(solution)/shard_map/all_to_all | solution.py:440
  206.4 5.1 %shard_map.141 = bf16[8,512,128]{2,1,0:T(8,128)(2,1)} custom-call(s32[2]{0:T(128)} %pad_add_fusion.where_ref.refs_0_, f32[512,128]{1,0:T(8,128)} %get-tuple-element.30.refs_1_, bf16[512,128]{1,0:T(8,128)(2,1)} %bitcast.26, f32[512,128]{1,0:T(8,128)} %bitcast.27, bf16[128,1024]{1,0:T(8,128)(2,1)} %get-tuple-element.20.refs_3_.refs_4_, ...), custom_call_target="tpu_custom_call" | custom-call | tf_op jit(solution)/shard_map/pallas_call | solution.py:487
  211.5 13.7 %all-to-all-start.5 = ((bf16[256,16,128]{2,1,0:T(8,128)(2,1)}), bf16[256,16,128]{2,1,0:T(8,128)(2,1)S(1)}, u32[]{:S(2)}, u32[]{:S(2)}) async-start(bf16[256,16,128]{2,1,0:T(8,128)(2,1)} %bitcast.22), calls=%async_computation.5 | async-start | bytes 2097152 | tf_op jit(solution)/shard_map/all_to_all | solution.py:440
  225.3 6.2 %shard_map.142.refs_4_ = f32[8,256]{1,0:T(8,128)} custom-call(f32[256,128]{1,0:T(8,128)} %bitcast.24, bf16[16,256,256]{2,1,0:T(8,128)(2,1)} %shard_map.139.mj_ref, f32[8,256]{1,0:T(8,128)} %get-tuple-element.33.tot_ref), custom_call_target="tpu_custom_call" | custom-call | tf_op jit(solution)/shard_map/pallas_call | solution.py:491
  231.5 20.8 %all-to-all-done.5 = bf16[256,16,128]{2,1,0:T(8,128)(2,1)S(1)} async-done(((bf16[256,16,128]{2,1,0:T(8,128)(2,1)}), bf16[256,16,128]{2,1,0:T(8,128)(2,1)S(1)}, u32[]{:S(2)}, u32[]{:S(2)}) %all-to-all-start.5) | async-done | bytes 1048608 | tf_op jit(solution)/shard_map/all_to_all | solution.py:440
  253.3 3.4 %shard_map.143 = f32[256,128]{1,0:T(8,128)} custom-call(bf16[4096,128]{1,0:T(8,128)(2,1)} %bitcast.21, bf16[4096,256]{1,0:T(8,128)(2,1)} %shard_map.133.refs_3_.m_ref.refs_1_, f32[256,128]{1,0:T(8,128)} %get-tuple-element.32.refs_2_, f32[1,128]{1,0:T(1,128)} %bitcast.37, f32[8,256]{1,0:T(8,128)} %shard_map.142.refs_4_), custom_call_target="tpu_custom_call" | custom-call | tf_op jit(solution)/shard_map/pallas_call | solution.py:492
  (36 shorter events, 13.0 us)
Async XLA Ops:
  3.4 10.4 %collective-permute-start = (bf16[1808,128]{1,0:T(8,128)(2,1)}, bf16[1808,128]{1,0:T(8,128)(2,1)S(1)}, u32[]{:S(2)}, u32[]{:S(2)}) collective-permute-start(bf16[1808,128]{1,0:T(8,128)(2,1)} %shard_map.131), channel_id=1, source_target_pairs={{0,32},{32,0},{1,33},{33,1},{2,34},{34,2},{3,35},{35,3},{4,36},{36... | collective-permute-start | bytes 1388552 | tf_op jit(solution)/shard_map/ppermute | solution.py:449
  13.7 0.8 copy-start.11
  18.2 22.2 %all-to-all-start = ((bf16[8,272,128]{2,1,0:T(8,128)(2,1)}), bf16[8,272,128]{2,1,0:T(8,128)(2,1)S(1)}, u32[]{:S(2)}, u32[]{:S(2)}) async-start(bf16[8,272,128]{2,1,0:T(8,128)(2,1)} %shard_map.132), calls=%async_computation | async-start | bytes 1114112 | tf_op jit(solution)/shard_map/all_to_all | solution.py:440
  40.4 0.8 copy-start.2
  44.9 83.4 %all-to-all-start.1 = ((bf16[256,16,128]{2,1,0:T(8,128)(2,1)}), bf16[256,16,128]{2,1,0:T(8,128)(2,1)S(1)}, u32[]{:S(2)}, u32[]{:S(2)}) async-start(bf16[256,16,128]{2,1,0:T(8,128)(2,1)} %bitcast.28), calls=%async_computation.1 | async-start | bytes 2097152 | tf_op jit(solution)/shard_map/all_to_all | solution.py:440
  63.6 25.6 %collective-permute-start.1 = (bf16[128,1024]{1,0:T(8,128)(2,1)}, bf16[128,1024]{1,0:T(8,128)(2,1)S(1)}, u32[]{:S(2)}, u32[]{:S(2)}) collective-permute-start(bf16[128,1024]{1,0:T(8,128)(2,1)} %get-tuple-element.21), channel_id=1, source_target_pairs={{0,64},{64,128},{128,192},{192,256},{256,320},{320,384},{384,448},... | collective-permute-start | bytes 786440 | tf_op jit(solution)/shard_map/ppermute | solution.py:453
  65.5 34.2 %collective-permute-start.2 = (bf16[128,1024]{1,0:T(8,128)(2,1)}, bf16[128,1024]{1,0:T(8,128)(2,1)S(1)}, u32[]{:S(2)}, u32[]{:S(2)}) collective-permute-start(bf16[128,1024]{1,0:T(8,128)(2,1)} %get-tuple-element.22), channel_id=1, source_target_pairs={{0,128},{64,192},{128,256},{192,320},{256,384},{320,448},{384,0},{... | collective-permute-start | bytes 786440 | tf_op jit(solution)/shard_map/ppermute | solution.py:453
  69.7 47.0 %collective-permute-start.3 = (bf16[128,1024]{1,0:T(8,128)(2,1)}, bf16[128,1024]{1,0:T(8,128)(2,1)S(1)}, u32[]{:S(2)}, u32[]{:S(2)}) collective-permute-start(bf16[128,1024]{1,0:T(8,128)(2,1)} %get-tuple-element.23), channel_id=1, source_target_pairs={{0,192},{64,256},{128,320},{192,384},{256,448},{320,0},{384,64},{4... | collective-permute-start | bytes 786440 | tf_op jit(solution)/shard_map/ppermute | solution.py:453
  74.7 53.6 %collective-permute-start.4 = (bf16[128,1024]{1,0:T(8,128)(2,1)}, bf16[128,1024]{1,0:T(8,128)(2,1)S(1)}, u32[]{:S(2)}, u32[]{:S(2)}) collective-permute-start(bf16[128,1024]{1,0:T(8,128)(2,1)} %get-tuple-element.24), channel_id=1, source_target_pairs={{0,256},{64,320},{128,384},{192,448},{256,0},{320,64},{384,128},{4... | collective-permute-start | bytes 786440 | tf_op jit(solution)/shard_map/ppermute | solution.py:453
  77.8 50.5 %collective-permute-start.5 = (bf16[128,1024]{1,0:T(8,128)(2,1)}, bf16[128,1024]{1,0:T(8,128)(2,1)S(1)}, u32[]{:S(2)}, u32[]{:S(2)}) collective-permute-start(bf16[128,1024]{1,0:T(8,128)(2,1)} %get-tuple-element.25), channel_id=1, source_target_pairs={{0,320},{64,384},{128,448},{192,0},{256,64},{320,128},{384,192},{4... | collective-permute-start | bytes 786440 | tf_op jit(solution)/shard_map/ppermute | solution.py:453
  89.2 39.2 %copy-start.4 = (bf16[128,1024]{1,0:T(8,128)(2,1)}, bf16[128,1024]{1,0:T(8,128)(2,1)S(1)}, u32[]{:S(2)}) copy-start(bf16[128,1024]{1,0:T(8,128)(2,1)S(1)} %collective-permute-done.1.refs_4_.refs_5_) | copy-start | bytes 786436
  89.2 39.1 %collective-permute-start.6 = (bf16[128,1024]{1,0:T(8,128)(2,1)}, bf16[128,1024]{1,0:T(8,128)(2,1)S(1)}, u32[]{:S(2)}, u32[]{:S(2)}) collective-permute-start(bf16[128,1024]{1,0:T(8,128)(2,1)} %get-tuple-element.26), channel_id=1, source_target_pairs={{0,384},{64,448},{128,0},{192,64},{256,128},{320,192},{384,256},{4... | collective-permute-start | bytes 786440 | tf_op jit(solution)/shard_map/ppermute | solution.py:453
  99.7 28.7 %copy-start.5 = (bf16[128,1024]{1,0:T(8,128)(2,1)}, bf16[128,1024]{1,0:T(8,128)(2,1)S(1)}, u32[]{:S(2)}) copy-start(bf16[128,1024]{1,0:T(8,128)(2,1)S(1)} %collective-permute-done.2.refs_5_.refs_6_) | copy-start | bytes 786436
  99.7 28.6 %collective-permute-start.7 = (bf16[128,1024]{1,0:T(8,128)(2,1)}, bf16[128,1024]{1,0:T(8,128)(2,1)S(1)}, u32[]{:S(2)}, u32[]{:S(2)}) collective-permute-start(bf16[128,1024]{1,0:T(8,128)(2,1)} %get-tuple-element.27), channel_id=1, source_target_pairs={{0,448},{64,0},{128,64},{192,128},{256,192},{320,256},{384,320},{4... | collective-permute-start | bytes 786440 | tf_op jit(solution)/shard_map/ppermute | solution.py:453
  116.7 11.7 %copy-start.6 = (bf16[128,1024]{1,0:T(8,128)(2,1)}, bf16[128,1024]{1,0:T(8,128)(2,1)S(1)}, u32[]{:S(2)}) copy-start(bf16[128,1024]{1,0:T(8,128)(2,1)S(1)} %collective-permute-done.3.refs_6_.refs_7_) | copy-start | bytes 786436
  128.3 0.7 copy-start.7
  128.3 0.8 copy-start.8
  128.3 0.9 copy-start.9
  128.3 0.9 copy-start.10
  128.3 1.3 copy-start
  135.0 25.9 %collective-permute-start.8 = (f32[536,128]{1,0:T(8,128)}, f32[536,128]{1,0:T(8,128)S(1)}, u32[]{:S(2)}, u32[]{:S(2)}) collective-permute-start(f32[536,128]{1,0:T(8,128)} %shard_map.136.refs_0_), channel_id=1, source_target_pairs={{0,32},{32,0},{1,33},{33,1},{2,34},{34,2},{3,35},{35,3},{4,36},{36... | collective-permute-start | bytes 823304 | tf_op jit(solution)/shard_map/ppermute | solution.py:475
  160.9 0.7 copy-start.12
  164.4 21.4 %all-to-all-start.3 = ((f32[256,1,128]{2,1,0:T(1,128)}), f32[256,1,128]{2,1,0:T(1,128)S(1)}, u32[]{:S(2)}, u32[]{:S(2)}) async-start(f32[256,1,128]{2,1,0:T(1,128)} %bitcast.31), calls=%async_computation.3 | async-start | bytes 262144 | tf_op jit(solution)/shard_map/all_to_all | solution.py:440
  185.8 0.7 copy-start.3
  211.5 40.8 %all-to-all-start.5 = ((bf16[256,16,128]{2,1,0:T(8,128)(2,1)}), bf16[256,16,128]{2,1,0:T(8,128)(2,1)S(1)}, u32[]{:S(2)}, u32[]{:S(2)}) async-start(bf16[256,16,128]{2,1,0:T(8,128)(2,1)} %bitcast.22), calls=%async_computation.5 | async-start | bytes 2097152 | tf_op jit(solution)/shard_map/all_to_all | solution.py:440
  252.3 1.0 copy-start.1

commit v4 on v3

--- a/solution.py
+++ b/solution.py
@@ -108,21 +108,33 @@
     return (r0 < r1).astype(F32).astype(BF16)
 
 
-def code_kernel(where_ref, list_ref, tslot_ref, toff_ref, code_ref, *, blocks, group):
+def code_kernel(where_ref, all_ref, code_ref, named_ref, value_ref, *, blocks, group, picks):
+    sents, _, rows = all_ref.shape
     pieces = group * MOST
-    span = code_ref.shape[0]
-    listed = list_ref[...]
-    tslot = tslot_ref[...]
-    rows = listed.shape[1]
-    target_block = jnp.zeros((1, rows), I32)
-    for k in range(listed.shape[0]):
-        target_block = jnp.where(tslot == k, listed[k : k + 1, :], target_block)
-    i = lax.broadcasted_iota(I32, (span, 1), 0)
-    u = jnp.full((span, 1), where_ref[0], I32)
-    m, block = mask_of(listed, earlier_of(rows), u, lax.div(i, pieces), lax.rem(i, pieces), blocks, group)
-    hit = jnp.where(block == target_block, toff_ref[...].astype(F32) + 1.0, 0.0)
-    code = jnp.sum(m * (hit + 1.0), axis=1, keepdims=True) - 2.0
-    code_ref[...] = jnp.broadcast_to(code, code_ref.shape).astype(BF16)
+    j = lax.broadcasted_iota(I32, (pieces, 1), 0)
+    local = where_ref[0] * group + lax.rem(j, group)
+    block = jnp.where(local < blocks, where_ref[2] * blocks + local, -1)
+
+    def sentence(t, carry):
+        listed = all_ref[t]
+        named = block == listed[0:1, :]
+        tslot = listed[picks : picks + 1, :]
+        target_block = jnp.where(tslot == 0, listed[0:1, :], 0)
+        for k in range(1, picks):
+            named = jnp.logical_or(named, block == listed[k : k + 1, :])
+            target_block = jnp.where(tslot == k, listed[k : k + 1, :], target_block)
+        hit = jnp.where(block == target_block, listed[picks + 1 : picks + 2, :] + 2, 1).astype(F32)
+        at = pl.ds(pl.multiple_of(t * pieces, pieces), pieces)
+        named_ref[at, :] = named.astype(F32)
+        value_ref[at, :] = jnp.where(named, hit, 0.0)
+        return carry
+
+    lax.fori_loop(0, sents, sentence, 0)
+    rank = dot(named_ref[...].astype(BF16), earlier_of(rows), 1, 0)
+    place = lax.rem(lax.broadcasted_iota(I32, (sents * pieces, 1), 0), pieces)
+    want = lax.div(place, group).astype(F32)
+    code = jnp.sum(jnp.where(rank == want, value_ref[...], 0.0), axis=1, keepdims=True) - 2.0
+    code_ref[...] = jnp.broadcast_to(code, code_ref.shape)
 
 
 def slots_kernel(list_ref, m_ref, *, blocks, group, vocs):
@@ -430,7 +442,7 @@
     pairs = chips * vocs
     slots = pairs * pieces
     span = vocs * pieces
-    here = jnp.stack([lax.axis_index("chip"), lax.axis_index("core")]).astype(I32)
+    here = jnp.stack([lax.axis_index("chip"), lax.axis_index("core"), lax.axis_index("vocab")]).astype(I32)
     gain = norm_gain.reshape(1, width)
     bias = norm_bias.reshape(1, width)
     partner = [(i, CORES - 1 - i) for i in range(CORES)]
@@ -439,10 +451,6 @@
     def exchange(x, axis):
         return lax.all_to_all(x, axis, split_axis=0, concat_axis=0, tiled=True)
 
-    (code,) = call(
-        lambda *refs: code_kernel(*refs, blocks=blocks, group=group), [((span, 128), BF16)], [SM, VM, VM, VM]
-    )(here, lists, target_slot.reshape(1, rows), target_offset.reshape(1, rows))
-    codes = exchange(code.reshape(vocs, pieces, 128), "vocab").reshape(span, 128)
     (share,) = call(
         share_kernel, [((rows + 2 * mem + chips * width + EXTRA, width), BF16)], [SM] + [VM] * 5
     )(here, queries, enc_keys, enc_values, out_proj, dec_state)
@@ -467,6 +475,17 @@
         [VM] * 4,
     )(parts, dec_state, gain, m)
     incoming = exchange(outgoing.reshape(pairs, pieces, width), places)
+    picks = lists.shape[0]
+    facts = jnp.concatenate(
+        [lists, target_slot.reshape(1, rows), target_offset.reshape(1, rows), jnp.zeros((16 - picks - 2, rows), I32)], axis=0
+    )
+    facts = lax.all_gather(facts, "vocab", axis=0, tiled=False)
+    (codes,) = call(
+        lambda *refs: code_kernel(*refs, blocks=blocks, group=group, picks=picks),
+        [((span, 128), F32)],
+        [SM, VM],
+        scratch=[pltpu.VMEM((span, rows), F32), pltpu.VMEM((span, rows), F32)],
+    )(here, facts)
     lines = 3 * (rows // 128)
     height = -(-(span + span // 128 + 2 * group) // 8) * 8
     (half,) = call(

time: 262 us -> 292 us (1.11)
  the two profiles are of different devices: /device:TPU:1 before, /device:TPU:2 now
where the time goes in v4:
time: 292 us; the launch traced here: 290 us
  starting transfers between devices  83 us (28%)
  waiting for transfers between devices  70.3 us (24%)
  blocking collectives  68.7 us (24%)
  Pallas kernels  60.9 us (21%)
  local copies, waits for them, and re-layouts  5.24 us (2%)
    all_gather x1, blocking collectives, step(): facts = lax.all_gather(facts, 'vocab', axis=0, tiled=False)  53.3 us
    all_to_all x4, starting transfers between devices, exchange(): return lax.all_to_all(x, axis, split_axis=0, concat_axis=0, tiled=True)  47.6 us
    ppermute x7, waiting for transfers between devices, step(): lax.ppermute(wsend[o], 'chip', [(i, (i + o) % chips) for i in range(chips)])  36.8 us
    all_to_all x4, waiting for transfers between devices, exchange(): return lax.all_to_all(x, axis, split_axis=0, concat_axis=0, tiled=True)  32.2 us
    ppermute x7, starting transfers between devices, step(): lax.ppermute(wsend[o], 'chip', [(i, (i + o) % chips) for i in range(chips)])  31.6 us
    all_to_all x1, blocking collectives, exchange(): return lax.all_to_all(x, axis, split_axis=0, concat_axis=0, tiled=True)  15.4 us
    pallas_call x1, Pallas kernels, step(): call(lambda *refs: slots_kernel(*refs, blocks=blocks, group=group, vocs=v...  8.37 us
    pallas_call x1, Pallas kernels, step(): call(lambda *refs: major_kernel(*refs, blocks=blocks, group=group, vocs=v...  8.15 us
  transfers between devices with their start and end apart: 13, of which 8 were waited for; matrix products, arithmetic and copies ran while one was open for 0% of the time, Pallas kernels for 10%

profile of v4, /device:TPU:2, one launch (start us, length us, event | category | flops | bytes accessed | tf_op | source)
XLA Modules:
  0.0 290.4 jit_solution(9111580504957732814)
XLA Ops:
  8.2 3.7 %shard_map.132 = bf16[8,272,128]{2,1,0:T(8,128)(2,1)} custom-call(s32[3]{0:T(128)} %pad_add_fusion.where_ref.refs_0_, s32[1]{0:T(128)S(6)} %copy.15.len_ref, bf16[256,128]{1,0:T(8,128)(2,1)} %q_ref.3, bf16[1,256,128]{2,1,0:T(8,128)(2,1)} %k_ref.3, bf16[1,256,128]{2,1,0:T(8,128)(2,1)} %v_ref.3, bf16[128,2048]{1,0:T(8,128)(2,1)} %proj_ref.3, ...), custom_call_target="tpu_custom_call" | custom-call | tf_op jit(solution)/shard_map/pallas_call | solution.py:468
  11.8 7.1 %all-to-all-start = ((bf16[8,272,128]{2,1,0:T(8,128)(2,1)}), bf16[8,272,128]{2,1,0:T(8,128)(2,1)S(1)}, u32[]{:S(2)}, u32[]{:S(2)}) async-start(bf16[8,272,128]{2,1,0:T(8,128)(2,1)} %shard_map.132), calls=%async_computation | async-start | bytes 1114112 | tf_op jit(solution)/shard_map/all_to_all | solution.py:452
  18.9 8.4 %shard_map.133.refs_3_.m_ref.refs_1_ = bf16[4096,256]{1,0:T(8,128)(2,1)} custom-call(s32[8,256]{1,0:T(8,128)} %bitcast.30), custom_call_target="tpu_custom_call" | custom-call | tf_op jit(solution)/shard_map/pallas_call | solution.py:462
  27.3 10.1 %all-to-all-done.refs_0_ = bf16[8,272,128]{2,1,0:T(8,128)(2,1)S(1)} async-done(((bf16[8,272,128]{2,1,0:T(8,128)(2,1)}), bf16[8,272,128]{2,1,0:T(8,128)(2,1)S(1)}, u32[]{:S(2)}, u32[]{:S(2)}) %all-to-all-start) | async-done | bytes 557088 | tf_op jit(solution)/shard_map/all_to_all | solution.py:452
  38.2 3.8 %shard_map.134 = (f32[256,128]{1,0:T(8,128)}, bf16[8,16,128]{2,1,0:T(8,128)(2,1)}, bf16[4096,128]{1,0:T(8,128)(2,1)}) custom-call(bf16[8,272,128]{2,1,0:T(8,128)(2,1)} %copy-done.2, bf16[256,128]{1,0:T(8,128)(2,1)} %refs_1_.1, f32[1,128]{1,0:T(1,128)} %bitcast.34, bf16[4096,256]{1,0:T(8,128)(2,1)} %shard_map.133.refs_3_.m_ref.refs_1_), custom_call_target="tpu_custom_call" | custom-call | tf_op jit(solution)/shard_map/pallas_call | solution.py:472
  42.0 16.2 %all-to-all-start.1 = ((bf16[256,16,128]{2,1,0:T(8,128)(2,1)}), bf16[256,16,128]{2,1,0:T(8,128)(2,1)S(1)}, u32[]{:S(2)}, u32[]{:S(2)}) async-start(bf16[256,16,128]{2,1,0:T(8,128)(2,1)} %bitcast.27), calls=%async_computation.1 | async-start | bytes 2097152 | tf_op jit(solution)/shard_map/all_to_all | solution.py:452
  58.2 3.6 %shard_map.135 = (bf16[128,1024]{1,0:T(8,128)(2,1)}, bf16[128,1024]{1,0:T(8,128)(2,1)}, bf16[128,1024]{1,0:T(8,128)(2,1)}, bf16[128,1024]{1,0:T(8,128)(2,1)}, bf...) custom-call(s32[3]{0:T(128)} %pad_add_fusion.where_ref.refs_0_, ...), custom_call_target="tpu_custom_call" | custom-call | tf_op jit(solution)/shard_map/pallas_call | solution.py:458
  61.8 3.7 %collective-permute-start.1 = (bf16[128,1024]{1,0:T(8,128)(2,1)}, bf16[128,1024]{1,0:T(8,128)(2,1)S(1)}, u32[]{:S(2)}, u32[]{:S(2)}) collective-permute-start(bf16[128,1024]{1,0:T(8,128)(2,1)} %get-tuple-element.21), channel_id=1, source_target_pairs={{0,64},{64,128},{128,192},{192,256},{256,320},{320,384},{384,448},... | collective-permute-start | bytes 786440 | tf_op jit(solution)/shard_map/ppermute | solution.py:461
  65.4 4.7 %collective-permute-start.2 = (bf16[128,1024]{1,0:T(8,128)(2,1)}, bf16[128,1024]{1,0:T(8,128)(2,1)S(1)}, u32[]{:S(2)}, u32[]{:S(2)}) collective-permute-start(bf16[128,1024]{1,0:T(8,128)(2,1)} %get-tuple-element.22), channel_id=1, source_target_pairs={{0,128},{64,192},{128,256},{192,320},{256,384},{320,448},{384,0},{... | collective-permute-start | bytes 786440 | tf_op jit(solution)/shard_map/ppermute | solution.py:461
  70.1 5.2 %collective-permute-start.3 = (bf16[128,1024]{1,0:T(8,128)(2,1)}, bf16[128,1024]{1,0:T(8,128)(2,1)S(1)}, u32[]{:S(2)}, u32[]{:S(2)}) collective-permute-start(bf16[128,1024]{1,0:T(8,128)(2,1)} %get-tuple-element.23), channel_id=1, source_target_pairs={{0,192},{64,256},{128,320},{192,384},{256,448},{320,0},{384,64},{4... | collective-permute-start | bytes 786440 | tf_op jit(solution)/shard_map/ppermute | solution.py:461
  75.4 3.4 %collective-permute-start.4 = (bf16[128,1024]{1,0:T(8,128)(2,1)}, bf16[128,1024]{1,0:T(8,128)(2,1)S(1)}, u32[]{:S(2)}, u32[]{:S(2)}) collective-permute-start(bf16[128,1024]{1,0:T(8,128)(2,1)} %get-tuple-element.24), channel_id=1, source_target_pairs={{0,256},{64,320},{128,384},{192,448},{256,0},{320,64},{384,128},{4... | collective-permute-start | bytes 786440 | tf_op jit(solution)/shard_map/ppermute | solution.py:461
  78.8 5.7 %collective-permute-start.5 = (bf16[128,1024]{1,0:T(8,128)(2,1)}, bf16[128,1024]{1,0:T(8,128)(2,1)S(1)}, u32[]{:S(2)}, u32[]{:S(2)}) collective-permute-start(bf16[128,1024]{1,0:T(8,128)(2,1)} %get-tuple-element.25), channel_id=1, source_target_pairs={{0,320},{64,384},{128,448},{192,0},{256,64},{320,128},{384,192},{4... | collective-permute-start | bytes 786440 | tf_op jit(solution)/shard_map/ppermute | solution.py:461
  84.5 5.8 %collective-permute-done.1.refs_4_.refs_5_ = bf16[128,1024]{1,0:T(8,128)(2,1)S(1)} collective-permute-done((bf16[128,1024]{1,0:T(8,128)(2,1)}, bf16[128,1024]{1,0:T(8,128)(2,1)S(1)}, u32[]{:S(2)}, u32[]{:S(2)}) %collective-permute-start.1) | collective-permute-done | bytes 262176 | tf_op jit(solution)/shard_map/ppermute | solution.py:461
  90.3 4.1 %collective-permute-start.6 = (bf16[128,1024]{1,0:T(8,128)(2,1)}, bf16[128,1024]{1,0:T(8,128)(2,1)S(1)}, u32[]{:S(2)}, u32[]{:S(2)}) collective-permute-start(bf16[128,1024]{1,0:T(8,128)(2,1)} %get-tuple-element.26), channel_id=1, source_target_pairs={{0,384},{64,448},{128,0},{192,64},{256,128},{320,192},{384,256},{4... | collective-permute-start | bytes 786440 | tf_op jit(solution)/shard_map/ppermute | solution.py:461
  94.4 8.2 %collective-permute-done.2.refs_5_.refs_6_ = bf16[128,1024]{1,0:T(8,128)(2,1)S(1)} collective-permute-done((bf16[128,1024]{1,0:T(8,128)(2,1)}, bf16[128,1024]{1,0:T(8,128)(2,1)S(1)}, u32[]{:S(2)}, u32[]{:S(2)}) %collective-permute-start.2) | collective-permute-done | bytes 262176 | tf_op jit(solution)/shard_map/ppermute | solution.py:461
  102.6 4.9 %collective-permute-start.7 = (bf16[128,1024]{1,0:T(8,128)(2,1)}, bf16[128,1024]{1,0:T(8,128)(2,1)S(1)}, u32[]{:S(2)}, u32[]{:S(2)}) collective-permute-start(bf16[128,1024]{1,0:T(8,128)(2,1)} %get-tuple-element.27), channel_id=1, source_target_pairs={{0,448},{64,0},{128,64},{192,128},{256,192},{320,256},{384,320},{4... | collective-permute-start | bytes 786440 | tf_op jit(solution)/shard_map/ppermute | solution.py:461
  107.5 9.2 %collective-permute-done.3.refs_6_.refs_7_ = bf16[128,1024]{1,0:T(8,128)(2,1)S(1)} collective-permute-done((bf16[128,1024]{1,0:T(8,128)(2,1)}, bf16[128,1024]{1,0:T(8,128)(2,1)S(1)}, u32[]{:S(2)}, u32[]{:S(2)}) %collective-permute-start.3) | collective-permute-done | bytes 262176 | tf_op jit(solution)/shard_map/ppermute | solution.py:461
  116.8 13.5 %collective-permute-done.4.refs_7_.refs_8_ = bf16[128,1024]{1,0:T(8,128)(2,1)S(1)} collective-permute-done((bf16[128,1024]{1,0:T(8,128)(2,1)}, bf16[128,1024]{1,0:T(8,128)(2,1)S(1)}, u32[]{:S(2)}, u32[]{:S(2)}) %collective-permute-start.4) | collective-permute-done | bytes 262176 | tf_op jit(solution)/shard_map/ppermute | solution.py:461
  131.6 5.4 %shard_map.136.refs_0_ = f32[536,128]{1,0:T(8,128)} custom-call(s32[3]{0:T(128)} %pad_add_fusion.where_ref.refs_0_, bf16[8,512,128]{2,1,0:T(8,128)(2,1)} %bitcast.20, bf16[8,16,128]{2,1,0:T(8,128)(2,1)} %get-tuple-element.19.refs_2_, bf16[128,1024]{1,0:T(8,128)(2,1)} %get-tuple-element.20.refs_3_.refs_4_, bf16[128,1024]{1,0:T(8,128)(2,1)} %copy-done.4, ...), custom_call_target="tpu_custom_call" | custom-call | tf_op jit(solution)/shard_map/pallas_call | solution.py:491
  139.0 53.3 %all-gather = s32[512,256]{1,0:T(8,128)} all-gather(s32[16,256]{1,0:T(8,128)S(1)} %add_add_fusion), channel_id=2, replica_groups=mesh['chip'=8,'core'=2,'vocab'=32] {'vocab'}, dimensions={0}, use_global_device_ids=true | all-gather | bytes 540672 | tf_op jit(solution)/shard_map/all_gather | solution.py:482
  192.3 2.7 shard_map.137.refs_2_
  195.7 2.8 shard_map.138
  198.5 11.4 %all-to-all-start.2 = ((f32[256,1,128]{2,1,0:T(1,128)}), f32[256,1,128]{2,1,0:T(1,128)S(1)}, u32[]{:S(2)}, u32[]{:S(2)}) async-start(f32[256,1,128]{2,1,0:T(1,128)} %bitcast.29), calls=%async_computation.2 | async-start | bytes 262144 | tf_op jit(solution)/shard_map/all_to_all | solution.py:452
  209.9 8.2 %shard_map.139.mj_ref = bf16[16,256,256]{2,1,0:T(8,128)(2,1)} custom-call(s32[8,256]{1,0:T(8,128)} %bitcast.31), custom_call_target="tpu_custom_call" | custom-call | tf_op jit(solution)/shard_map/pallas_call | solution.py:465
  218.0 5.5 %all-to-all-done.2 = f32[256,1,128]{2,1,0:T(1,128)S(1)} async-done(((f32[256,1,128]{2,1,0:T(1,128)}), f32[256,1,128]{2,1,0:T(1,128)S(1)}, u32[]{:S(2)}, u32[]{:S(2)}) %all-to-all-start.2) | async-done | bytes 131104 | tf_op jit(solution)/shard_map/all_to_all | solution.py:452
  224.1 5.6 %shard_map.140 = (f32[8,256]{1,0:T(8,128)}, f32[1,256]{1,0:T(1,128)}, f32[512,128]{1,0:T(8,128)}) custom-call(s32[3]{0:T(128)} %pad_add_fusion.where_ref.refs_0_, f32[256,128]{1,0:T(8,128)} %bitcast.24, bf16[16,256,256]{2,1,0:T(8,128)(2,1)} %shard_map.139.mj_ref, bf16[4096,256]{1,0:T(8,128)(2,1)} %shard_map.133.refs_3_.m_ref.refs_1_), custom_call_target="tpu_custom_call" | custom-call | tf_op jit(solution)/shard_map/pallas_call | solution.py:502
  229.8 15.4 %all_to_all.25 = f32[32,16,128]{2,1,0:T(8,128)} all-to-all(f32[32,16,128]{2,1,0:T(8,128)} %bitcast.28), channel_id=1, replica_groups=mesh['chip'=8,'core'=2,'vocab'=32] {'vocab'}, dimensions={0} | all-to-all | bytes 524288 | tf_op jit(solution)/shard_map/all_to_all | solution.py:452
  245.1 5.1 %shard_map.141 = bf16[8,512,128]{2,1,0:T(8,128)(2,1)} custom-call(s32[3]{0:T(128)} %pad_add_fusion.where_ref.refs_0_, f32[512,128]{1,0:T(8,128)} %get-tuple-element.30.refs_1_, f32[512,128]{1,0:T(8,128)} %shard_map.137.refs_2_, f32[512,128]{1,0:T(8,128)} %bitcast.26, bf16[128,1024]{1,0:T(8,128)(2,1)} %get-tuple-element.20.refs_3_.refs_4_, ...), custom_call_target="tpu_custom_call" | custom-call | tf_op jit(solution)/shard_map/pallas_call | solution.py:506
  250.3 12.9 %all-to-all-start.4 = ((bf16[256,16,128]{2,1,0:T(8,128)(2,1)}), bf16[256,16,128]{2,1,0:T(8,128)(2,1)S(1)}, u32[]{:S(2)}, u32[]{:S(2)}) async-start(bf16[256,16,128]{2,1,0:T(8,128)(2,1)} %bitcast.22), calls=%async_computation.4 | async-start | bytes 2097152 | tf_op jit(solution)/shard_map/all_to_all | solution.py:452
  263.2 6.2 %shard_map.142.refs_4_ = f32[8,256]{1,0:T(8,128)} custom-call(f32[256,128]{1,0:T(8,128)} %bitcast.25, bf16[16,256,256]{2,1,0:T(8,128)(2,1)} %shard_map.139.mj_ref, f32[8,256]{1,0:T(8,128)} %get-tuple-element.33.tot_ref), custom_call_target="tpu_custom_call" | custom-call | tf_op jit(solution)/shard_map/pallas_call | solution.py:510
  269.4 16.6 %all-to-all-done.4 = bf16[256,16,128]{2,1,0:T(8,128)(2,1)S(1)} async-done(((bf16[256,16,128]{2,1,0:T(8,128)(2,1)}), bf16[256,16,128]{2,1,0:T(8,128)(2,1)S(1)}, u32[]{:S(2)}, u32[]{:S(2)}) %all-to-all-start.4) | async-done | bytes 1048608 | tf_op jit(solution)/shard_map/all_to_all | solution.py:452
  287.0 3.4 %shard_map.143 = f32[256,128]{1,0:T(8,128)} custom-call(bf16[4096,128]{1,0:T(8,128)(2,1)} %bitcast.21, bf16[4096,256]{1,0:T(8,128)(2,1)} %shard_map.133.refs_3_.m_ref.refs_1_, f32[256,128]{1,0:T(8,128)} %get-tuple-element.32.refs_2_, f32[1,128]{1,0:T(1,128)} %bitcast.35, f32[8,256]{1,0:T(8,128)} %shard_map.142.refs_4_), custom_call_target="tpu_custom_call" | custom-call | tf_op jit(solution)/shard_map/pallas_call | solution.py:511
  (45 shorter events, 13.3 us)
Async XLA Ops:
  3.5 3.9 %collective-permute-start = (bf16[1808,128]{1,0:T(8,128)(2,1)}, bf16[1808,128]{1,0:T(8,128)(2,1)S(1)}, u32[]{:S(2)}, u32[]{:S(2)}) collective-permute-start(bf16[1808,128]{1,0:T(8,128)(2,1)} %shard_map.131), channel_id=1, source_target_pairs={{0,32},{32,0},{1,33},{33,1},{2,34},{34,2},{3,35},{35,3},{4,36},{36... | collective-permute-start | bytes 1388552 | tf_op jit(solution)/shard_map/ppermute | solution.py:457
  7.4 0.8 copy-start.11
  11.8 25.6 %all-to-all-start = ((bf16[8,272,128]{2,1,0:T(8,128)(2,1)}), bf16[8,272,128]{2,1,0:T(8,128)(2,1)S(1)}, u32[]{:S(2)}, u32[]{:S(2)}) async-start(bf16[8,272,128]{2,1,0:T(8,128)(2,1)} %shard_map.132), calls=%async_computation | async-start | bytes 1114112 | tf_op jit(solution)/shard_map/all_to_all | solution.py:452
  37.4 0.8 copy-start.2
  42.0 88.3 %all-to-all-start.1 = ((bf16[256,16,128]{2,1,0:T(8,128)(2,1)}), bf16[256,16,128]{2,1,0:T(8,128)(2,1)S(1)}, u32[]{:S(2)}, u32[]{:S(2)}) async-start(bf16[256,16,128]{2,1,0:T(8,128)(2,1)} %bitcast.27), calls=%async_computation.1 | async-start | bytes 2097152 | tf_op jit(solution)/shard_map/all_to_all | solution.py:452
  61.8 77.1 %copy-start.13 = (s32[256,8]{0,1:T(8,128)S(1)}, s32[256,8]{0,1:T(8,128)}, u32[]{:S(2)}) copy-start(s32[256,8]{0,1:T(8,128)} %param.21) | copy-start | bytes 24580
  61.8 77.1 %copy-start.14 = (s32[256]{0:T(256)S(1)}, s32[256]{0:T(256)}, u32[]{:S(2)}) copy-start(s32[256]{0:T(256)} %param.23) | copy-start | bytes 3076
  61.8 77.1 %copy-start.15 = (s32[256]{0:T(256)S(1)}, s32[256]{0:T(256)}, u32[]{:S(2)}) copy-start(s32[256]{0:T(256)} %param.22) | copy-start | bytes 3076
  61.8 28.5 %collective-permute-start.1 = (bf16[128,1024]{1,0:T(8,128)(2,1)}, bf16[128,1024]{1,0:T(8,128)(2,1)S(1)}, u32[]{:S(2)}, u32[]{:S(2)}) collective-permute-start(bf16[128,1024]{1,0:T(8,128)(2,1)} %get-tuple-element.21), channel_id=1, source_target_pairs={{0,64},{64,128},{128,192},{192,256},{256,320},{320,384},{384,448},... | collective-permute-start | bytes 786440 | tf_op jit(solution)/shard_map/ppermute | solution.py:461
  65.4 37.1 %collective-permute-start.2 = (bf16[128,1024]{1,0:T(8,128)(2,1)}, bf16[128,1024]{1,0:T(8,128)(2,1)S(1)}, u32[]{:S(2)}, u32[]{:S(2)}) collective-permute-start(bf16[128,1024]{1,0:T(8,128)(2,1)} %get-tuple-element.22), channel_id=1, source_target_pairs={{0,128},{64,192},{128,256},{192,320},{256,384},{320,448},{384,0},{... | collective-permute-start | bytes 786440 | tf_op jit(solution)/shard_map/ppermute | solution.py:461
  70.1 46.6 %collective-permute-start.3 = (bf16[128,1024]{1,0:T(8,128)(2,1)}, bf16[128,1024]{1,0:T(8,128)(2,1)S(1)}, u32[]{:S(2)}, u32[]{:S(2)}) collective-permute-start(bf16[128,1024]{1,0:T(8,128)(2,1)} %get-tuple-element.23), channel_id=1, source_target_pairs={{0,192},{64,256},{128,320},{192,384},{256,448},{320,0},{384,64},{4... | collective-permute-start | bytes 786440 | tf_op jit(solution)/shard_map/ppermute | solution.py:461
  75.4 54.9 %collective-permute-start.4 = (bf16[128,1024]{1,0:T(8,128)(2,1)}, bf16[128,1024]{1,0:T(8,128)(2,1)S(1)}, u32[]{:S(2)}, u32[]{:S(2)}) collective-permute-start(bf16[128,1024]{1,0:T(8,128)(2,1)} %get-tuple-element.24), channel_id=1, source_target_pairs={{0,256},{64,320},{128,384},{192,448},{256,0},{320,64},{384,128},{4... | collective-permute-start | bytes 786440 | tf_op jit(solution)/shard_map/ppermute | solution.py:461
  78.8 51.5 %collective-permute-start.5 = (bf16[128,1024]{1,0:T(8,128)(2,1)}, bf16[128,1024]{1,0:T(8,128)(2,1)S(1)}, u32[]{:S(2)}, u32[]{:S(2)}) collective-permute-start(bf16[128,1024]{1,0:T(8,128)(2,1)} %get-tuple-element.25), channel_id=1, source_target_pairs={{0,320},{64,384},{128,448},{192,0},{256,64},{320,128},{384,192},{4... | collective-permute-start | bytes 786440 | tf_op jit(solution)/shard_map/ppermute | solution.py:461
  90.3 40.1 %copy-start.4 = (bf16[128,1024]{1,0:T(8,128)(2,1)}, bf16[128,1024]{1,0:T(8,128)(2,1)S(1)}, u32[]{:S(2)}) copy-start(bf16[128,1024]{1,0:T(8,128)(2,1)S(1)} %collective-permute-done.1.refs_4_.refs_5_) | copy-start | bytes 786436
  90.3 40.0 %collective-permute-start.6 = (bf16[128,1024]{1,0:T(8,128)(2,1)}, bf16[128,1024]{1,0:T(8,128)(2,1)S(1)}, u32[]{:S(2)}, u32[]{:S(2)}) collective-permute-start(bf16[128,1024]{1,0:T(8,128)(2,1)} %get-tuple-element.26), channel_id=1, source_target_pairs={{0,384},{64,448},{128,0},{192,64},{256,128},{320,192},{384,256},{4... | collective-permute-start | bytes 786440 | tf_op jit(solution)/shard_map/ppermute | solution.py:461
  102.6 27.8 %copy-start.5 = (bf16[128,1024]{1,0:T(8,128)(2,1)}, bf16[128,1024]{1,0:T(8,128)(2,1)S(1)}, u32[]{:S(2)}) copy-start(bf16[128,1024]{1,0:T(8,128)(2,1)S(1)} %collective-permute-done.2.refs_5_.refs_6_) | copy-start | bytes 786436
  102.6 27.8 %collective-permute-start.7 = (bf16[128,1024]{1,0:T(8,128)(2,1)}, bf16[128,1024]{1,0:T(8,128)(2,1)S(1)}, u32[]{:S(2)}, u32[]{:S(2)}) collective-permute-start(bf16[128,1024]{1,0:T(8,128)(2,1)} %get-tuple-element.27), channel_id=1, source_target_pairs={{0,448},{64,0},{128,64},{192,128},{256,192},{320,256},{384,320},{4... | collective-permute-start | bytes 786440 | tf_op jit(solution)/shard_map/ppermute | solution.py:461
  116.8 13.6 %copy-start.6 = (bf16[128,1024]{1,0:T(8,128)(2,1)}, bf16[128,1024]{1,0:T(8,128)(2,1)S(1)}, u32[]{:S(2)}) copy-start(bf16[128,1024]{1,0:T(8,128)(2,1)S(1)} %collective-permute-done.3.refs_6_.refs_7_) | copy-start | bytes 786436
  130.3 0.7 copy-start.7
  130.3 0.8 copy-start.8
  130.3 0.9 copy-start.9
  130.3 0.9 copy-start.10
  130.3 1.2 copy-start
  137.0 58.0 %collective-permute-start.8 = (f32[536,128]{1,0:T(8,128)}, f32[536,128]{1,0:T(8,128)S(1)}, u32[]{:S(2)}, u32[]{:S(2)}) collective-permute-start(f32[536,128]{1,0:T(8,128)} %shard_map.136.refs_0_), channel_id=1, source_target_pairs={{0,32},{32,0},{1,33},{33,1},{2,34},{34,2},{3,35},{35,3},{4,36},{36... | collective-permute-start | bytes 823304 | tf_op jit(solution)/shard_map/ppermute | solution.py:494
  195.0 0.7 copy-start.12
  198.5 25.0 %all-to-all-start.2 = ((f32[256,1,128]{2,1,0:T(1,128)}), f32[256,1,128]{2,1,0:T(1,128)S(1)}, u32[]{:S(2)}, u32[]{:S(2)}) async-start(f32[256,1,128]{2,1,0:T(1,128)} %bitcast.29), calls=%async_computation.2 | async-start | bytes 262144 | tf_op jit(solution)/shard_map/all_to_all | solution.py:452
  223.5 0.7 copy-start.3
  250.3 35.7 %all-to-all-start.4 = ((bf16[256,16,128]{2,1,0:T(8,128)(2,1)}), bf16[256,16,128]{2,1,0:T(8,128)(2,1)S(1)}, u32[]{:S(2)}, u32[]{:S(2)}) async-start(bf16[256,16,128]{2,1,0:T(8,128)(2,1)} %bitcast.22), calls=%async_computation.4 | async-start | bytes 2097152 | tf_op jit(solution)/shard_map/all_to_all | solution.py:452
  286.0 1.0 copy-start.1

commit v5 on v3

--- a/solution.py
+++ b/solution.py
@@ -23,6 +23,10 @@
 CORES = 2
 STATS = 8
 EXTRA = 16
+
+
+def near(x):
+    return pltpu.with_memory_space_constraint(x, pltpu.VMEM)
 
 
 def call(body, outs, specs, scratch=()):
@@ -125,39 +129,56 @@
     code_ref[...] = jnp.broadcast_to(code, code_ref.shape).astype(BF16)
 
 
+def block_of(u, v, at, blocks, group):
+    local = u * group + at
+    return jnp.where(local < blocks, v * blocks + local, -1)
+
+
+def named_ranks(listed, earlier, block):
+    named = block == listed[0:1, :]
+    for k in range(1, listed.shape[0]):
+        named = jnp.logical_or(named, block == listed[k : k + 1, :])
+    named = named.astype(F32)
+    rank = dot(named.astype(BF16), earlier, 1, 0)
+    return jnp.where(named > 0.0, rank, -1.0)
+
+
 def slots_kernel(list_ref, m_ref, *, blocks, group, vocs):
-    pieces = group * MOST
     slots, rows = m_ref.shape
     listed = list_ref[...]
     earlier = earlier_of(rows)
     step = 256
-    span = vocs * pieces
+    span = vocs * group
     sub = lax.broadcasted_iota(I32, (step, 1), 0)
 
     def travel(t, carry):
         i = t * step + sub
-        u = lax.div(i, span)
-        v = lax.div(lax.rem(i, span), pieces)
-        m, _ = mask_of(listed, earlier, u, v, lax.rem(i, pieces), blocks, group)
-        m_ref[pl.ds(pl.multiple_of(t * step, step), step), :] = m.astype(BF16)
+        v = lax.div(lax.rem(i, span), group)
+        block = block_of(lax.div(i, span), v, lax.rem(i, group), blocks, group)
+        rank = named_ranks(listed, earlier, block).reshape(step // group, group, rows)
+        both = jnp.concatenate([(rank == n).astype(F32) for n in range(MOST)], axis=1)
+        size = MOST * step
+        m_ref[pl.ds(pl.multiple_of(t * size, size), size), :] = both.reshape(size, rows).astype(BF16)
         return carry
 
-    lax.fori_loop(0, slots // step, travel, 0)
+    lax.fori_loop(0, slots // (MOST * step), travel, 0)
 
 
 def major_kernel(list_ref, mj_ref, *, blocks, group, vocs):
-    pieces, pairs, rows = mj_ref.shape
+    _, pairs, rows = mj_ref.shape
     listed = list_ref[...]
     earlier = earlier_of(rows)
     w = lax.broadcasted_iota(I32, (pairs, 1), 0)
 
     def major(t, carry):
-        j = jnp.full((pairs, 1), t, I32)
-        m, _ = mask_of(listed, earlier, lax.div(w, vocs), lax.rem(w, vocs), j, blocks, group)
-        mj_ref[t] = m.astype(BF16)
+        at = jnp.full((pairs, 1), t, I32)
+        block = block_of(lax.div(w, vocs), lax.rem(w, vocs), at, blocks, group)
+        rank = named_ranks(listed, earlier, block)
+        for n in range(MOST):
+            mj_ref[n * group + t] = (rank == n).astype(F32).astype(BF16)
         return carry
 
-    lax.fori_loop(0, pieces, major, 0)
+    lax.fori_loop(0, group, major, 0)
 
 
 def whole_line(lines, first, n):
@@ -430,7 +451,7 @@
     pairs = chips * vocs
     slots = pairs * pieces
     span = vocs * pieces
-    here = jnp.stack([lax.axis_index("chip"), lax.axis_index("core")]).astype(I32)
+    here = jnp.stack([lax.axis_index("chip"), lax.axis_index("core"), lax.axis_index("vocab")]).astype(I32)
     gain = norm_gain.reshape(1, width)
     bias = norm_bias.reshape(1, width)
     partner = [(i, CORES - 1 - i) for i in range(CORES)]
@@ -439,10 +460,6 @@
     def exchange(x, axis):
         return lax.all_to_all(x, axis, split_axis=0, concat_axis=0, tiled=True)
 
-    (code,) = call(
-        lambda *refs: code_kernel(*refs, blocks=blocks, group=group), [((span, 128), BF16)], [SM, VM, VM, VM]
-    )(here, lists, target_slot.reshape(1, rows), target_offset.reshape(1, rows))
-    codes = exchange(code.reshape(vocs, pieces, 128), "vocab").reshape(span, 128)
     (share,) = call(
         share_kernel, [((rows + 2 * mem + chips * width + EXTRA, width), BF16)], [SM] + [VM] * 5
     )(here, queries, enc_keys, enc_values, out_proj, dec_state)
@@ -458,40 +475,44 @@
         lambda *refs: major_kernel(*refs, blocks=blocks, group=group, vocs=vocs), [((pieces, pairs, rows), BF16)], [VM]
     )(lists)
     (parts,) = call(attend_kernel, [((chips, rows + EXTRA, width), BF16)], [SM, SM] + [VM] * 8)(
-        here, source_lengths, queries, enc_keys, enc_values, out_proj, dec_state, gain, bias, other
+        here, source_lengths, queries, enc_keys, enc_values, out_proj, dec_state, gain, bias, near(other)
     )
     parts = exchange(parts, "chip")
     c, extras, outgoing = call(
         lambda *refs: residual_kernel(*refs, total=total),
         [((rows, width), F32), ((chips, EXTRA, width), BF16), ((slots, width), BF16)],
         [VM] * 4,
-    )(parts, dec_state, gain, m)
+    )(near(parts), dec_state, gain, m)
     incoming = exchange(outgoing.reshape(pairs, pieces, width), places)
+    (code,) = call(
+        lambda *refs: code_kernel(*refs, blocks=blocks, group=group), [((span, 128), BF16)], [SM, VM, VM, VM]
+    )(here, lists, target_slot.reshape(1, rows), target_offset.reshape(1, rows))
+    codes = exchange(code.reshape(vocs, pieces, 128), "vocab").reshape(span, 128)
     lines = 3 * (rows // 128)
     height = -(-(span + span // 128 + 2 * group) // 8) * 8
     (half,) = call(
         lambda *refs: half_kernel(*refs, group=group, lines=lines), [((height, BLK), F32)], [SM] + [VM] * (2 + chips)
-    )(here, incoming.reshape(chips, span, width), extras, *win)
+    )(here, near(incoming.reshape(chips, span, width)), extras, *win)
     half_in = lax.ppermute(half, "core", partner)
     logits, stats = call(
         lambda *refs: score_kernel(*refs, group=group, total=total),
         [((span, BLK), F32), ((pairs, 128), F32)],
         [VM] * 3,
         scratch=[pltpu.VMEM((span, BLK), F32)],
-    )(half, half_in, codes)
+    )(half, near(half_in), codes)
     back_stats = exchange(stats.reshape(pairs, 1, 128), places).reshape(pairs, 128)
     totals, loss, back = call(
         total_kernel, [((8, rows), F32), ((1, rows), F32), ((span, 128), F32)], [SM, VM, VM, VM]
-    )(here, back_stats, mj, m)
+    )(here, near(back_stats), mj, m)
     back_in = exchange(back.reshape(vocs, pieces, 128), "vocab").reshape(span, 128)
     (grads,) = call(
         lambda *refs: delta_kernel(*refs, group=group), [((chips, span, width), BF16)], [SM] + [VM] * (3 + chips)
-    )(here, logits, codes, back_in, *win)
+    )(here, logits, codes, near(back_in), *win)
     returned = exchange(grads.reshape(pairs, pieces, width), places).reshape(slots, width)
     (sums,) = call(sums_kernel, [((8, rows), F32)], [VM] * 3)(back_stats, mj, totals)
     (grad_state,) = call(
         lambda *refs: final_kernel(*refs, total=total), [((rows, width), F32)], [VM] * 5
-    )(returned, m, c, gain, sums)
+    )(near(returned), m, c, gain, sums)
     return (loss.reshape(rows), grad_state)
 
 

time: 262 us -> 253 us (0.966)
  Pallas kernels: 60.3 us -> 53.1 us
  waiting for transfers between devices: 74.1 us -> 80.4 us
  local copies, waits for them, and re-layouts: 5.15 us -> 0.9 us
    all_to_all x4, waiting for transfers between devices: 35 us -> 41.3 us  [exchange(): return lax.all_to_all(x, axis, split_axis=0, concat_axis=0, tiled=True)]
    unnamed x26 -> x16, local copies, waits for them, and re-layouts: 5.15 us -> 0.9 us
    pallas_call x1, Pallas kernels: 8.39 us -> 5.21 us  [step(): call(lambda *refs: slots_kernel(*refs, blocks=blocks, group=group, vocs=v...]
    pallas_call x1, Pallas kernels: 8.15 us -> 5.09 us  [step(): call(lambda *refs: major_kernel(*refs, blocks=blocks, group=group, vocs=v...]
  transfers between devices with their start and end apart: 13 -> 13, of which waited for: 8 -> 8; matrix products, arithmetic and copies ran while one was open for 0% -> 0% of each run, Pallas kernels for 11% -> 9%
where the time goes in v5:
time: 253 us; the launch traced here: 248 us
  waiting for transfers between devices  80.4 us (32%)
  starting transfers between devices  79.6 us (31%)
  Pallas kernels  53.1 us (21%)
  blocking collectives  32.3 us (13%)
    all_to_all x4, waiting for transfers between devices, exchange(): return lax.all_to_all(x, axis, split_axis=0, concat_axis=0, tiled=True)  41.3 us
    all_to_all x4, starting transfers between devices, exchange(): return lax.all_to_all(x, axis, split_axis=0, concat_axis=0, tiled=True)  39.2 us
    ppermute x7, waiting for transfers between devices, step(): lax.ppermute(wsend[o], 'chip', [(i, (i + o) % chips) for i in range(chips)])  38.2 us
    all_to_all x2, blocking collectives, exchange(): return lax.all_to_all(x, axis, split_axis=0, concat_axis=0, tiled=True)  32.3 us
    ppermute x7, starting transfers between devices, step(): lax.ppermute(wsend[o], 'chip', [(i, (i + o) % chips) for i in range(chips)])  26.5 us
    ppermute x1, starting transfers between devices, step(): other = lax.ppermute(share, 'core', partner)  8.73 us
    pallas_call x1, Pallas kernels, step(): call(sums_kernel, [((8, rows), F32)], [VM] * 3)(back_stats, mj, totals)  6.21 us
    pallas_call x1, Pallas kernels, step(): call(total_kernel, [((8, rows), F32), ((1, rows), F32), ((span, 128), F32...  5.61 us
  transfers between devices with their start and end apart: 13, of which 8 were waited for; matrix products, arithmetic and copies ran while one was open for 0% of the time, Pallas kernels for 9%

profile of v5, /device:TPU:1, one launch (start us, length us, event | category | flops | bytes accessed | tf_op | source)
XLA Modules:
  0.0 248.4 jit_solution(2867566955811305030)
XLA Ops:
  3.5 8.7 %collective-permute-start = (bf16[1808,128]{1,0:T(8,128)(2,1)}, bf16[1808,128]{1,0:T(8,128)(2,1)S(1)}, u32[]{:S(2)}, u32[]{:S(2)}) collective-permute-start(bf16[1808,128]{1,0:T(8,128)(2,1)} %shard_map.131), channel_id=1, source_target_pairs={{0,32},{32,0},{1,33},{33,1},{2,34},{34,2},{3,35},{35,3},{4,36},{36... | collective-permute-start | bytes 1388552 | tf_op jit(solution)/shard_map/ppermute | solution.py:466
  13.9 3.5 %shard_map.132 = bf16[8,272,128]{2,1,0:T(8,128)(2,1)} custom-call(s32[3]{0:T(128)} %pad_add_fusion.where_ref.refs_0_, s32[1]{0:T(128)S(6)} %copy.15.len_ref, bf16[256,128]{1,0:T(8,128)(2,1)} %q_ref.3, bf16[1,256,128]{2,1,0:T(8,128)(2,1)} %k_ref.3, bf16[1,256,128]{2,1,0:T(8,128)(2,1)} %v_ref.3, bf16[128,2048]{1,0:T(8,128)(2,1)} %proj_ref.3, ...), custom_call_target="tpu_custom_call" | custom-call | tf_op jit(solution)/shard_map/pallas_call | solution.py:477
  17.3 3.5 %all-to-all-start = ((bf16[8,272,128]{2,1,0:T(8,128)(2,1)}), bf16[8,272,128]{2,1,0:T(8,128)(2,1)S(1)}, u32[]{:S(2)}, u32[]{:S(2)}) async-start(bf16[8,272,128]{2,1,0:T(8,128)(2,1)} %shard_map.132), calls=%async_computation | async-start | bytes 1114112 | tf_op jit(solution)/shard_map/all_to_all | solution.py:461
  20.9 5.2 %shard_map.133.refs_3_.m_ref.refs_1_ = bf16[4096,256]{1,0:T(8,128)(2,1)} custom-call(s32[8,256]{1,0:T(8,128)} %bitcast.33), custom_call_target="tpu_custom_call" | custom-call | tf_op jit(solution)/shard_map/pallas_call | solution.py:471
  26.1 13.4 %all-to-all-done.refs_0_ = bf16[8,272,128]{2,1,0:T(8,128)(2,1)S(1)} async-done(((bf16[8,272,128]{2,1,0:T(8,128)(2,1)}), bf16[8,272,128]{2,1,0:T(8,128)(2,1)S(1)}, u32[]{:S(2)}, u32[]{:S(2)}) %all-to-all-start) | async-done | bytes 557088 | tf_op jit(solution)/shard_map/all_to_all | solution.py:461
  39.5 3.6 %shard_map.134 = (f32[256,128]{1,0:T(8,128)}, bf16[8,16,128]{2,1,0:T(8,128)(2,1)}, bf16[4096,128]{1,0:T(8,128)(2,1)}) custom-call(bf16[8,272,128]{2,1,0:T(8,128)(2,1)S(1)} %all-to-all-done.refs_0_, bf16[256,128]{1,0:T(8,128)(2,1)} %refs_1_.1, f32[1,128]{1,0:T(1,128)} %bitcast.37, bf16[4096,256]{1,0:T(8,128)(2,1)} %shard_map.133.refs_3_.m_ref.refs_1_), custom_call_target="tpu_custom_call" | custom-call | tf_op jit(solution)/shard_map/pallas_call | solution.py:481
  43.1 15.1 %all-to-all-start.1 = ((bf16[256,16,128]{2,1,0:T(8,128)(2,1)}), bf16[256,16,128]{2,1,0:T(8,128)(2,1)S(1)}, u32[]{:S(2)}, u32[]{:S(2)}) async-start(bf16[256,16,128]{2,1,0:T(8,128)(2,1)} %bitcast.29), calls=%async_computation.1 | async-start | bytes 2097152 | tf_op jit(solution)/shard_map/all_to_all | solution.py:461
  58.2 3.6 %shard_map.135 = (bf16[128,1024]{1,0:T(8,128)(2,1)}, bf16[128,1024]{1,0:T(8,128)(2,1)}, bf16[128,1024]{1,0:T(8,128)(2,1)}, bf16[128,1024]{1,0:T(8,128)(2,1)}, bf...) custom-call(s32[3]{0:T(128)} %pad_add_fusion.where_ref.refs_0_, ...), custom_call_target="tpu_custom_call" | custom-call | tf_op jit(solution)/shard_map/pallas_call | solution.py:467
  63.7 4.2 %collective-permute-start.2 = (bf16[128,1024]{1,0:T(8,128)(2,1)}, bf16[128,1024]{1,0:T(8,128)(2,1)S(1)}, u32[]{:S(2)}, u32[]{:S(2)}) collective-permute-start(bf16[128,1024]{1,0:T(8,128)(2,1)} %get-tuple-element.22), channel_id=1, source_target_pairs={{0,128},{64,192},{128,256},{192,320},{256,384},{320,448},{384,0},{... | collective-permute-start | bytes 786440 | tf_op jit(solution)/shard_map/ppermute | solution.py:470
  67.9 5.0 %collective-permute-start.3 = (bf16[128,1024]{1,0:T(8,128)(2,1)}, bf16[128,1024]{1,0:T(8,128)(2,1)S(1)}, u32[]{:S(2)}, u32[]{:S(2)}) collective-permute-start(bf16[128,1024]{1,0:T(8,128)(2,1)} %get-tuple-element.23), channel_id=1, source_target_pairs={{0,192},{64,256},{128,320},{192,384},{256,448},{320,0},{384,64},{4... | collective-permute-start | bytes 786440 | tf_op jit(solution)/shard_map/ppermute | solution.py:470
  72.9 3.1 %collective-permute-start.4 = (bf16[128,1024]{1,0:T(8,128)(2,1)}, bf16[128,1024]{1,0:T(8,128)(2,1)S(1)}, u32[]{:S(2)}, u32[]{:S(2)}) collective-permute-start(bf16[128,1024]{1,0:T(8,128)(2,1)} %get-tuple-element.24), channel_id=1, source_target_pairs={{0,256},{64,320},{128,384},{192,448},{256,0},{320,64},{384,128},{4... | collective-permute-start | bytes 786440 | tf_op jit(solution)/shard_map/ppermute | solution.py:470
  76.0 5.4 %collective-permute-start.5 = (bf16[128,1024]{1,0:T(8,128)(2,1)}, bf16[128,1024]{1,0:T(8,128)(2,1)S(1)}, u32[]{:S(2)}, u32[]{:S(2)}) collective-permute-start(bf16[128,1024]{1,0:T(8,128)(2,1)} %get-tuple-element.25), channel_id=1, source_target_pairs={{0,320},{64,384},{128,448},{192,0},{256,64},{320,128},{384,192},{4... | collective-permute-start | bytes 786440 | tf_op jit(solution)/shard_map/ppermute | solution.py:470
  81.4 6.0 %collective-permute-done.1.refs_4_.refs_5_ = bf16[128,1024]{1,0:T(8,128)(2,1)S(1)} collective-permute-done((bf16[128,1024]{1,0:T(8,128)(2,1)}, bf16[128,1024]{1,0:T(8,128)(2,1)S(1)}, u32[]{:S(2)}, u32[]{:S(2)}) %collective-permute-start.1) | collective-permute-done | bytes 262176 | tf_op jit(solution)/shard_map/ppermute | solution.py:470
  87.4 3.6 %collective-permute-start.6 = (bf16[128,1024]{1,0:T(8,128)(2,1)}, bf16[128,1024]{1,0:T(8,128)(2,1)S(1)}, u32[]{:S(2)}, u32[]{:S(2)}) collective-permute-start(bf16[128,1024]{1,0:T(8,128)(2,1)} %get-tuple-element.26), channel_id=1, source_target_pairs={{0,384},{64,448},{128,0},{192,64},{256,128},{320,192},{384,256},{4... | collective-permute-start | bytes 786440 | tf_op jit(solution)/shard_map/ppermute | solution.py:470
  91.0 6.9 %collective-permute-done.2.refs_5_.refs_6_ = bf16[128,1024]{1,0:T(8,128)(2,1)S(1)} collective-permute-done((bf16[128,1024]{1,0:T(8,128)(2,1)}, bf16[128,1024]{1,0:T(8,128)(2,1)S(1)}, u32[]{:S(2)}, u32[]{:S(2)}) %collective-permute-start.2) | collective-permute-done | bytes 262176 | tf_op jit(solution)/shard_map/ppermute | solution.py:470
  97.9 3.4 %collective-permute-start.7 = (bf16[128,1024]{1,0:T(8,128)(2,1)}, bf16[128,1024]{1,0:T(8,128)(2,1)S(1)}, u32[]{:S(2)}, u32[]{:S(2)}) collective-permute-start(bf16[128,1024]{1,0:T(8,128)(2,1)} %get-tuple-element.27), channel_id=1, source_target_pairs={{0,448},{64,0},{128,64},{192,128},{256,192},{320,256},{384,320},{4... | collective-permute-start | bytes 786440 | tf_op jit(solution)/shard_map/ppermute | solution.py:470
  101.2 13.7 %collective-permute-done.3.refs_6_.refs_7_ = bf16[128,1024]{1,0:T(8,128)(2,1)S(1)} collective-permute-done((bf16[128,1024]{1,0:T(8,128)(2,1)}, bf16[128,1024]{1,0:T(8,128)(2,1)S(1)}, u32[]{:S(2)}, u32[]{:S(2)}) %collective-permute-start.3) | collective-permute-done | bytes 262176 | tf_op jit(solution)/shard_map/ppermute | solution.py:470
  114.9 11.6 %collective-permute-done.4.refs_7_.refs_8_ = bf16[128,1024]{1,0:T(8,128)(2,1)S(1)} collective-permute-done((bf16[128,1024]{1,0:T(8,128)(2,1)}, bf16[128,1024]{1,0:T(8,128)(2,1)S(1)}, u32[]{:S(2)}, u32[]{:S(2)}) %collective-permute-start.4) | collective-permute-done | bytes 262176 | tf_op jit(solution)/shard_map/ppermute | solution.py:470
  127.5 5.0 %shard_map.136.refs_0_ = f32[536,128]{1,0:T(8,128)} custom-call(s32[3]{0:T(128)} %pad_add_fusion.where_ref.refs_0_, bf16[8,512,128]{2,1,0:T(8,128)(2,1)S(1)} %bitcast.21, bf16[8,16,128]{2,1,0:T(8,128)(2,1)} %get-tuple-element.19.refs_2_, bf16[128,1024]{1,0:T(8,128)(2,1)} %get-tuple-element.20.refs_3_.refs_4_, bf16[128,1024]{1,0:T(8,128)(2,1)} %copy-done.1, ...), custom_call_target="tpu_custom_call" | custom-call | tf_op jit(solution)/shard_map/pallas_call | solution.py:493
  132.5 5.1 %collective-permute-start.8 = (f32[536,128]{1,0:T(8,128)}, f32[536,128]{1,0:T(8,128)S(1)}, u32[]{:S(2)}, u32[]{:S(2)}) collective-permute-start(f32[536,128]{1,0:T(8,128)} %shard_map.136.refs_0_), channel_id=1, source_target_pairs={{0,32},{32,0},{1,33},{33,1},{2,34},{34,2},{3,35},{35,3},{4,36},{36... | collective-permute-start | bytes 823304 | tf_op jit(solution)/shard_map/ppermute | solution.py:496
  139.8 18.6 %all_to_all.30 = bf16[32,16,128]{2,1,0:T(8,128)(2,1)} all-to-all(bf16[32,16,128]{2,1,0:T(8,128)(2,1)} %bitcast.30), channel_id=1, replica_groups=mesh['chip'=8,'core'=2,'vocab'=32] {'vocab'}, dimensions={0} | all-to-all | bytes 262144 | tf_op jit(solution)/shard_map/all_to_all | solution.py:461
  158.4 2.7 %shard_map.138 = (f32[512,128]{1,0:T(8,128)}, f32[256,128]{1,0:T(8,128)}) custom-call(f32[536,128]{1,0:T(8,128)} %shard_map.136.refs_0_, f32[536,128]{1,0:T(8,128)S(1)} %collective-permute-done.8.refs_1_, bf16[512,128]{1,0:T(8,128)(2,1)} %bitcast.27), custom_call_target="tpu_custom_call" | custom-call | tf_op jit(solution)/shard_map/pallas_call | solution.py:497
  161.1 9.4 %all-to-all-start.3 = ((f32[256,1,128]{2,1,0:T(1,128)}), f32[256,1,128]{2,1,0:T(1,128)S(1)}, u32[]{:S(2)}, u32[]{:S(2)}) async-start(f32[256,1,128]{2,1,0:T(1,128)} %bitcast.32), calls=%async_computation.3 | async-start | bytes 262144 | tf_op jit(solution)/shard_map/all_to_all | solution.py:461
  170.5 5.1 %shard_map.139.mj_ref = bf16[16,256,256]{2,1,0:T(8,128)(2,1)} custom-call(s32[8,256]{1,0:T(8,128)} %bitcast.35), custom_call_target="tpu_custom_call" | custom-call | tf_op jit(solution)/shard_map/pallas_call | solution.py:474
  175.5 7.0 %all-to-all-done.3 = f32[256,1,128]{2,1,0:T(1,128)S(1)} async-done(((f32[256,1,128]{2,1,0:T(1,128)}), f32[256,1,128]{2,1,0:T(1,128)S(1)}, u32[]{:S(2)}, u32[]{:S(2)}) %all-to-all-start.3) | async-done | bytes 131104 | tf_op jit(solution)/shard_map/all_to_all | solution.py:461
  182.6 5.6 %shard_map.140 = (f32[8,256]{1,0:T(8,128)}, f32[1,256]{1,0:T(1,128)}, f32[512,128]{1,0:T(8,128)}) custom-call(s32[3]{0:T(128)} %pad_add_fusion.where_ref.refs_0_, f32[256,128]{1,0:T(8,128)S(1)} %bitcast.23, bf16[16,256,256]{2,1,0:T(8,128)(2,1)} %shard_map.139.mj_ref, bf16[4096,256]{1,0:T(8,128)(2,1)} %shard_map.133.refs_3_.m_ref.refs_1_), custom_call_target="tpu_custom_call" | custom-call | tf_op jit(solution)/shard_map/pallas_call | solution.py:504
  188.2 13.6 %all_to_all.31 = f32[32,16,128]{2,1,0:T(8,128)S(1)} all-to-all(f32[32,16,128]{2,1,0:T(8,128)} %bitcast.31), channel_id=1, replica_groups=mesh['chip'=8,'core'=2,'vocab'=32] {'vocab'}, dimensions={0} | all-to-all | bytes 524288 | tf_op jit(solution)/shard_map/all_to_all | solution.py:461
  201.8 5.0 %shard_map.141 = bf16[8,512,128]{2,1,0:T(8,128)(2,1)} custom-call(s32[3]{0:T(128)} %pad_add_fusion.where_ref.refs_0_, f32[512,128]{1,0:T(8,128)} %get-tuple-element.30.refs_1_, bf16[512,128]{1,0:T(8,128)(2,1)} %bitcast.28, f32[512,128]{1,0:T(8,128)S(1)} %bitcast.25, bf16[128,1024]{1,0:T(8,128)(2,1)} %get-tuple-element.20.refs_3_.refs_4_, ...), custom_call_target="tpu_custom_call" | custom-call | tf_op jit(solution)/shard_map/pallas_call | solution.py:508
  206.8 11.3 %all-to-all-start.5 = ((bf16[256,16,128]{2,1,0:T(8,128)(2,1)}), bf16[256,16,128]{2,1,0:T(8,128)(2,1)S(1)}, u32[]{:S(2)}, u32[]{:S(2)}) async-start(bf16[256,16,128]{2,1,0:T(8,128)(2,1)} %bitcast.26), calls=%async_computation.5 | async-start | bytes 2097152 | tf_op jit(solution)/shard_map/all_to_all | solution.py:461
  218.1 6.2 %shard_map.142.refs_4_ = f32[8,256]{1,0:T(8,128)} custom-call(f32[256,128]{1,0:T(8,128)} %bitcast.24, bf16[16,256,256]{2,1,0:T(8,128)(2,1)} %shard_map.139.mj_ref, f32[8,256]{1,0:T(8,128)} %get-tuple-element.33.tot_ref), custom_call_target="tpu_custom_call" | custom-call | tf_op jit(solution)/shard_map/pallas_call | solution.py:512
  224.3 20.8 %all-to-all-done.5 = bf16[256,16,128]{2,1,0:T(8,128)(2,1)S(1)} async-done(((bf16[256,16,128]{2,1,0:T(8,128)(2,1)}), bf16[256,16,128]{2,1,0:T(8,128)(2,1)S(1)}, u32[]{:S(2)}, u32[]{:S(2)}) %all-to-all-start.5) | async-done | bytes 1048608 | tf_op jit(solution)/shard_map/all_to_all | solution.py:461
  245.2 3.2 %shard_map.143 = f32[256,128]{1,0:T(8,128)} custom-call(bf16[4096,128]{1,0:T(8,128)(2,1)S(1)} %bitcast.22, bf16[4096,256]{1,0:T(8,128)(2,1)} %shard_map.133.refs_3_.m_ref.refs_1_, f32[256,128]{1,0:T(8,128)} %get-tuple-element.32.refs_2_, f32[1,128]{1,0:T(1,128)} %bitcast.38, f32[8,256]{1,0:T(8,128)} %shard_map.142.refs_4_), custom_call_target="tpu_custom_call" | custom-call | tf_op jit(solution)/shard_map/pallas_call | solution.py:513
  (26 shorter events, 8.8 us)
Async XLA Ops:
  3.5 10.4 %collective-permute-start = (bf16[1808,128]{1,0:T(8,128)(2,1)}, bf16[1808,128]{1,0:T(8,128)(2,1)S(1)}, u32[]{:S(2)}, u32[]{:S(2)}) collective-permute-start(bf16[1808,128]{1,0:T(8,128)(2,1)} %shard_map.131), channel_id=1, source_target_pairs={{0,32},{32,0},{1,33},{33,1},{2,34},{34,2},{3,35},{35,3},{4,36},{36... | collective-permute-start | bytes 1388552 | tf_op jit(solution)/shard_map/ppermute | solution.py:466
  17.3 22.2 %all-to-all-start = ((bf16[8,272,128]{2,1,0:T(8,128)(2,1)}), bf16[8,272,128]{2,1,0:T(8,128)(2,1)S(1)}, u32[]{:S(2)}, u32[]{:S(2)}) async-start(bf16[8,272,128]{2,1,0:T(8,128)(2,1)} %shard_map.132), calls=%async_computation | async-start | bytes 1114112 | tf_op jit(solution)/shard_map/all_to_all | solution.py:461
  43.1 83.4 %all-to-all-start.1 = ((bf16[256,16,128]{2,1,0:T(8,128)(2,1)}), bf16[256,16,128]{2,1,0:T(8,128)(2,1)S(1)}, u32[]{:S(2)}, u32[]{:S(2)}) async-start(bf16[256,16,128]{2,1,0:T(8,128)(2,1)} %bitcast.29), calls=%async_computation.1 | async-start | bytes 2097152 | tf_op jit(solution)/shard_map/all_to_all | solution.py:461
  61.8 25.6 %collective-permute-start.1 = (bf16[128,1024]{1,0:T(8,128)(2,1)}, bf16[128,1024]{1,0:T(8,128)(2,1)S(1)}, u32[]{:S(2)}, u32[]{:S(2)}) collective-permute-start(bf16[128,1024]{1,0:T(8,128)(2,1)} %get-tuple-element.21), channel_id=1, source_target_pairs={{0,64},{64,128},{128,192},{192,256},{256,320},{320,384},{384,448},... | collective-permute-start | bytes 786440 | tf_op jit(solution)/shard_map/ppermute | solution.py:470
  63.7 34.2 %collective-permute-start.2 = (bf16[128,1024]{1,0:T(8,128)(2,1)}, bf16[128,1024]{1,0:T(8,128)(2,1)S(1)}, u32[]{:S(2)}, u32[]{:S(2)}) collective-permute-start(bf16[128,1024]{1,0:T(8,128)(2,1)} %get-tuple-element.22), channel_id=1, source_target_pairs={{0,128},{64,192},{128,256},{192,320},{256,384},{320,448},{384,0},{... | collective-permute-start | bytes 786440 | tf_op jit(solution)/shard_map/ppermute | solution.py:470
  67.9 47.0 %collective-permute-start.3 = (bf16[128,1024]{1,0:T(8,128)(2,1)}, bf16[128,1024]{1,0:T(8,128)(2,1)S(1)}, u32[]{:S(2)}, u32[]{:S(2)}) collective-permute-start(bf16[128,1024]{1,0:T(8,128)(2,1)} %get-tuple-element.23), channel_id=1, source_target_pairs={{0,192},{64,256},{128,320},{192,384},{256,448},{320,0},{384,64},{4... | collective-permute-start | bytes 786440 | tf_op jit(solution)/shard_map/ppermute | solution.py:470
  72.9 53.6 %collective-permute-start.4 = (bf16[128,1024]{1,0:T(8,128)(2,1)}, bf16[128,1024]{1,0:T(8,128)(2,1)S(1)}, u32[]{:S(2)}, u32[]{:S(2)}) collective-permute-start(bf16[128,1024]{1,0:T(8,128)(2,1)} %get-tuple-element.24), channel_id=1, source_target_pairs={{0,256},{64,320},{128,384},{192,448},{256,0},{320,64},{384,128},{4... | collective-permute-start | bytes 786440 | tf_op jit(solution)/shard_map/ppermute | solution.py:470
  76.0 50.5 %collective-permute-start.5 = (bf16[128,1024]{1,0:T(8,128)(2,1)}, bf16[128,1024]{1,0:T(8,128)(2,1)S(1)}, u32[]{:S(2)}, u32[]{:S(2)}) collective-permute-start(bf16[128,1024]{1,0:T(8,128)(2,1)} %get-tuple-element.25), channel_id=1, source_target_pairs={{0,320},{64,384},{128,448},{192,0},{256,64},{320,128},{384,192},{4... | collective-permute-start | bytes 786440 | tf_op jit(solution)/shard_map/ppermute | solution.py:470
  87.4 39.2 %copy-start.1 = (bf16[128,1024]{1,0:T(8,128)(2,1)}, bf16[128,1024]{1,0:T(8,128)(2,1)S(1)}, u32[]{:S(2)}) copy-start(bf16[128,1024]{1,0:T(8,128)(2,1)S(1)} %collective-permute-done.1.refs_4_.refs_5_) | copy-start | bytes 786436
  87.4 39.1 %collective-permute-start.6 = (bf16[128,1024]{1,0:T(8,128)(2,1)}, bf16[128,1024]{1,0:T(8,128)(2,1)S(1)}, u32[]{:S(2)}, u32[]{:S(2)}) collective-permute-start(bf16[128,1024]{1,0:T(8,128)(2,1)} %get-tuple-element.26), channel_id=1, source_target_pairs={{0,384},{64,448},{128,0},{192,64},{256,128},{320,192},{384,256},{4... | collective-permute-start | bytes 786440 | tf_op jit(solution)/shard_map/ppermute | solution.py:470
  97.9 28.7 %copy-start.2 = (bf16[128,1024]{1,0:T(8,128)(2,1)}, bf16[128,1024]{1,0:T(8,128)(2,1)S(1)}, u32[]{:S(2)}) copy-start(bf16[128,1024]{1,0:T(8,128)(2,1)S(1)} %collective-permute-done.2.refs_5_.refs_6_) | copy-start | bytes 786436
  97.9 28.7 %collective-permute-start.7 = (bf16[128,1024]{1,0:T(8,128)(2,1)}, bf16[128,1024]{1,0:T(8,128)(2,1)S(1)}, u32[]{:S(2)}, u32[]{:S(2)}) collective-permute-start(bf16[128,1024]{1,0:T(8,128)(2,1)} %get-tuple-element.27), channel_id=1, source_target_pairs={{0,448},{64,0},{128,64},{192,128},{256,192},{320,256},{384,320},{4... | collective-permute-start | bytes 786440 | tf_op jit(solution)/shard_map/ppermute | solution.py:470
  114.9 11.7 %copy-start.3 = (bf16[128,1024]{1,0:T(8,128)(2,1)}, bf16[128,1024]{1,0:T(8,128)(2,1)S(1)}, u32[]{:S(2)}) copy-start(bf16[128,1024]{1,0:T(8,128)(2,1)S(1)} %collective-permute-done.3.refs_6_.refs_7_) | copy-start | bytes 786436
  126.5 0.7 copy-start.4
  126.5 0.8 copy-start.5
  126.5 0.9 copy-start.6
  126.5 0.9 copy-start.7
  132.5 25.9 %collective-permute-start.8 = (f32[536,128]{1,0:T(8,128)}, f32[536,128]{1,0:T(8,128)S(1)}, u32[]{:S(2)}, u32[]{:S(2)}) collective-permute-start(f32[536,128]{1,0:T(8,128)} %shard_map.136.refs_0_), channel_id=1, source_target_pairs={{0,32},{32,0},{1,33},{33,1},{2,34},{34,2},{3,35},{35,3},{4,36},{36... | collective-permute-start | bytes 823304 | tf_op jit(solution)/shard_map/ppermute | solution.py:496
  161.1 21.5 %all-to-all-start.3 = ((f32[256,1,128]{2,1,0:T(1,128)}), f32[256,1,128]{2,1,0:T(1,128)S(1)}, u32[]{:S(2)}, u32[]{:S(2)}) async-start(f32[256,1,128]{2,1,0:T(1,128)} %bitcast.32), calls=%async_computation.3 | async-start | bytes 262144 | tf_op jit(solution)/shard_map/all_to_all | solution.py:461
  182.6 5.6 %copy-start = (f32[256,1,128]{2,1,0:T(1,128)}, f32[256,1,128]{2,1,0:T(1,128)S(1)}, u32[]{:S(2)}) copy-start(f32[256,1,128]{2,1,0:T(1,128)S(1)} %all-to-all-done.3) | copy-start | bytes 393220
  206.8 38.3 %all-to-all-start.5 = ((bf16[256,16,128]{2,1,0:T(8,128)(2,1)}), bf16[256,16,128]{2,1,0:T(8,128)(2,1)S(1)}, u32[]{:S(2)}, u32[]{:S(2)}) async-start(bf16[256,16,128]{2,1,0:T(8,128)(2,1)} %bitcast.26), calls=%async_computation.5 | async-start | bytes 2097152 | tf_op jit(solution)/shard_map/all_to_all | solution.py:461
